TPU v7x, 32 devices: a whole 2x2x4 slice. The times are simulated.
32 devices in a mesh: dp: 2 (over core), expert: 4 (over y, x), tensor: 4 (over z).
Axes of the slice: x: 2, y: 2, z: 4, core: 2. Of those that a mesh axis runs over, the one named last changes fastest.
Arguments:
- tokens: bfloat16 [256, 5120], P(('dp', 'expert'), 'tensor'), may hold values from -50 to 50
- expert_ids: int32 [256, 2], P(('dp', 'expert')), may hold values from 0 to 3, all different within a row; in each aligned block of 32 rows (0 to 31, 32 to 63, ...) at most 32 rows name the same one
- gate_weights: float32 [256, 2], P(('dp', 'expert')), may hold values from 0.1 to 1
- t_gate: bfloat16 [4, 5120, 8192], P('expert', None, ('dp', 'tensor')), may hold values from -0.078125 to 0.078125
- t_up: bfloat16 [4, 5120, 8192], P('expert', None, ('dp', 'tensor')), may hold values from -0.078125 to 0.078125
- t_down: bfloat16 [4, 8192, 5120], P('expert', ('dp', 'tensor')), may hold values from -0.09375 to 0.09375
- s_gate: bfloat16 [5120, 8192], P(None, ('expert', 'tensor')), may hold values from -0.078125 to 0.078125
- s_up: bfloat16 [5120, 8192], P(None, ('expert', 'tensor')), may hold values from -0.078125 to 0.078125
- s_down: bfloat16 [8192, 5120], P(('expert', 'tensor')), may hold values from -0.09375 to 0.09375
Outputs:
- grad_gate: bfloat16 [5120, 8192], P(None, ('expert', 'tensor'))
- grad_up: bfloat16 [5120, 8192], P(None, ('expert', 'tensor'))
- grad_down: bfloat16 [8192, 5120], P(('expert', 'tensor'))
- loss: float32 [], replicated
Inputs may be any that keep to these rules, and one draw needn't show every extreme that they name: `expert_ids`: in each aligned block of 32 tokens no expert is named by more than 32 tokens; a token's two experts differ.
All inputs are finite; a program needn't handle non-finite values.
Results may differ from a plain program's by a relative error of at most 0.018.
Values may be sent and summed in bfloat16 or wider, within the bound.
No kernel may reach another device: no remote copies, remote signals or barrier semaphores. Data moves between devices by JAX's collectives and lax.ppermute only.
A program may use at most 128 MiB of HBM per device.

v0:
```python
import math

import jax
import jax.numpy as jnp
from jax import lax
from jax.sharding import PartitionSpec as P


def pair_slots(route_ids, experts, capacity):
    flat_ids = route_ids.reshape(-1)
    onehot = (flat_ids[:, None] == jnp.arange(experts, dtype=jnp.int32)[None, :]).astype(jnp.int32)
    before = jnp.cumsum(onehot, axis=0) - onehot
    slot_rank = jnp.sum(before * onehot, axis=1)
    return (flat_ids * capacity + slot_rank).reshape(route_ids.shape)


def body(tokens, expert_ids, gate_weights, t_gate, t_up, t_down, s_gate, s_up, s_down):
    experts = lax.axis_size("expert")
    tensor_count = lax.axis_size("tensor")
    data_count = lax.axis_size("dp")
    group_rows = tokens.shape[0]
    slice_width = tokens.shape[1]
    model_width = slice_width * tensor_count
    capacity = 4 * group_rows // experts
    pair_codes = pair_slots(expert_ids, experts, capacity)
    slot_codes = jnp.arange(experts * capacity, dtype=jnp.int32)
    placing = jnp.sum(
        (pair_codes[None, :, :] == slot_codes[:, None, None]).astype(jnp.float32), axis=2
    ).astype(jnp.bfloat16)
    full_rows = lax.all_gather(tokens, "tensor", axis=1, tiled=True)
    sent = jnp.dot(placing, full_rows, preferred_element_type=jnp.float32).astype(jnp.bfloat16)
    sent = sent.reshape(experts, capacity, model_width)
    received = lax.all_to_all(sent, "expert", split_axis=0, concat_axis=0, tiled=True)
    slot_rows = received.reshape(experts * capacity, model_width)
    shard_rows = lax.all_gather(slot_rows, "dp", axis=0, tiled=True)
    gate_pre = jnp.dot(shard_rows, t_gate[0], preferred_element_type=jnp.float32)
    up_pre = jnp.dot(shard_rows, t_up[0], preferred_element_type=jnp.float32)
    teacher_act = (gate_pre * jax.nn.sigmoid(gate_pre) * up_pre).astype(jnp.bfloat16)
    hidden_local = teacher_act.shape[1]
    slot_total = experts * capacity
    teacher_part = jnp.einsum(
        "dqf,ftc->dtqc",
        teacher_act.reshape(data_count, slot_total, hidden_local),
        t_down[0].reshape(hidden_local, tensor_count, slice_width),
        preferred_element_type=jnp.float32,
    )
    teacher_part = teacher_part.reshape(data_count * tensor_count * slot_total, slice_width)
    expert_out = lax.psum_scatter(
        teacher_part.astype(jnp.bfloat16), ("dp", "tensor"), scatter_dimension=0, tiled=True
    )
    back = lax.all_to_all(
        expert_out.reshape(experts, capacity, slice_width),
        "expert",
        split_axis=0,
        concat_axis=0,
        tiled=True,
    )
    weighting = gate_weights / jnp.sum(gate_weights, axis=1, keepdims=True)
    mixing = jnp.sum(
        weighting[:, :, None]
        * (pair_codes[:, :, None] == slot_codes[None, None, :]).astype(jnp.float32),
        axis=1,
    )
    teacher_out = jnp.dot(
        mixing,
        back.reshape(slot_total, slice_width).astype(jnp.float32),
        precision=lax.Precision.HIGHEST,
    )
    group_x = lax.all_gather(full_rows, "expert", axis=0, tiled=True)
    gate_pre = jnp.dot(group_x, s_gate, preferred_element_type=jnp.float32)
    up_pre = jnp.dot(group_x, s_up, preferred_element_type=jnp.float32)
    gate_sig = jax.nn.sigmoid(gate_pre)
    activation = (gate_pre * gate_sig * up_pre).astype(jnp.bfloat16)
    student_local = activation.shape[1]
    act_split = activation.reshape(experts, group_rows, student_local)
    down_split = s_down.reshape(student_local, tensor_count, slice_width)
    partial_value = jnp.dot(activation, s_down, preferred_element_type=jnp.float32)
    column_part = lax.psum_scatter(
        partial_value.astype(jnp.bfloat16), "tensor", scatter_dimension=1, tiled=True
    )
    student_out = lax.psum_scatter(column_part, "expert", scatter_dimension=0, tiled=True).astype(
        jnp.float32
    )
    residual = student_out - teacher_out
    total_tokens = group_rows * experts * data_count
    loss_total = lax.psum(jnp.sum(residual * residual), ("dp", "expert", "tensor"))
    loss_value = loss_total / (total_tokens * model_width)
    grad_scale = 1.0 / math.sqrt(total_tokens)
    d_out = (residual * grad_scale).astype(jnp.bfloat16)
    gathered = lax.all_gather(d_out, ("expert", "tensor"), axis=0, tiled=True)
    gathered = gathered.reshape(experts, tensor_count, group_rows, slice_width)
    d_act = jnp.einsum("etrc,ftc->erf", gathered, down_split, preferred_element_type=jnp.float32)
    d_act = d_act.reshape(experts * group_rows, student_local)
    d_down = jnp.einsum("erf,etrc->ftc", act_split, gathered, preferred_element_type=jnp.float32)
    d_down = d_down.reshape(student_local, model_width)
    d_gate_pre = (d_act * up_pre * gate_sig * (1.0 + gate_pre * (1.0 - gate_sig))).astype(
        jnp.bfloat16
    )
    d_up_pre = (d_act * gate_pre * gate_sig).astype(jnp.bfloat16)
    d_gate = jnp.einsum("rd,rf->df", group_x, d_gate_pre, preferred_element_type=jnp.float32)
    d_up = jnp.einsum("rd,rf->df", group_x, d_up_pre, preferred_element_type=jnp.float32)
    grad_sums = (
        lax.psum(d_gate.astype(jnp.bfloat16), "dp").astype(jnp.float32),
        lax.psum(d_up.astype(jnp.bfloat16), "dp").astype(jnp.float32),
        lax.psum(d_down.astype(jnp.bfloat16), "dp").astype(jnp.float32),
    )
    return (
        grad_sums[0].astype(jnp.bfloat16),
        grad_sums[1].astype(jnp.bfloat16),
        grad_sums[2].astype(jnp.bfloat16),
        loss_value,
    )


def solution(mesh):
    return jax.shard_map(
        body,
        mesh=mesh,
        in_specs=(
            P(("dp", "expert"), "tensor"),
            P(("dp", "expert"), None),
            P(("dp", "expert"), None),
            P("expert", None, ("dp", "tensor")),
            P("expert", None, ("dp", "tensor")),
            P("expert", ("dp", "tensor"), None),
            P(None, ("expert", "tensor")),
            P(None, ("expert", "tensor")),
            P(("expert", "tensor"), None),
        ),
        out_specs=(
            P(None, ("expert", "tensor")),
            P(None, ("expert", "tensor")),
            P(("expert", "tensor"), None),
            P(),
        ),
        check_vma=False,
    )
```

profile of v0, /device:TPU:0, one launch (start us, length us, event | category | flops | bytes accessed | tf_op | source)
XLA Modules:
  0.0 361.4 jit_solution(18171295579013143067)
XLA Ops:
  7.2 0.0 all-gather.4.cloned.1.call-start
  7.2 17.9 %all_gather.12 = bf16[32,5120]{1,0:T(8,128)(2,1)} all-gather(bf16[32,1280]{1,0:T(8,128)(2,1)} %param.9), channel_id=1, replica_groups=mesh['dp'=2,'expert'=4,'tensor'=4] {'tensor'}, dimensions={1}, use_global_device_ids=true | all-gather | bytes 409600 | tf_op jit(solution)/shard_map/all_gather | solution.py:30
  25.1 0.0 all-gather.4.cloned.1.call-update
  25.1 0.0 all-gather.6.cloned.1.call-start
  25.1 0.8 copy.44
  25.9 0.1 eq.20
  26.0 0.1 fusion.26
  26.1 0.1 reduce_window_sum.11
  26.2 0.2 select_reduce_fusion.1
  26.4 0.1 reduce_sum.48
  26.5 0.1 copy.45
  26.6 0.7 multiply_add_fusion
  27.3 0.1 convert_reduce_fusion
  27.3 1.5 convolution_convert_fusion.2
  28.8 21.5 %all_to_all.10 = bf16[4,32,5120]{2,1,0:T(8,128)(2,1)} all-to-all(bf16[4,32,5120]{2,1,0:T(8,128)(2,1)S(1)} %bitcast.74), channel_id=1, replica_groups=mesh['dp'=2,'expert'=4,'tensor'=4] {'expert'}, dimensions={0} | all-to-all | bytes 2621440 | tf_op jit(solution)/shard_map/all_to_all | solution.py:33
  50.3 0.0 all-gather.6.cloned.1.call-update
  50.4 0.0 reduce-scatter.4.cloned.1.call-start
  50.4 19.4 %reshape_squeeze.3 = bf16[1024,4,1280]{2,1,0:T(4,128)(2,1)} reshape(bf16[1,1024,5120]{2,1,0:T(8,128)(2,1)} %param.14) | data formatting | bytes 20971520 | tf_op jit(solution)/shard_map/reshape;squeeze | solution.py:44
  69.8 4.2 %fusion.30 = f32[128,512]{1,0:T(8,128)S(1)} fusion(bf16[128,5120]{1,0:T(8,128)(2,1)} %all-gather.4.cloned.1.call-done, bf16[5120,512]{1,0:T(8,128)(2,1)} %param.15), kind=kOutput, calls=%fused_computation.42 | convolution fusion | flops 671088640 | bytes 6815744 | tf_op jit(solution)/shard_map/dot_general | solution.py:70
  74.1 0.0 copy-done
  74.1 3.3 multiply_convert_fusion.2
  77.4 4.4 %convolution_convert_fusion.3 = bf16[128,5120]{1,0:T(8,128)(2,1)} fusion(bf16[128,512]{1,0:T(8,128)(2,1)S(1)} %get-tuple-element.25, bf16[512,5120]{1,0:T(8,128)(2,1)} %param.17), kind=kOutput, calls=%fused_computation.13 | convolution fusion | flops 671744000 | bytes 6684672 | tf_op jit(solution)/shard_map/dot_general | solution.py:77
  81.8 0.0 reduce-scatter.4.cloned.1.call-update
  81.9 0.0 reduce-scatter.8.cloned.1.call-start
  81.9 0.0 all-gather.6.cloned.1.call-done
  81.9 0.0 copy-start.2
  82.0 0.0 slice-start
  82.0 0.0 slice-start.1
  82.0 7.7 %fusion.4 = f32[256,1024]{1,0:T(8,128)S(1)} fusion(bf16[256,5120]{1,0:T(8,128)(2,1)} %all-gather.6.cloned.1.call-done, bf16[1,5120,1024]{2,1,0:T(8,128)(2,1)} %param.12), kind=kOutput, calls=%fused_computation.5 | convolution fusion | flops 2684354560 | bytes 14155776 | tf_op jit(solution)/shard_map/dot_general | solution.py:36
  89.7 0.0 copy-done.2
  89.7 0.0 slice-start.2
  89.7 7.1 %fusion.18 = bf16[256,1024]{1,0:T(8,128)(2,1)S(1)} fusion(bf16[256,5120]{1,0:T(8,128)(2,1)S(1)} %copy-done.2, bf16[1,5120,1024]{2,1,0:T(8,128)(2,1)} %param.13, f32[256,1024]{1,0:T(8,128)S(1)} %fusion.4), kind=kOutput, calls=%fused_computation.20 | convolution fusion | flops 2685927424 | bytes 14680064 | tf_op jit(solution)/shard_map/dot_general | solution.py:37
  96.8 0.0 slice-done
  96.8 0.0 slice-done.1
  96.8 0.0 slice-done.2
  96.8 0.0 copy-start.1
  96.8 4.4 %fusion.12 = bf16[2,128,4,1280]{3,1,2,0:T(8,128)(2,1)} fusion(bf16[2,128,1024,1]{2,1,3,0:T(8,128)(2,1)S(1)} %bitcast.81, bf16[1024,4,1280]{2,1,0:T(4,128)(2,1)S(1)} %bitcast.70), kind=kOutput, calls=%fused_computation.17 | convolution fusion | flops 2685665280 | bytes 13631488 | tf_op jit(solution)/shard_map/dqf,ftc->dtqc/dot_general | solution.py:41
  101.2 0.0 reduce-scatter.8.cloned.1.call-update
  101.2 0.0 reduce-scatter.6.cloned.1.call-start
  101.3 10.5 %reduce-scatter.4.cloned.1.call-done = bf16[128,1280]{1,0:T(8,128)(2,1)} async-done(((bf16[128,5120]{1,0:T(8,128)(2,1)}), bf16[128,1280]{1,0:T(8,128)(2,1)}) %reduce-scatter.4.cloned.1.call-update) | async-done | bytes 327696 | tf_op jit(solution)/shard_map/reduce_scatter | solution.py:78
  111.7 0.0 reduce-scatter.6.cloned.1.call-update
  111.8 0.0 copy-done.1
  111.8 60.2 %reduce-scatter.8.cloned.1.call-done = bf16[128,1280]{1,0:T(8,128)(2,1)} async-done(((bf16[1024,1280]{1,0:T(8,128)(2,1)}), bf16[128,1280]{1,0:T(8,128)(2,1)}) %reduce-scatter.8.cloned.1.call-update) | async-done | bytes 327696 | tf_op jit(solution)/shard_map/reduce_scatter | solution.py:48
  172.0 3.6 %all-to-all-start.1 = ((bf16[4,32,1280]{2,1,0:T(8,128)(2,1)}), bf16[4,32,1280]{2,1,0:T(8,128)(2,1)S(1)}, u32[]{:S(2)}, u32[]{:S(2)}) async-start(bf16[4,32,1280]{2,1,0:T(8,128)(2,1)} %bitcast.80), calls=%async_computation.4 | async-start | bytes 655360 | tf_op jit(solution)/shard_map/all_to_all | solution.py:51
  175.6 0.0 all-gather.8.cloned.1.call-start
  175.6 0.1 select_reduce_fusion
  175.7 22.8 %reduce-scatter.6.cloned.1.call-done = bf16[32,1280]{1,0:T(8,128)(2,1)} async-done(((bf16[128,1280]{1,0:T(8,128)(2,1)}), bf16[32,1280]{1,0:T(8,128)(2,1)}) %reduce-scatter.6.cloned.1.call-update) | async-done | bytes 81936 | tf_op jit(solution)/shard_map/reduce_scatter | solution.py:81
  198.5 0.0 all-to-all-done.1
  198.5 2.4 multiply_reduce_fusion
  200.8 0.0 all-gather.8.cloned.1.call-update
  200.9 0.2 all-reduce.3.cloned.1.call-start
  201.1 57.3 %all-gather.8.cloned.1.call-done = bf16[512,1280]{1,0:T(8,128)(2,1)} async-done(((bf16[32,1280]{1,0:T(8,128)(2,1)}), bf16[512,1280]{1,0:T(8,128)(2,1)}) %all-gather.8.cloned.1.call-update) | async-done | bytes 1310736 | tf_op jit(solution)/shard_map/all_gather | solution.py:90
  258.4 1.4 copy.54
  259.8 1.4 copy.47
  261.2 4.4 %fusion.21 = f32[128,512]{1,0:T(8,128)S(1)} fusion(bf16[128,1280,4]{1,0,2:T(8,128)(2,1)S(1)} %bitcast.77, bf16[64,4,8,1280]{3,2,1,0:T(8,128)(2,1)} %bitcast.68), kind=kOutput, calls=%fused_computation.21 | convolution fusion | flops 671088640 | bytes 6815744 | tf_op jit(solution)/shard_map/etrc,ftc->erf/dot_general | solution.py:92
  265.6 3.9 %bitcast_convert_fusion = bf16[512,5120]{1,0:T(8,128)(2,1)} fusion(bf16[4,32,512]{2,1,0:T(8,128)(2,1)S(1)} %bitcast.79, bf16[5120,4,32]{0,2,1:T(8,128)(2,1)S(1)} %bitcast.76), kind=kOutput, calls=%fused_computation | convolution fusion | flops 673710080 | bytes 6684672 | tf_op jit(solution)/shard_map/erf,etrc->ftc/dot_general | solution.py:94
  269.5 3.9 %fusion.8 = bf16[5120,512]{0,1:T(8,128)(2,1)} fusion(bf16[128,5120]{1,0:T(8,128)(2,1)S(1)} %copy-done, f32[128,512]{1,0:T(8,128)S(1)} %fusion.21, f32[128,512]{1,0:T(8,128)S(1)} %fusion.30), kind=kOutput, calls=%fused_computation.11 | convolution fusion | flops 674103296 | bytes 7077888 | tf_op jit(solution)/shard_map/rd,rf->df/dot_general | solution.py:101
  273.4 4.0 %fusion.7 = bf16[5120,512]{0,1:T(8,128)(2,1)} fusion(bf16[128,5120]{1,0:T(8,128)(2,1)S(1)} %copy-done, f32[128,512]{1,0:T(8,128)S(1)} %fusion.30, f32[128,512]{1,0:T(8,128)S(1)} %fusion.21, f32[128,512]{1,0:T(8,128)S(1)} %get-tuple-element.26), kind=kOutput, calls=%fused_computation.10 | convolution fusion | flops 674365440 | bytes 7340032 | tf_op jit(solution)/shard_map/rd,rf->df/dot_general | solution.py:100
  277.4 0.0 all-reduce.3.cloned.1.call-update
  277.4 38.4 %psum.31 = f32[]{:T(128)} all-reduce(f32[]{:T(128)} %get-tuple-element.23), channel_id=1, replica_groups=mesh['dp'=2,'expert'=4,'tensor'=4] {'dp','expert','tensor'}, use_global_device_ids=true, to_apply=%region_12.13 | all-reduce | flops 1 | bytes 8 | tf_op jit(solution)/shard_map/psum | solution.py:86
  316.5 16.0 %all-reduce.3.cloned.1.call-done = (bf16[5120,512]{0,1:T(8,128)(2,1)}, bf16[5120,512]{0,1:T(8,128)(2,1)}, bf16[512,5120]{1,0:T(8,128)(2,1)}) async-done(((bf16[5120,512]{0,1:T(8,128)(2,1)}, bf16[5120,512]{0,1:T(8,128)(2,1)}, bf16[512,5120]{1,0:T(8,128)(2,1)}), (bf16[5120,512]{0,1:T(8,128)(2,1)}, bf16[5120,512]{0,1:T(8,128)(2,1)}, bf16[512,5120]{1,0:T(8,128)(2,1)})) %all-reduce.3.cloned.1.call-update) | async-done | bytes 15728656 | tf_op jit(solution)/shard_map/psum | solution.py:103
  332.4 7.9 %copy.50 = bf16[5120,512]{1,0:T(8,128)(2,1)} copy(bf16[5120,512]{0,1:T(8,128)(2,1)} %get-tuple-element.20) | data formatting | bytes 10485760
  340.4 7.9 %copy.51 = bf16[5120,512]{1,0:T(8,128)(2,1)} copy(bf16[5120,512]{0,1:T(8,128)(2,1)} %get-tuple-element.21) | data formatting | bytes 10485760
  348.3 5.2 %copy.70 = bf16[512,5120]{1,0:T(8,128)(2,1)} copy(bf16[512,5120]{1,0:T(8,128)(2,1)} %get-tuple-element.29) | data formatting | bytes 10485760
  (5 shorter events, 0.0 us)
Async XLA Ops:
  7.2 62.7 %all-gather.4.cloned.1.call-start = ((), (), s32[]{:S(2)}) async-start(), calls=%async_computation.5 | async-start | bytes 1638400 | tf_op jit(solution)/shard_map/all_gather | solution.py:69
  25.1 56.8 %all-gather.6.cloned.1.call-start = ((), (), s32[]{:S(2)}) async-start(), calls=%async_computation.8 | async-start | bytes 3932160 | tf_op jit(solution)/shard_map/all_gather | solution.py:35
  50.4 61.4 %reduce-scatter.4.cloned.1.call-start = ((), (), s32[]{:S(2)}) async-start(), calls=%async_computation.6 | async-start | bytes 1638400 | tf_op jit(solution)/shard_map/reduce_scatter | solution.py:78
  69.8 4.2 %copy-start = (bf16[128,5120]{1,0:T(8,128)(2,1)S(1)}, bf16[128,5120]{1,0:T(8,128)(2,1)}, u32[]{:S(2)}) copy-start(bf16[128,5120]{1,0:T(8,128)(2,1)} %all-gather.4.cloned.1.call-done) | copy-start | bytes 3932164
  81.9 90.1 %reduce-scatter.8.cloned.1.call-start = ((), (), s32[]{:S(2)}) async-start(), calls=%async_computation.9 | async-start | bytes 2949120 | tf_op jit(solution)/shard_map/reduce_scatter | solution.py:48
  81.9 7.7 %copy-start.2 = (bf16[256,5120]{1,0:T(8,128)(2,1)S(1)}, bf16[256,5120]{1,0:T(8,128)(2,1)}, u32[]{:S(2)}) copy-start(bf16[256,5120]{1,0:T(8,128)(2,1)} %all-gather.6.cloned.1.call-done) | copy-start | bytes 7864324
  82.0 14.8 %slice-start = ((s8[10485760]{0:T(1024)(128)(4,1)}), s8[4194304]{0:T(1024)(128)(4,1)S(1)}, s32[]{:S(2)}) async-start(s8[10485760]{0:T(1024)(128)(4,1)} %bitcast.69), calls=%async_computation.12 | async-start | bytes 8388608
  82.0 14.8 %slice-start.1 = ((s8[10485760]{0:T(1024)(128)(4,1)}), s8[4194304]{0:T(1024)(128)(4,1)S(1)}, s32[]{:S(2)}) async-start(s8[10485760]{0:T(1024)(128)(4,1)} %bitcast.69), calls=%async_computation.13 | async-start | bytes 8388608
  89.7 7.1 %slice-start.2 = ((s8[10485760]{0:T(1024)(128)(4,1)}), s8[2097152]{0:T(1024)(128)(4,1)S(1)}, s32[]{:S(2)}) async-start(s8[10485760]{0:T(1024)(128)(4,1)} %bitcast.69), calls=%async_computation.14 | async-start | bytes 4194304
  96.8 14.9 %copy-start.1 = (f32[32,2]{0,1:T(2,128)S(1)}, f32[32,2]{0,1:T(2,128)}, u32[]{:S(2)}) copy-start(f32[32,2]{0,1:T(2,128)} %param.11) | copy-start | bytes 772
  101.2 97.2 %reduce-scatter.6.cloned.1.call-start = ((), (), s32[]{:S(2)}) async-start(), calls=%async_computation.7 | async-start | bytes 409600 | tf_op jit(solution)/shard_map/reduce_scatter | solution.py:81
  172.0 26.5 %all-to-all-start.1 = ((bf16[4,32,1280]{2,1,0:T(8,128)(2,1)}), bf16[4,32,1280]{2,1,0:T(8,128)(2,1)S(1)}, u32[]{:S(2)}, u32[]{:S(2)}) async-start(bf16[4,32,1280]{2,1,0:T(8,128)(2,1)} %bitcast.80), calls=%async_computation.4 | async-start | bytes 655360 | tf_op jit(solution)/shard_map/all_to_all | solution.py:51
  175.6 82.8 %all-gather.8.cloned.1.call-start = ((), (), s32[]{:S(2)}) async-start(), calls=%async_computation.10 | async-start | bytes 1392640 | tf_op jit(solution)/shard_map/all_gather | solution.py:90
  200.9 131.6 %all-reduce.3.cloned.1.call-start = ((), (), s32[]{:S(2)}) async-start(), calls=%async_computation.11 | async-start | bytes 31457280 | tf_op jit(solution)/shard_map/psum | solution.py:103
Sparse Core Ops, SparseCore 0:
  25.2 34.9 all-gather.3
  61.7 11.3 all-gather.5
  82.0 29.6 reduce-scatter.3
  114.5 57.4 reduce-scatter.7
  174.6 23.8 reduce-scatter.5
  201.6 56.7 all-gather.7
  277.5 54.8 all-reduce.2
where the time goes:
time: 363 us; the launch traced here: 361 us
  waiting for transfers between devices  167 us (46%)
  blocking collectives  77.7 us (21%)
  matrix products  51.2 us (14%)
  local copies, waits for them, and re-layouts  44.4 us (12%)
  between operations  16.1 us (4%)
  starting transfers between devices  4.08 us (1%)
    reduce_scatter x1, waiting for transfers between devices, body(): lax.psum_scatter(teacher_part.astype(jnp.bfloat16), ('dp', 'tensor'), sca...  60.2 us
    all_gather x1, waiting for transfers between devices, body(): gathered = lax.all_gather(d_out, ('expert', 'tensor'), axis=0, tiled=True)  57.3 us
    psum x1, blocking collectives, body(): lax.psum(jnp.sum(residual * residual), ('dp', 'expert', 'tensor'))  38.4 us
    reduce_scatter x1, waiting for transfers between devices, body(): lax.psum_scatter(column_part, 'expert', scatter_dimension=0, tiled=True)  22.8 us
    unnamed x16, local copies, waits for them, and re-layouts  21.8 us
    all_to_all x1, blocking collectives, body(): lax.all_to_all(sent, 'expert', split_axis=0, concat_axis=0, tiled=True)  21.5 us
    another operation x1, local copies, waits for them, and re-layouts, body(): t_down[0].reshape(hidden_local, tensor_count, slice_width)  19.4 us
    all_gather x1, blocking collectives, body(): full_rows = lax.all_gather(tokens, 'tensor', axis=1, tiled=True)  17.9 us
  transfers between devices with their start and end apart: 8, of which 5 were waited for; matrix products, arithmetic and copies ran while one was open for 15% of the time, Pallas kernels for 0%

commit v1 on v0

v1 whole, which is shorter than its diff:
```python
import functools
import math

import jax
import jax.numpy as jnp
from jax import lax
from jax.experimental import pallas as pl
from jax.experimental.pallas import tpu as pltpu
from jax.sharding import PartitionSpec as P

BF = jnp.bfloat16
F32 = jnp.float32
ANY = pl.BlockSpec(memory_space=pl.ANY)
VMEM_LIMIT = 60 * 1024 * 1024


def swap(x, axis, n, r):
    return lax.ppermute(x, axis, [(i, i ^ r) for i in range(n)])


def tile_of(n, most):
    t = min(n, most)
    while n % t:
        t //= 2
    return t


def cost(flops, moved):
    return pl.CostEstimate(flops=int(flops), bytes_accessed=int(moved), transcendentals=0)


def params(n=1):
    return pltpu.CompilerParams(
        dimension_semantics=("arbitrary",) * n, vmem_limit_bytes=VMEM_LIMIT
    )


def dot(a, b):
    return jnp.dot(a, b, preferred_element_type=F32)


def up_kernel(nd, ne, nz, rows, width, steps_t, sc, w_ref, tg, tu, sg, su, *rest):
    pieces = rest[: nd * ne]
    at_ref, act_ref, f1_ref, f2_ref, xs, sem = rest[nd * ne :]
    step = pl.program_id(0)

    @pl.when(step == 0)
    def _():
        copies = []
        for a in range(nd):
            for b in range(ne):
                for j in range(nz):
                    row = pl.multiple_of((b * nd + (sc[0] ^ a)) * rows, rows)
                    col = pl.multiple_of((sc[2] ^ j) * width, 128)
                    copies.append(
                        pltpu.make_async_copy(
                            pieces[a * ne + b].at[j],
                            xs.at[pl.ds(row, rows), pl.ds(col, width)],
                            sem.at[(a * ne + b) * nz + j],
                        )
                    )
        for c in copies:
            c.start()
        for c in copies:
            c.wait()

    @pl.when(step < steps_t)
    def _():
        g = dot(xs[...], tg[0])
        u = dot(xs[...], tu[0])
        w = w_ref[...]
        a = g * jax.nn.sigmoid(g) * u
        at_ref[...] = jnp.where(w != 0.0, -w * a, 0.0).astype(BF)

    @pl.when(step >= steps_t)
    def _():
        g = dot(xs[...], sg[...])
        u = dot(xs[...], su[...])
        s = jax.nn.sigmoid(g)
        f2 = g * s
        act_ref[...] = (f2 * u).astype(BF)
        f1_ref[...] = u * s * (1.0 + g * (1.0 - s))
        f2_ref[...] = f2


def up_call(sc, w_rows, t_gate, t_up, s_gate, s_up, pieces, dims):
    nd, ne, nz, rows, width = dims
    total, model = rows * nd * ne, width * nz
    ht, hs = t_gate.shape[2], s_gate.shape[1]
    bt, bs = tile_of(ht, 256), tile_of(hs, 256)
    nt, ns = ht // bt, hs // bs
    t_at = lambda i, sc: jnp.minimum(i, nt - 1)
    s_at = lambda i, sc: jnp.maximum(i - nt, 0)
    return pl.pallas_call(
        functools.partial(up_kernel, nd, ne, nz, rows, width, nt),
        grid_spec=pltpu.PrefetchScalarGridSpec(
            num_scalar_prefetch=1,
            grid=(nt + ns,),
            in_specs=[
                pl.BlockSpec((total, 1), lambda i, sc: (0, 0)),
                pl.BlockSpec((1, model, bt), lambda i, sc: (0, 0, t_at(i, sc))),
                pl.BlockSpec((1, model, bt), lambda i, sc: (0, 0, t_at(i, sc))),
                pl.BlockSpec((model, bs), lambda i, sc: (0, s_at(i, sc))),
                pl.BlockSpec((model, bs), lambda i, sc: (0, s_at(i, sc))),
            ]
            + [ANY] * (nd * ne),
            out_specs=[
                pl.BlockSpec((total, bt), lambda i, sc: (0, t_at(i, sc))),
                pl.BlockSpec((total, bs), lambda i, sc: (0, s_at(i, sc))),
                pl.BlockSpec((total, bs), lambda i, sc: (0, s_at(i, sc))),
                pl.BlockSpec((total, bs), lambda i, sc: (0, s_at(i, sc))),
                pl.BlockSpec((total, model), lambda i, sc: (0, 0)),
            ],
            scratch_shapes=[pltpu.SemaphoreType.DMA((nd * ne * nz,))],
        ),
        out_shape=[
            jax.ShapeDtypeStruct((total, ht), BF),
            jax.ShapeDtypeStruct((total, hs), BF),
            jax.ShapeDtypeStruct((total, hs), F32),
            jax.ShapeDtypeStruct((total, hs), F32),
            jax.ShapeDtypeStruct((total, model), BF),
        ],
        compiler_params=params(),
        cost_estimate=cost(4 * total * model * (ht + hs), 4 * model * (ht + hs)),
        name="up",
    )(sc, w_rows, t_gate, t_up, s_gate, s_up, *pieces)


def down_kernel(with_student, sc, at, act, td, sd, out):
    p = dot(at[...], td[0])
    if with_student:
        p = p + dot(act[...], sd[...])
    out[...] = p.astype(BF)


def down_call(sc, at, act, t_down, s_down, nd, with_student):
    total, ht = at.shape
    hs, model = s_down.shape
    half = model // nd
    bn = tile_of(half, 512)
    n = half // bn
    return pl.pallas_call(
        functools.partial(down_kernel, with_student),
        grid_spec=pltpu.PrefetchScalarGridSpec(
            num_scalar_prefetch=1,
            grid=(n,),
            in_specs=[
                pl.BlockSpec((total, ht), lambda i, sc: (0, 0)),
                pl.BlockSpec((total, hs), lambda i, sc: (0, 0)),
                pl.BlockSpec((1, ht, bn), lambda i, sc: (0, 0, sc[0] * n + i)),
                pl.BlockSpec((hs, bn), lambda i, sc: (0, sc[0] * n + i))
                if with_student
                else ANY,
            ],
            out_specs=pl.BlockSpec((total, bn), lambda i, sc: (0, i)),
        ),
        out_shape=jax.ShapeDtypeStruct((total, half), BF),
        compiler_params=params(),
        cost_estimate=cost(2 * total * half * (ht + hs), 2 * half * (ht + hs)),
        name="down",
    )(sc, at, act, t_down, s_down)


def back_kernel(ne, last, n, model_tokens, grad_scale, sc, act, sd, *rest):
    blocks = rest[:ne]
    if last:
        dact_in, sq_in, f1, f2, gd_in, gd, dgp, dup, loss, acc, sq, act_t = rest[ne:]
    else:
        gd, acc, sq, act_t = rest[ne:]
    step = pl.program_id(0)

    @pl.when(step == 0)
    def _():
        act_t[...] = act[...].T
        if last:
            acc[...] = dact_in[...]
        else:
            acc[...] = jnp.zeros_like(acc)
        sq[...] = jnp.zeros_like(sq)

    d = jnp.concatenate([b[...] for b in blocks], axis=0)
    acc[...] += lax.dot_general(d, sd[...], (((1,), (1,)), ((), ())), preferred_element_type=F32)
    gd[...] = dot(act_t[...], d).astype(BF)
    f = d.astype(F32)
    s = sq[...]
    for k in range(d.shape[1] // 128):
        part = f[:, k * 128 : (k + 1) * 128]
        s = s + part * part
    sq[...] = s

    if last:

        @pl.when(step == n - 1)
        def _():
            dact = acc[...]
            dgp[...] = (dact * f1[...]).astype(BF)
            dup[...] = (dact * f2[...]).astype(BF)
            rb = sq.shape[0] // ne
            first = sc[0] == 1
            tot = jnp.zeros((rb, 128), F32)
            for e in range(ne):
                row = pl.multiple_of((sc[1] ^ e) * rb, rb)
                tot = tot + jnp.where(first, sq_in[pl.ds(row, rb), :], sq[pl.ds(row, rb), :])
            for e in range(ne):
                row = pl.multiple_of((sc[1] ^ e) * rb, rb)
                tot = tot + jnp.where(first, sq[pl.ds(row, rb), :], sq_in[pl.ds(row, rb), :])
            value = jnp.sum(jnp.sum(tot, axis=0, keepdims=True), axis=1, keepdims=True)
            loss[...] = value * (1.0 / (grad_scale * grad_scale)) / model_tokens


def back_call(sc, act, s_down, blocks, nd, carry, model_tokens, grad_scale):
    total, hs = act.shape
    model = s_down.shape[1]
    half = model // nd
    ne = len(blocks)
    rb = total // ne
    bn = tile_of(half, 512)
    n = half // bn
    last = carry is not None
    whole = lambda i, sc: (0, 0)
    col = lambda i, sc: (0, sc[0] * n + i)
    in_specs = [
        pl.BlockSpec((total, hs), whole),
        pl.BlockSpec((hs, bn), col),
    ] + [pl.BlockSpec((rb, bn), lambda i, sc: (0, i))] * ne
    args = [sc, act, s_down, *blocks]
    gd_shape = jax.ShapeDtypeStruct((hs, model), BF)
    if last:
        dact, sq, f1, f2, gd = carry
        in_specs += [
            pl.BlockSpec((total, hs), whole),
            pl.BlockSpec((total, 128), whole),
            pl.BlockSpec((total, hs), whole),
            pl.BlockSpec((total, hs), whole),
            ANY,
        ]
        args += [dact, sq, f1, f2, gd]
        out_specs = [
            pl.BlockSpec((hs, bn), col),
            pl.BlockSpec((total, hs), whole),
            pl.BlockSpec((total, hs), whole),
            pl.BlockSpec((1, 1), whole),
        ]
        out_shape = [
            gd_shape,
            jax.ShapeDtypeStruct((total, hs), BF),
            jax.ShapeDtypeStruct((total, hs), BF),
            jax.ShapeDtypeStruct((1, 1), F32),
        ]
        scratch = [
            pltpu.VMEM((total, hs), F32),
            pltpu.VMEM((total, 128), F32),
            pltpu.VMEM((hs, total), BF),
        ]
        aliases = {len(args) - 1: 0}
    else:
        out_specs = [
            pl.BlockSpec((hs, bn), col),
            pl.BlockSpec((total, hs), whole),
            pl.BlockSpec((total, 128), whole),
        ]
        out_shape = [
            gd_shape,
            jax.ShapeDtypeStruct((total, hs), F32),
            jax.ShapeDtypeStruct((total, 128), F32),
        ]
        scratch = [pltpu.VMEM((hs, total), BF)]
        aliases = {}
    return pl.pallas_call(
        functools.partial(back_kernel, ne, last, n, model_tokens, grad_scale),
        grid_spec=pltpu.PrefetchScalarGridSpec(
            num_scalar_prefetch=1,
            grid=(n,),
            in_specs=in_specs,
            out_specs=out_specs,
            scratch_shapes=scratch,
        ),
        out_shape=out_shape,
        input_output_aliases=aliases,
        compiler_params=params(),
        cost_estimate=cost(4 * total * half * hs, 4 * half * hs),
        name="back",
    )(*args)


def grad_kernel(xs, dgp, dup, gg, gu):
    x = xs[...]
    dims = (((0,), (0,)), ((), ()))
    gg[...] = lax.dot_general(x, dgp[...], dims, preferred_element_type=F32).astype(BF)
    gu[...] = lax.dot_general(x, dup[...], dims, preferred_element_type=F32).astype(BF)


def grad_call(xs, dgp, dup):
    total, model = xs.shape
    hs = dgp.shape[1]
    bn = tile_of(model, 512)
    whole = lambda i: (0, 0)
    return pl.pallas_call(
        grad_kernel,
        grid=(model // bn,),
        in_specs=[
            pl.BlockSpec((total, bn), lambda i: (0, i)),
            pl.BlockSpec((total, hs), whole),
            pl.BlockSpec((total, hs), whole),
        ],
        out_specs=[pl.BlockSpec((bn, hs), lambda i: (i, 0))] * 2,
        out_shape=[jax.ShapeDtypeStruct((model, hs), BF)] * 2,
        compiler_params=params(),
        cost_estimate=cost(4 * total * model * hs, 4 * model * hs),
        name="grad",
    )(xs, dgp, dup)


def body(tokens, expert_ids, gate_weights, t_gate, t_up, t_down, s_gate, s_up, s_down):
    nd, ne, nz = lax.axis_size("dp"), lax.axis_size("expert"), lax.axis_size("tensor")
    dp, ex, tz = lax.axis_index("dp"), lax.axis_index("expert"), lax.axis_index("tensor")
    rows, width = tokens.shape
    model = width * nz
    total = rows * ne * nd
    sc = jnp.stack([dp, ex, tz]).astype(jnp.int32)

    share = gate_weights / jnp.sum(gate_weights, axis=1, keepdims=True)
    names = expert_ids[:, :, None] == jnp.arange(ne, dtype=jnp.int32)[None, None, :]
    mix = jnp.sum(jnp.where(names, share[:, :, None], 0.0), axis=1)
    other = swap(mix, "dp", nd, 1)
    pair = jnp.where(dp == 0, jnp.stack([mix, other]), jnp.stack([other, mix]))
    mixes = [pair] + [swap(pair, "expert", ne, b) for b in range(1, ne)]
    w_all = jnp.stack(mixes).reshape(total, ne)
    own = jnp.arange(ne, dtype=jnp.int32)[None, :] == ex
    w_rows = jnp.sum(jnp.where(own, w_all, 0.0), axis=1, keepdims=True)

    zs = jnp.stack([tokens] + [swap(tokens, "tensor", nz, j) for j in range(1, nz)])
    xy = [zs] + [swap(zs, "expert", ne, b) for b in range(1, ne)]
    far = [swap(x, "dp", nd, 1) for x in xy]
    at, act, f1, f2, xs = up_call(
        sc, w_rows, t_gate, t_up, s_gate, s_up, xy + far, (nd, ne, nz, rows, width)
    )

    mine, theirs = dp[None].astype(jnp.int32), (1 - dp)[None].astype(jnp.int32)
    sent = down_call(theirs, at, act, t_down, s_down, nd, False)
    kept = down_call(mine, at, act, t_down, s_down, nd, True)
    got = swap(sent, "dp", nd, 1)
    half = model // nd
    rb = total // ne
    q = [
        (
            kept[b * rb : (b + 1) * rb].astype(F32) + got[b * rb : (b + 1) * rb].astype(F32)
        ).astype(BF)
        for b in range(ne)
    ]
    parts = [q[0]] + [swap(q[b], "expert", ne, b) for b in range(1, ne)]
    r = sum(p.astype(F32) for p in parts).astype(BF).reshape(nz, rb // nz, half)
    piece = lambda j: lax.dynamic_index_in_dim(r, tz ^ j, 0, keepdims=False)
    pieces = [piece(0)] + [swap(piece(j), "tensor", nz, j) for j in range(1, nz)]
    diff = sum(p.astype(F32) for p in pieces)
    grad_scale = 1.0 / math.sqrt(total)
    d_out = (diff * grad_scale).astype(BF)

    dz = [d_out] + [swap(d_out, "tensor", nz, j) for j in range(1, nz)]
    block = jnp.zeros((nz, rb // nz, half), BF)
    for j in range(nz):
        block = lax.dynamic_update_index_in_dim(block, dz[j], tz ^ j, 0)
    block = block.reshape(rb, half)
    near = [block] + [swap(block, "expert", ne, b) for b in range(1, ne)]
    far = [swap(x, "dp", nd, 1) for x in near]
    back = functools.partial(back_call, nd=nd, model_tokens=total * model, grad_scale=grad_scale)
    gd, dact, sq = back(jnp.stack([dp, ex]).astype(jnp.int32), act, s_down, near, carry=None)
    gd, dgp, dup, loss = back(
        jnp.stack([1 - dp, ex]).astype(jnp.int32), act, s_down, far, carry=(dact, sq, f1, f2, gd)
    )
    gg, gu = grad_call(xs, dgp, dup)
    return gg, gu, gd, loss[0, 0]


def solution(mesh):
    return jax.shard_map(
        body,
        mesh=mesh,
        in_specs=(
            P(("dp", "expert"), "tensor"),
            P(("dp", "expert"), None),
            P(("dp", "expert"), None),
            P("expert", None, ("dp", "tensor")),
            P("expert", None, ("dp", "tensor")),
            P("expert", ("dp", "tensor"), None),
            P(None, ("expert", "tensor")),
            P(None, ("expert", "tensor")),
            P(("expert", "tensor"), None),
        ),
        out_specs=(
            P(None, ("expert", "tensor")),
            P(None, ("expert", "tensor")),
            P(("expert", "tensor"), None),
            P(),
        ),
        check_vma=False,
    )
```

time: 363 us -> 159 us (0.44)
  waiting for transfers between devices: 167 us -> 56.7 us
  blocking collectives: 77.7 us -> 0 us
  Pallas kernels: 0 us -> 59.3 us
  matrix products: 51.2 us -> 0 us
  local copies, waits for them, and re-layouts: 44.4 us -> 3.49 us
  starting transfers between devices: 4.08 us -> 30.3 us
  between operations: 16.1 us -> 0.9 us
  other arithmetic: 1.23 us -> 7.5 us
    reduce_scatter x3 -> x0, waiting for transfers between devices: 93.4 us -> none  [the longest x1 60.2 us: body(): lax.psum_scatter(teacher_part.astype(jnp.bfloat16), ('dp', 'tensor'), sca...]
    pallas_call x0 -> x6, Pallas kernels: none -> 59.3 us  [the longest x1 21.6 us: up_call(): pl.pallas_call(functools.partial(up_kernel, nd, ne, nz, rows, width, nt),...]
    all_gather x3 -> x0, waiting for transfers between devices: 57.3 us -> none  [the longest x1 57.3 us: body(): gathered = lax.all_gather(d_out, ('expert', 'tensor'), axis=0, tiled=True)]
    ppermute x0 -> x31, waiting for transfers between devices: none -> 56.7 us  [swap(): return lax.ppermute(x, axis, [(i, i ^ r) for i in range(n)])]
    dot_general x12 -> x0, matrix products: 51.2 us -> none  [the longest x1 7.67 us: body(): jnp.dot(shard_rows, t_gate[0], preferred_element_type=jnp.float32)]
    psum x1 -> x0, blocking collectives: 38.4 us -> none  [body(): lax.psum(jnp.sum(residual * residual), ('dp', 'expert', 'tensor'))]
    ppermute x0 -> x31, starting transfers between devices: none -> 30.3 us  [swap(): return lax.ppermute(x, axis, [(i, i ^ r) for i in range(n)])]
    all_to_all x1 -> x0, blocking collectives: 21.5 us -> none  [body(): lax.all_to_all(sent, 'expert', split_axis=0, concat_axis=0, tiled=True)]
  transfers between devices with their start and end apart: 8 -> 31, of which waited for: 5 -> 16; matrix products, arithmetic and copies ran while one was open for 15% -> 3% of each run, Pallas kernels for 0% -> 9%
where the time goes in v1:
time: 159 us; the launch traced here: 158 us
  Pallas kernels  59.3 us (37%)
  waiting for transfers between devices  56.7 us (36%)
  starting transfers between devices  30.3 us (19%)
  other arithmetic  7.5 us (5%)
  local copies, waits for them, and re-layouts  3.49 us (2%)
    ppermute x31, waiting for transfers between devices, swap(): return lax.ppermute(x, axis, [(i, i ^ r) for i in range(n)])  56.7 us
    ppermute x31, starting transfers between devices, swap(): return lax.ppermute(x, axis, [(i, i ^ r) for i in range(n)])  30.3 us
    pallas_call x1, Pallas kernels, up_call(): pl.pallas_call(functools.partial(up_kernel, nd, ne, nz, rows, width, nt),...  21.6 us
    pallas_call x2, Pallas kernels, back_call(): pl.pallas_call(functools.partial(back_kernel, ne, last, n, model_tokens,...  14.9 us
    pallas_call x2, Pallas kernels, down_call(): pl.pallas_call(functools.partial(down_kernel, with_student), grid_spec=pl...  13.2 us
    pallas_call x1, Pallas kernels, grad_call(): pl.pallas_call(grad_kernel, grid=(model // bn,), in_specs=[pl.BlockSpec((...  9.65 us
  transfers between devices with their start and end apart: 31, of which 16 were waited for; matrix products, arithmetic and copies ran while one was open for 3% of the time, Pallas kernels for 9%

profile of v1, /device:TPU:0, one launch (start us, length us, event | category | flops | bytes accessed | tf_op | source)
XLA Modules:
  0.0 158.3 jit_solution(15939341619226652877)
XLA Ops:
  0.6 3.1 %collective-permute-start.4 = (bf16[32,1280]{1,0:T(8,128)(2,1)}, bf16[32,1280]{1,0:T(8,128)(2,1)S(1)}, u32[]{:S(2)}, u32[]{:S(2)}) collective-permute-start(bf16[32,1280]{1,0:T(8,128)(2,1)} %param.9), channel_id=1, source_target_pairs={{0,1},{1,0},{2,3},{3,2},{4,5},{5,4},{6,7},{7,6},{8,9},{9,8},{10,11... | collective-permute-start | bytes 245768 | tf_op jit(solution)/shard_map/ppermute | solution.py:18
  3.7 2.5 %collective-permute-start.6 = (bf16[32,1280]{1,0:T(8,128)(2,1)}, bf16[32,1280]{1,0:T(8,128)(2,1)S(1)}, u32[]{:S(2)}, u32[]{:S(2)}) collective-permute-start(bf16[32,1280]{1,0:T(8,128)(2,1)} %param.9), channel_id=1, source_target_pairs={{0,3},{1,2},{2,1},{3,0},{4,7},{5,6},{6,5},{7,4},{8,11},{9,10},{10,... | collective-permute-start | bytes 245768 | tf_op jit(solution)/shard_map/ppermute | solution.py:18
  6.2 0.1 collective-permute-start.5
  6.3 0.7 reduce_sum.27
  7.0 0.7 broadcast_divide_fusion
  7.7 3.8 %collective-permute-done.6 = bf16[32,1280]{1,0:T(8,128)(2,1)S(1)} collective-permute-done((bf16[32,1280]{1,0:T(8,128)(2,1)}, bf16[32,1280]{1,0:T(8,128)(2,1)S(1)}, u32[]{:S(2)}, u32[]{:S(2)}) %collective-permute-start.6) | collective-permute-done | bytes 81952 | tf_op jit(solution)/shard_map/ppermute | solution.py:18
  11.5 2.6 %collective-permute-done.5 = bf16[32,1280]{1,0:T(8,128)(2,1)S(1)} collective-permute-done((bf16[32,1280]{1,0:T(8,128)(2,1)}, bf16[32,1280]{1,0:T(8,128)(2,1)S(1)}, u32[]{:S(2)}, u32[]{:S(2)}) %collective-permute-start.5) | collective-permute-done | bytes 81952 | tf_op jit(solution)/shard_map/ppermute | solution.py:18
  14.1 0.9 pad_maximum_fusion.rest_0_
  15.1 2.5 %collective-permute-start.9 = (bf16[4,32,1280]{2,1,0:T(8,128)(2,1)S(1)}, bf16[4,32,1280]{2,1,0:T(8,128)(2,1)S(1)}, u32[]{:S(2)}, u32[]{:S(2)}) collective-permute-start(bf16[4,32,1280]{2,1,0:T(8,128)(2,1)S(1)} %pad_maximum_fusion.rest_0_), channel_id=1, source_target_pairs={{0,12},{4,8},{8,4},{12,0},{1,13},{5,9},{9,5},{13,1},{2,14},{6,10},... | collective-permute-start | bytes 983048 | tf_op jit(solution)/shard_map/ppermute | solution.py:18
  17.6 0.5 collective-permute-start.8
  18.1 0.5 collective-permute-start.7
  18.6 0.7 select_reduce_fusion
  19.3 1.2 collective-permute-done
  20.5 2.4 %collective-permute-start.3 = (f32[2,32,4]{1,2,0:T(4,128)S(1)}, f32[2,32,4]{1,2,0:T(4,128)S(1)}, u32[]{:S(2)}, u32[]{:S(2)}) collective-permute-start(f32[2,32,4]{1,2,0:T(4,128)S(1)} %maximum_select_fusion.2), channel_id=1, source_target_pairs={{0,12},{4,8},{8,4},{12,0},{1,13},{5,9},{9,5},{13,1},{2,14},{6,10},... | collective-permute-start | bytes 3080 | tf_op jit(solution)/shard_map/ppermute | solution.py:18
  22.9 0.5 collective-permute-start.2
  23.4 9.2 %collective-permute-done.3 = f32[2,32,4]{1,2,0:T(4,128)S(1)} collective-permute-done((f32[2,32,4]{1,2,0:T(4,128)S(1)}, f32[2,32,4]{1,2,0:T(4,128)S(1)}, u32[]{:S(2)}, u32[]{:S(2)}) %collective-permute-start.3) | collective-permute-done | bytes 1056 | tf_op jit(solution)/shard_map/ppermute | solution.py:18
  32.6 0.5 collective-permute-start.13
  33.1 0.1 collective-permute-start.12
  33.2 0.4 collective-permute-start.11
  33.7 0.6 pad_add_fusion.sc
  34.3 1.5 collective-permute-start.1
  35.8 2.1 %collective-permute-done.1 = f32[2,32,4]{1,2,0:T(4,128)S(1)} collective-permute-done((f32[2,32,4]{1,2,0:T(4,128)S(1)}, f32[2,32,4]{1,2,0:T(4,128)S(1)}, u32[]{:S(2)}, u32[]{:S(2)}) %collective-permute-start.1) | collective-permute-done | bytes 1056 | tf_op jit(solution)/shard_map/ppermute | solution.py:18
  37.9 0.1 fusion.4
  38.0 0.8 broadcast_in_dim.60.w_ref
  38.8 0.6 copy-done.5
  39.5 0.1 copy-done.6
  39.6 0.1 copy-done.7
  39.7 0.7 copy-done.8
  40.4 21.6 %up.1 = (bf16[256,1024]{1,0:T(8,128)(2,1)}, bf16[256,512]{1,0:T(8,128)(2,1)}, f32[256,512]{1,0:T(8,128)}, f32[256,512]{1,0:T(8,128)}, bf16[256,5120]{1,0:T(8,128)(2,1)}) custom-call(s32[3]{0:T(128)} %pad_add_fusion.sc, f32[256,1]{1,0:T(8,128)} %broadcast_in_dim.60.w_ref, bf16[1,5120,1024]{2,1,0:T(8,128)(2,1)} %tg.1, bf16[1,5120,1024]{2,1,0:T(8,128)(2,1)} %tu.1, ...), custom_call_target="tpu_custom_call" | custom-call | flops 8053063680 | bytes 31457280 | tf_op jit(solution)/shard_map/up/pallas_call | solution.py:94
  62.0 6.2 %down.3 = bf16[256,2560]{1,0:T(8,128)(2,1)} custom-call(s32[1]{0:T(128)} %bitcast.14.sc, bf16[256,1024]{1,0:T(8,128)(2,1)} %get-tuple-element.20.at, bf16[256,512]{1,0:T(8,128)(2,1)} %get-tuple-element.19.act, bf16[1,1024,5120]{2,1,0:T(8,128)(2,1)} %td.3, bf16[512,5120]{1,0:T(8,128)(2,1)} %sd.7), custom_call_target="tpu_custom_call" | custom-call | flops 2013265920 | bytes 7864320 | tf_op jit(solution)/shard_map/down/pallas_call | solution.py:142
  68.2 7.0 %down.2 = bf16[256,2560]{1,0:T(8,128)(2,1)} custom-call(s32[1]{0:T(128)} %bitcast.sc, bf16[256,1024]{1,0:T(8,128)(2,1)} %get-tuple-element.20.at, bf16[256,512]{1,0:T(8,128)(2,1)} %get-tuple-element.19.act, bf16[1,1024,5120]{2,1,0:T(8,128)(2,1)} %td.3, bf16[512,5120]{1,0:T(8,128)(2,1)} %sd.7), custom_call_target="tpu_custom_call" | custom-call | flops 2013265920 | bytes 7864320 | tf_op jit(solution)/shard_map/down/pallas_call | solution.py:142
  75.2 1.4 add_convert_fusion.3
  76.6 1.6 collective-permute-start.15
  78.2 1.5 collective-permute-start.17
  79.7 0.5 collective-permute-start.16
  80.2 7.1 %collective-permute-done.15 = bf16[64,2560]{1,0:T(8,128)(2,1)S(1)} collective-permute-done((bf16[64,2560]{1,0:T(8,128)(2,1)S(1)}, bf16[64,2560]{1,0:T(8,128)(2,1)S(1)}, u32[]{:S(2)}, u32[]{:S(2)}) %collective-permute-start.15) | collective-permute-done | bytes 327712 | tf_op jit(solution)/shard_map/ppermute | solution.py:18
  87.3 7.6 %collective-permute-done.17 = bf16[64,2560]{1,0:T(8,128)(2,1)S(1)} collective-permute-done((bf16[64,2560]{1,0:T(8,128)(2,1)S(1)}, bf16[64,2560]{1,0:T(8,128)(2,1)S(1)}, u32[]{:S(2)}, u32[]{:S(2)}) %collective-permute-start.17) | collective-permute-done | bytes 327712 | tf_op jit(solution)/shard_map/ppermute | solution.py:18
  94.9 1.4 collective-permute-done.16
  96.2 1.2 add_convert_fusion
  97.5 0.1 collective-permute-start.18
  97.5 1.7 %collective-permute-start.20 = (bf16[16,2560]{1,0:T(8,128)(2,1)S(1)}, bf16[16,2560]{1,0:T(8,128)(2,1)S(1)}, u32[]{:S(2)}, u32[]{:S(2)}) collective-permute-start(bf16[16,2560]{1,0:T(8,128)(2,1)S(1)} %get-tuple-element.38), channel_id=1, source_target_pairs={{0,3},{1,2},{2,1},{3,0},{4,7},{5,6},{6,5},{7,4},{8,11},{9,10},{10,... | collective-permute-start | bytes 245768 | tf_op jit(solution)/shard_map/ppermute | solution.py:18
  99.3 1.8 %collective-permute-start.19 = (bf16[16,2560]{1,0:T(8,128)(2,1)S(1)}, bf16[16,2560]{1,0:T(8,128)(2,1)S(1)}, u32[]{:S(2)}, u32[]{:S(2)}) collective-permute-start(bf16[16,2560]{1,0:T(8,128)(2,1)S(1)} %get-tuple-element.39), channel_id=1, source_target_pairs={{0,2},{1,3},{2,0},{3,1},{4,6},{5,7},{6,4},{7,5},{8,10},{9,11},{10,... | collective-permute-start | bytes 245768 | tf_op jit(solution)/shard_map/ppermute | solution.py:18
  101.0 2.3 %collective-permute-done.18 = bf16[16,2560]{1,0:T(8,128)(2,1)S(1)} collective-permute-done((bf16[16,2560]{1,0:T(8,128)(2,1)S(1)}, bf16[16,2560]{1,0:T(8,128)(2,1)S(1)}, u32[]{:S(2)}, u32[]{:S(2)}) %collective-permute-start.18) | collective-permute-done | bytes 81952 | tf_op jit(solution)/shard_map/ppermute | solution.py:18
  103.3 1.1 collective-permute-done.20
  104.4 3.1 %collective-permute-done.19 = bf16[16,2560]{1,0:T(8,128)(2,1)S(1)} collective-permute-done((bf16[16,2560]{1,0:T(8,128)(2,1)S(1)}, bf16[16,2560]{1,0:T(8,128)(2,1)S(1)}, u32[]{:S(2)}, u32[]{:S(2)}) %collective-permute-start.19) | collective-permute-done | bytes 81952 | tf_op jit(solution)/shard_map/ppermute | solution.py:18
  107.7 2.3 %collective-permute-start.22 = (bf16[16,2560]{1,0:T(8,128)(2,1)S(1)}, bf16[16,2560]{1,0:T(8,128)(2,1)S(1)}, u32[]{:S(2)}, u32[]{:S(2)}) collective-permute-start(bf16[16,2560]{1,0:T(8,128)(2,1)S(1)} %get-tuple-element.33), channel_id=1, source_target_pairs={{0,2},{1,3},{2,0},{3,1},{4,6},{5,7},{6,4},{7,5},{8,10},{9,11},{10,... | collective-permute-start | bytes 245768 | tf_op jit(solution)/shard_map/ppermute | solution.py:18
  110.0 2.0 %collective-permute-start.23 = (bf16[16,2560]{1,0:T(8,128)(2,1)S(1)}, bf16[16,2560]{1,0:T(8,128)(2,1)S(1)}, u32[]{:S(2)}, u32[]{:S(2)}) collective-permute-start(bf16[16,2560]{1,0:T(8,128)(2,1)S(1)} %get-tuple-element.33), channel_id=1, source_target_pairs={{0,3},{1,2},{2,1},{3,0},{4,7},{5,6},{6,5},{7,4},{8,11},{9,10},{10,... | collective-permute-start | bytes 245768 | tf_op jit(solution)/shard_map/ppermute | solution.py:18
  112.1 2.9 %collective-permute-done.22 = bf16[16,2560]{1,0:T(8,128)(2,1)S(1)} collective-permute-done((bf16[16,2560]{1,0:T(8,128)(2,1)S(1)}, bf16[16,2560]{1,0:T(8,128)(2,1)S(1)}, u32[]{:S(2)}, u32[]{:S(2)}) %collective-permute-start.22) | collective-permute-done | bytes 81952 | tf_op jit(solution)/shard_map/ppermute | solution.py:18
  115.1 1.3 collective-permute-done.23
  116.4 1.5 collective-permute-start.29
  117.9 1.5 collective-permute-start.27
  119.3 0.6 collective-permute-start.25
  119.9 7.6 %collective-permute-done.29.rest_3_ = bf16[64,2560]{1,0:T(8,128)(2,1)S(1)} collective-permute-done((bf16[64,2560]{1,0:T(8,128)(2,1)S(1)}, bf16[64,2560]{1,0:T(8,128)(2,1)S(1)}, u32[]{:S(2)}, u32[]{:S(2)}) %collective-permute-start.29) | collective-permute-done | bytes 327712 | tf_op jit(solution)/shard_map/ppermute | solution.py:18
  127.5 3.5 %collective-permute-done.27.rest_2_ = bf16[64,2560]{1,0:T(8,128)(2,1)S(1)} collective-permute-done((bf16[64,2560]{1,0:T(8,128)(2,1)S(1)}, bf16[64,2560]{1,0:T(8,128)(2,1)S(1)}, u32[]{:S(2)}, u32[]{:S(2)}) %collective-permute-start.27) | collective-permute-done | bytes 327712 | tf_op jit(solution)/shard_map/ppermute | solution.py:18
  131.0 0.5 collective-permute-start.26
  131.5 0.6 pad_add_fusion.2.sc
  132.1 0.6 pad_add_fusion.1.sc
  132.7 7.0 %back.2 = (bf16[512,5120]{1,0:T(8,128)(2,1)}, f32[256,512]{1,0:T(8,128)}, f32[256,128]{1,0:T(8,128)}) custom-call(s32[2]{0:T(128)} %pad_add_fusion.2.sc, bf16[256,512]{1,0:T(8,128)(2,1)} %get-tuple-element.19.act, bf16[512,5120]{1,0:T(8,128)(2,1)} %sd.7, bf16[64,2560]{1,0:T(8,128)(2,1)} %bitcast.42, bf16[64,2560]{1,0:T(8,128)(2,1)} %copy-done.15, ...), custom_call_target="tpu_custom_call" | custom-call | flops 1342177280 | bytes 5242880 | tf_op jit(solution)/shard_map/back/pallas_call | solution.py:269
  139.8 0.7 copy-done.9
  140.4 0.1 copy-done.10
  140.5 0.1 copy-done.11
  140.6 0.1 copy-done.12
  140.7 7.9 %back.3 = (bf16[512,5120]{1,0:T(8,128)(2,1)}, bf16[256,512]{1,0:T(8,128)(2,1)}, bf16[256,512]{1,0:T(8,128)(2,1)}, f32[1,1]{1,0:T(1,128)}) custom-call(s32[2]{0:T(128)} %pad_add_fusion.1.sc, bf16[256,512]{1,0:T(8,128)(2,1)} %get-tuple-element.19.act, bf16[512,5120]{1,0:T(8,128)(2,1)} %sd.7, ...), custom_call_target="tpu_custom_call", output_to_operand_aliasing={{0}: (11, {})} | custom-call | flops 1342177280 | bytes 5242880 | tf_op jit(solution)/shard_map/back/pallas_call | solution.py:269
  148.6 9.7 %grad.1 = (bf16[5120,512]{1,0:T(8,128)(2,1)}, bf16[5120,512]{1,0:T(8,128)(2,1)}) custom-call(bf16[256,5120]{1,0:T(8,128)(2,1)} %get-tuple-element.18.xs, bf16[256,512]{1,0:T(8,128)(2,1)} %get-tuple-element.26.dgp, bf16[256,512]{1,0:T(8,128)(2,1)} %get-tuple-element.27.dup), custom_call_target="tpu_custom_call" | custom-call | flops 2684354560 | bytes 10485760 | tf_op jit(solution)/shard_map/grad/pallas_call | solution.py:298
  (56 shorter events, 0.4 us)
Async XLA Ops:
  0.6 7.1 %collective-permute-start.4 = (bf16[32,1280]{1,0:T(8,128)(2,1)}, bf16[32,1280]{1,0:T(8,128)(2,1)S(1)}, u32[]{:S(2)}, u32[]{:S(2)}) collective-permute-start(bf16[32,1280]{1,0:T(8,128)(2,1)} %param.9), channel_id=1, source_target_pairs={{0,1},{1,0},{2,3},{3,2},{4,5},{5,4},{6,7},{7,6},{8,9},{9,8},{10,11... | collective-permute-start | bytes 245768 | tf_op jit(solution)/shard_map/ppermute | solution.py:18
  3.7 7.8 %collective-permute-start.6 = (bf16[32,1280]{1,0:T(8,128)(2,1)}, bf16[32,1280]{1,0:T(8,128)(2,1)S(1)}, u32[]{:S(2)}, u32[]{:S(2)}) collective-permute-start(bf16[32,1280]{1,0:T(8,128)(2,1)} %param.9), channel_id=1, source_target_pairs={{0,3},{1,2},{2,1},{3,0},{4,7},{5,6},{6,5},{7,4},{8,11},{9,10},{10,... | collective-permute-start | bytes 245768 | tf_op jit(solution)/shard_map/ppermute | solution.py:18
  6.2 7.9 %collective-permute-start.5 = (bf16[32,1280]{1,0:T(8,128)(2,1)}, bf16[32,1280]{1,0:T(8,128)(2,1)S(1)}, u32[]{:S(2)}, u32[]{:S(2)}) collective-permute-start(bf16[32,1280]{1,0:T(8,128)(2,1)} %param.9), channel_id=1, source_target_pairs={{0,2},{1,3},{2,0},{3,1},{4,6},{5,7},{6,4},{7,5},{8,10},{9,11},{10,... | collective-permute-start | bytes 245768 | tf_op jit(solution)/shard_map/ppermute | solution.py:18
  15.1 23.7 %copy-start = (bf16[4,32,1280]{2,1,0:T(8,128)(2,1)}, bf16[4,32,1280]{2,1,0:T(8,128)(2,1)S(1)}, u32[]{:S(2)}) copy-start(bf16[4,32,1280]{2,1,0:T(8,128)(2,1)S(1)} %pad_maximum_fusion.rest_0_) | copy-start | bytes 983044
  15.1 17.6 %collective-permute-start.9 = (bf16[4,32,1280]{2,1,0:T(8,128)(2,1)S(1)}, bf16[4,32,1280]{2,1,0:T(8,128)(2,1)S(1)}, u32[]{:S(2)}, u32[]{:S(2)}) collective-permute-start(bf16[4,32,1280]{2,1,0:T(8,128)(2,1)S(1)} %pad_maximum_fusion.rest_0_), channel_id=1, source_target_pairs={{0,12},{4,8},{8,4},{12,0},{1,13},{5,9},{9,5},{13,1},{2,14},{6,10},... | collective-permute-start | bytes 983048 | tf_op jit(solution)/shard_map/ppermute | solution.py:18
  17.6 15.6 %collective-permute-start.8 = (bf16[4,32,1280]{2,1,0:T(8,128)(2,1)S(1)}, bf16[4,32,1280]{2,1,0:T(8,128)(2,1)S(1)}, u32[]{:S(2)}, u32[]{:S(2)}) collective-permute-start(bf16[4,32,1280]{2,1,0:T(8,128)(2,1)S(1)} %pad_maximum_fusion.rest_0_), channel_id=1, source_target_pairs={{0,8},{4,12},{8,0},{12,4},{1,9},{5,13},{9,1},{13,5},{2,10},{6,14},... | collective-permute-start | bytes 983048 | tf_op jit(solution)/shard_map/ppermute | solution.py:18
  18.1 15.1 %collective-permute-start.7 = (bf16[4,32,1280]{2,1,0:T(8,128)(2,1)S(1)}, bf16[4,32,1280]{2,1,0:T(8,128)(2,1)S(1)}, u32[]{:S(2)}, u32[]{:S(2)}) collective-permute-start(bf16[4,32,1280]{2,1,0:T(8,128)(2,1)S(1)} %pad_maximum_fusion.rest_0_), channel_id=1, source_target_pairs={{0,4},{4,0},{8,12},{12,8},{1,5},{5,1},{9,13},{13,9},{2,6},{6,2},{1... | collective-permute-start | bytes 983048 | tf_op jit(solution)/shard_map/ppermute | solution.py:18
  19.3 1.2 collective-permute-start
  20.5 12.1 %collective-permute-start.3 = (f32[2,32,4]{1,2,0:T(4,128)S(1)}, f32[2,32,4]{1,2,0:T(4,128)S(1)}, u32[]{:S(2)}, u32[]{:S(2)}) collective-permute-start(f32[2,32,4]{1,2,0:T(4,128)S(1)} %maximum_select_fusion.2), channel_id=1, source_target_pairs={{0,12},{4,8},{8,4},{12,0},{1,13},{5,9},{9,5},{13,1},{2,14},{6,10},... | collective-permute-start | bytes 3080 | tf_op jit(solution)/shard_map/ppermute | solution.py:18
  22.9 11.3 %collective-permute-start.2 = (f32[2,32,4]{1,2,0:T(4,128)S(1)}, f32[2,32,4]{1,2,0:T(4,128)S(1)}, u32[]{:S(2)}, u32[]{:S(2)}) collective-permute-start(f32[2,32,4]{1,2,0:T(4,128)S(1)} %maximum_select_fusion.2), channel_id=1, source_target_pairs={{0,8},{4,12},{8,0},{12,4},{1,9},{5,13},{9,1},{13,5},{2,10},{6,14},... | collective-permute-start | bytes 3080 | tf_op jit(solution)/shard_map/ppermute | solution.py:18
  32.6 6.1 %collective-permute-start.10 = (bf16[4,32,1280]{2,1,0:T(8,128)(2,1)S(1)}, bf16[4,32,1280]{2,1,0:T(8,128)(2,1)S(1)}, u32[]{:S(2)}, u32[]{:S(2)}) collective-permute-start(bf16[4,32,1280]{2,1,0:T(8,128)(2,1)S(1)} %pad_maximum_fusion.rest_0_), channel_id=1, source_target_pairs={{0,16},{16,0},{1,17},{17,1},{2,18},{18,2},{3,19},{19,3},{4,20},{20... | collective-permute-start | bytes 983048 | tf_op jit(solution)/shard_map/ppermute | solution.py:18
  32.6 6.2 %copy-start.2 = (bf16[4,32,1280]{2,1,0:T(8,128)(2,1)}, bf16[4,32,1280]{2,1,0:T(8,128)(2,1)S(1)}, u32[]{:S(2)}) copy-start(bf16[4,32,1280]{2,1,0:T(8,128)(2,1)S(1)} %collective-permute-done.9.rest_3_) | copy-start | bytes 983044
  32.6 6.1 %collective-permute-start.13 = (bf16[4,32,1280]{2,1,0:T(8,128)(2,1)S(1)}, bf16[4,32,1280]{2,1,0:T(8,128)(2,1)S(1)}, u32[]{:S(2)}, u32[]{:S(2)}) collective-permute-start(bf16[4,32,1280]{2,1,0:T(8,128)(2,1)S(1)} %collective-permute-done.9.rest_3_), channel_id=1, source_target_pairs={{0,16},{16,0},{1,17},{17,1},{2,18},{18,2},{3,19},{19,3},{4,20},{20... | collective-permute-start | bytes 983048 | tf_op jit(solution)/shard_map/ppermute | solution.py:18
  33.1 5.7 %copy-start.3 = (bf16[4,32,1280]{2,1,0:T(8,128)(2,1)}, bf16[4,32,1280]{2,1,0:T(8,128)(2,1)S(1)}, u32[]{:S(2)}) copy-start(bf16[4,32,1280]{2,1,0:T(8,128)(2,1)S(1)} %collective-permute-done.8.rest_2_) | copy-start | bytes 983044
  33.1 5.6 %collective-permute-start.12 = (bf16[4,32,1280]{2,1,0:T(8,128)(2,1)S(1)}, bf16[4,32,1280]{2,1,0:T(8,128)(2,1)S(1)}, u32[]{:S(2)}, u32[]{:S(2)}) collective-permute-start(bf16[4,32,1280]{2,1,0:T(8,128)(2,1)S(1)} %collective-permute-done.8.rest_2_), channel_id=1, source_target_pairs={{0,16},{16,0},{1,17},{17,1},{2,18},{18,2},{3,19},{19,3},{4,20},{20... | collective-permute-start | bytes 983048 | tf_op jit(solution)/shard_map/ppermute | solution.py:18
  33.2 5.6 %copy-start.4 = (bf16[4,32,1280]{2,1,0:T(8,128)(2,1)}, bf16[4,32,1280]{2,1,0:T(8,128)(2,1)S(1)}, u32[]{:S(2)}) copy-start(bf16[4,32,1280]{2,1,0:T(8,128)(2,1)S(1)} %collective-permute-done.7.rest_1_) | copy-start | bytes 983044
  33.2 5.5 %collective-permute-start.11 = (bf16[4,32,1280]{2,1,0:T(8,128)(2,1)S(1)}, bf16[4,32,1280]{2,1,0:T(8,128)(2,1)S(1)}, u32[]{:S(2)}, u32[]{:S(2)}) collective-permute-start(bf16[4,32,1280]{2,1,0:T(8,128)(2,1)S(1)} %collective-permute-done.7.rest_1_), channel_id=1, source_target_pairs={{0,16},{16,0},{1,17},{17,1},{2,18},{18,2},{3,19},{19,3},{4,20},{20... | collective-permute-start | bytes 983048 | tf_op jit(solution)/shard_map/ppermute | solution.py:18
  34.3 3.6 %collective-permute-start.1 = (f32[2,32,4]{1,2,0:T(4,128)S(1)}, f32[2,32,4]{1,2,0:T(4,128)S(1)}, u32[]{:S(2)}, u32[]{:S(2)}) collective-permute-start(f32[2,32,4]{1,2,0:T(4,128)S(1)} %maximum_select_fusion.2), channel_id=1, source_target_pairs={{0,4},{4,0},{8,12},{12,8},{1,5},{5,1},{9,13},{13,9},{2,6},{6,2},{1... | collective-permute-start | bytes 3080 | tf_op jit(solution)/shard_map/ppermute | solution.py:18
  38.7 0.7 copy-start.5
  38.8 0.8 copy-start.6
  38.8 0.9 copy-start.7
  39.7 0.7 copy-start.8
  68.2 7.0 %collective-permute-start.14 = (bf16[256,2560]{1,0:T(8,128)(2,1)}, bf16[256,2560]{1,0:T(8,128)(2,1)S(1)}, u32[]{:S(2)}, u32[]{:S(2)}) collective-permute-start(bf16[256,2560]{1,0:T(8,128)(2,1)} %down.3), channel_id=1, source_target_pairs={{0,16},{16,0},{1,17},{17,1},{2,18},{18,2},{3,19},{19,3},{4,20},{20... | collective-permute-start | bytes 3932168 | tf_op jit(solution)/shard_map/ppermute | solution.py:18
  76.6 10.7 %collective-permute-start.15 = (bf16[64,2560]{1,0:T(8,128)(2,1)S(1)}, bf16[64,2560]{1,0:T(8,128)(2,1)S(1)}, u32[]{:S(2)}, u32[]{:S(2)}) collective-permute-start(bf16[64,2560]{1,0:T(8,128)(2,1)S(1)} %get-tuple-element.34), channel_id=1, source_target_pairs={{0,4},{4,0},{8,12},{12,8},{1,5},{5,1},{9,13},{13,9},{2,6},{6,2},{1... | collective-permute-start | bytes 983048 | tf_op jit(solution)/shard_map/ppermute | solution.py:18
  78.2 16.7 %collective-permute-start.17 = (bf16[64,2560]{1,0:T(8,128)(2,1)S(1)}, bf16[64,2560]{1,0:T(8,128)(2,1)S(1)}, u32[]{:S(2)}, u32[]{:S(2)}) collective-permute-start(bf16[64,2560]{1,0:T(8,128)(2,1)S(1)} %get-tuple-element.35), channel_id=1, source_target_pairs={{0,12},{4,8},{8,4},{12,0},{1,13},{5,9},{9,5},{13,1},{2,14},{6,10},... | collective-permute-start | bytes 983048 | tf_op jit(solution)/shard_map/ppermute | solution.py:18
  79.7 16.6 %collective-permute-start.16 = (bf16[64,2560]{1,0:T(8,128)(2,1)S(1)}, bf16[64,2560]{1,0:T(8,128)(2,1)S(1)}, u32[]{:S(2)}, u32[]{:S(2)}) collective-permute-start(bf16[64,2560]{1,0:T(8,128)(2,1)S(1)} %get-tuple-element.36), channel_id=1, source_target_pairs={{0,8},{4,12},{8,0},{12,4},{1,9},{5,13},{9,1},{13,5},{2,10},{6,14},... | collective-permute-start | bytes 983048 | tf_op jit(solution)/shard_map/ppermute | solution.py:18
  97.5 5.9 %collective-permute-start.18 = (bf16[16,2560]{1,0:T(8,128)(2,1)S(1)}, bf16[16,2560]{1,0:T(8,128)(2,1)S(1)}, u32[]{:S(2)}, u32[]{:S(2)}) collective-permute-start(bf16[16,2560]{1,0:T(8,128)(2,1)S(1)} %get-tuple-element.37), channel_id=1, source_target_pairs={{0,1},{1,0},{2,3},{3,2},{4,5},{5,4},{6,7},{7,6},{8,9},{9,8},{10,11... | collective-permute-start | bytes 245768 | tf_op jit(solution)/shard_map/ppermute | solution.py:18
  97.5 6.8 %collective-permute-start.20 = (bf16[16,2560]{1,0:T(8,128)(2,1)S(1)}, bf16[16,2560]{1,0:T(8,128)(2,1)S(1)}, u32[]{:S(2)}, u32[]{:S(2)}) collective-permute-start(bf16[16,2560]{1,0:T(8,128)(2,1)S(1)} %get-tuple-element.38), channel_id=1, source_target_pairs={{0,3},{1,2},{2,1},{3,0},{4,7},{5,6},{6,5},{7,4},{8,11},{9,10},{10,... | collective-permute-start | bytes 245768 | tf_op jit(solution)/shard_map/ppermute | solution.py:18
  99.3 8.2 %collective-permute-start.19 = (bf16[16,2560]{1,0:T(8,128)(2,1)S(1)}, bf16[16,2560]{1,0:T(8,128)(2,1)S(1)}, u32[]{:S(2)}, u32[]{:S(2)}) collective-permute-start(bf16[16,2560]{1,0:T(8,128)(2,1)S(1)} %get-tuple-element.39), channel_id=1, source_target_pairs={{0,2},{1,3},{2,0},{3,1},{4,6},{5,7},{6,4},{7,5},{8,10},{9,11},{10,... | collective-permute-start | bytes 245768 | tf_op jit(solution)/shard_map/ppermute | solution.py:18
  107.6 4.5 %collective-permute-start.21 = (bf16[16,2560]{1,0:T(8,128)(2,1)S(1)}, bf16[16,2560]{1,0:T(8,128)(2,1)S(1)}, u32[]{:S(2)}, u32[]{:S(2)}) collective-permute-start(bf16[16,2560]{1,0:T(8,128)(2,1)S(1)} %get-tuple-element.33), channel_id=1, source_target_pairs={{0,1},{1,0},{2,3},{3,2},{4,5},{5,4},{6,7},{7,6},{8,9},{9,8},{10,11... | collective-permute-start | bytes 245768 | tf_op jit(solution)/shard_map/ppermute | solution.py:18
  107.7 7.4 %collective-permute-start.22 = (bf16[16,2560]{1,0:T(8,128)(2,1)S(1)}, bf16[16,2560]{1,0:T(8,128)(2,1)S(1)}, u32[]{:S(2)}, u32[]{:S(2)}) collective-permute-start(bf16[16,2560]{1,0:T(8,128)(2,1)S(1)} %get-tuple-element.33), channel_id=1, source_target_pairs={{0,2},{1,3},{2,0},{3,1},{4,6},{5,7},{6,4},{7,5},{8,10},{9,11},{10,... | collective-permute-start | bytes 245768 | tf_op jit(solution)/shard_map/ppermute | solution.py:18
  110.0 6.3 %collective-permute-start.23 = (bf16[16,2560]{1,0:T(8,128)(2,1)S(1)}, bf16[16,2560]{1,0:T(8,128)(2,1)S(1)}, u32[]{:S(2)}, u32[]{:S(2)}) collective-permute-start(bf16[16,2560]{1,0:T(8,128)(2,1)S(1)} %get-tuple-element.33), channel_id=1, source_target_pairs={{0,3},{1,2},{2,1},{3,0},{4,7},{5,6},{6,5},{7,4},{8,11},{9,10},{10,... | collective-permute-start | bytes 245768 | tf_op jit(solution)/shard_map/ppermute | solution.py:18
  116.4 16.3 %copy-start.1 = (bf16[4,16,2560]{2,1,0:T(8,128)(2,1)}, bf16[4,16,2560]{2,1,0:T(8,128)(2,1)S(1)}, u32[]{:S(2)}) copy-start(bf16[4,16,2560]{2,1,0:T(8,128)(2,1)S(1)} %bitcast_dynamic-update-slice_fusion) | copy-start | bytes 983044
  116.4 11.1 %collective-permute-start.29 = (bf16[64,2560]{1,0:T(8,128)(2,1)S(1)}, bf16[64,2560]{1,0:T(8,128)(2,1)S(1)}, u32[]{:S(2)}, u32[]{:S(2)}) collective-permute-start(bf16[64,2560]{1,0:T(8,128)(2,1)S(1)} %bitcast.38), channel_id=1, source_target_pairs={{0,12},{4,8},{8,4},{12,0},{1,13},{5,9},{9,5},{13,1},{2,14},{6,10},... | collective-permute-start | bytes 983048 | tf_op jit(solution)/shard_map/ppermute | solution.py:18
  117.9 13.1 %collective-permute-start.27 = (bf16[64,2560]{1,0:T(8,128)(2,1)S(1)}, bf16[64,2560]{1,0:T(8,128)(2,1)S(1)}, u32[]{:S(2)}, u32[]{:S(2)}) collective-permute-start(bf16[64,2560]{1,0:T(8,128)(2,1)S(1)} %bitcast.39), channel_id=1, source_target_pairs={{0,8},{4,12},{8,0},{12,4},{1,9},{5,13},{9,1},{13,5},{2,10},{6,14},... | collective-permute-start | bytes 983048 | tf_op jit(solution)/shard_map/ppermute | solution.py:18
  119.3 11.6 %collective-permute-start.25 = (bf16[64,2560]{1,0:T(8,128)(2,1)S(1)}, bf16[64,2560]{1,0:T(8,128)(2,1)S(1)}, u32[]{:S(2)}, u32[]{:S(2)}) collective-permute-start(bf16[64,2560]{1,0:T(8,128)(2,1)S(1)} %bitcast.40), channel_id=1, source_target_pairs={{0,4},{4,0},{8,12},{12,8},{1,5},{5,1},{9,13},{13,9},{2,6},{6,2},{1... | collective-permute-start | bytes 983048 | tf_op jit(solution)/shard_map/ppermute | solution.py:18
  119.9 19.8 %collective-permute-start.24 = (bf16[64,2560]{1,0:T(8,128)(2,1)S(1)}, bf16[64,2560]{1,0:T(8,128)(2,1)S(1)}, u32[]{:S(2)}, u32[]{:S(2)}) collective-permute-start(bf16[64,2560]{1,0:T(8,128)(2,1)S(1)} %bitcast.41), channel_id=1, source_target_pairs={{0,16},{16,0},{1,17},{17,1},{2,18},{18,2},{3,19},{19,3},{4,20},{20... | collective-permute-start | bytes 983048 | tf_op jit(solution)/shard_map/ppermute | solution.py:18
  127.5 5.2 %copy-start.13 = (bf16[64,2560]{1,0:T(8,128)(2,1)}, bf16[64,2560]{1,0:T(8,128)(2,1)S(1)}, u32[]{:S(2)}) copy-start(bf16[64,2560]{1,0:T(8,128)(2,1)S(1)} %collective-permute-done.29.rest_3_) | copy-start | bytes 983044
  127.5 12.2 %collective-permute-start.30 = (bf16[64,2560]{1,0:T(8,128)(2,1)S(1)}, bf16[64,2560]{1,0:T(8,128)(2,1)S(1)}, u32[]{:S(2)}, u32[]{:S(2)}) collective-permute-start(bf16[64,2560]{1,0:T(8,128)(2,1)S(1)} %collective-permute-done.29.rest_3_), channel_id=1, source_target_pairs={{0,16},{16,0},{1,17},{17,1},{2,18},{18,2},{3,19},{19,3},{4,20},{20... | collective-permute-start | bytes 983048 | tf_op jit(solution)/shard_map/ppermute | solution.py:18
  131.0 1.7 %copy-start.14 = (bf16[64,2560]{1,0:T(8,128)(2,1)}, bf16[64,2560]{1,0:T(8,128)(2,1)S(1)}, u32[]{:S(2)}) copy-start(bf16[64,2560]{1,0:T(8,128)(2,1)S(1)} %collective-permute-done.27.rest_2_) | copy-start | bytes 983044
  131.0 8.8 %collective-permute-start.28 = (bf16[64,2560]{1,0:T(8,128)(2,1)S(1)}, bf16[64,2560]{1,0:T(8,128)(2,1)S(1)}, u32[]{:S(2)}, u32[]{:S(2)}) collective-permute-start(bf16[64,2560]{1,0:T(8,128)(2,1)S(1)} %collective-permute-done.27.rest_2_), channel_id=1, source_target_pairs={{0,16},{16,0},{1,17},{17,1},{2,18},{18,2},{3,19},{19,3},{4,20},{20... | collective-permute-start | bytes 983048 | tf_op jit(solution)/shard_map/ppermute | solution.py:18
  131.0 1.7 %copy-start.15 = (bf16[64,2560]{1,0:T(8,128)(2,1)}, bf16[64,2560]{1,0:T(8,128)(2,1)S(1)}, u32[]{:S(2)}) copy-start(bf16[64,2560]{1,0:T(8,128)(2,1)S(1)} %collective-permute-done.25.rest_1_) | copy-start | bytes 983044
  131.0 8.8 %collective-permute-start.26 = (bf16[64,2560]{1,0:T(8,128)(2,1)S(1)}, bf16[64,2560]{1,0:T(8,128)(2,1)S(1)}, u32[]{:S(2)}, u32[]{:S(2)}) collective-permute-start(bf16[64,2560]{1,0:T(8,128)(2,1)S(1)} %collective-permute-done.25.rest_1_), channel_id=1, source_target_pairs={{0,16},{16,0},{1,17},{17,1},{2,18},{18,2},{3,19},{19,3},{4,20},{20... | collective-permute-start | bytes 983048 | tf_op jit(solution)/shard_map/ppermute | solution.py:18
  139.7 0.7 copy-start.9
  139.7 0.8 copy-start.10
  139.7 0.9 copy-start.11
  139.8 1.0 copy-start.12

commit v2 on v0

v2 whole, which is shorter than its diff:
```python
import functools
import math

import jax
import jax.numpy as jnp
from jax import lax
from jax.experimental import pallas as pl
from jax.experimental.pallas import tpu as pltpu
from jax.sharding import PartitionSpec as P


BF = jnp.bfloat16
F32 = jnp.float32
ANY = pl.BlockSpec(memory_space=pl.ANY)
HBM = pl.BlockSpec(memory_space=pltpu.HBM)
VM = pl.BlockSpec(memory_space=pltpu.VMEM)
SM = pl.BlockSpec(memory_space=pltpu.SMEM)
MIB = 1024 * 1024
CHUNKS = 2


def swap(x, axis, n, r):
    return lax.ppermute(x, axis, [(i, i ^ r) for i in range(n)])


def tile_of(n, most):
    t = min(n, most)
    while n % t:
        t //= 2
    return t


def call(kernel, out_shape, in_specs, args, flops=0, moved=0, scratch=(), limit=4, out_specs=None):
    return pl.pallas_call(
        kernel,
        out_shape=out_shape,
        in_specs=in_specs,
        out_specs=jax.tree.map(lambda _: VM, out_shape) if out_specs is None else out_specs,
        scratch_shapes=list(scratch),
        compiler_params=pltpu.CompilerParams(vmem_limit_bytes=limit * MIB),
        cost_estimate=pl.CostEstimate(
            flops=int(flops), bytes_accessed=int(moved), transcendentals=0
        ),
    )(*args)


def shape(dims, dtype=BF):
    return jax.ShapeDtypeStruct(tuple(dims), dtype)


def dot(a, b):
    return jnp.dot(a, b, preferred_element_type=F32)


def whole(ref):
    return ref[...].astype(F32)


def pack_kernel(ne, sc, tokens, ids, gates, out):
    width = tokens.shape[1]
    out[:, :width] = tokens[...]
    g = gates[...]
    share = g / jnp.sum(g, axis=1, keepdims=True)
    lanes = lax.broadcasted_iota(jnp.int32, (tokens.shape[0], 128), 1)
    w = jnp.zeros(lanes.shape, F32)
    for k in range(ids.shape[1]):
        w = w + jnp.where(ids[:, k : k + 1] == lanes % ne, share[:, k : k + 1], 0.0)
    high = w.astype(BF).astype(F32)
    middle = (w - high).astype(BF).astype(F32)
    low = w - high - middle
    terms = jnp.where(lanes < ne, high, jnp.where(lanes < 2 * ne, middle, low))
    out[:, width:] = jnp.where(lanes < 3 * ne, terms, 0.0).astype(BF)


def pack(sc, tokens, ids, gates, ne):
    rows, width = tokens.shape
    return call(
        functools.partial(pack_kernel, ne),
        shape((rows, width + 128)),
        [SM] + [VM] * 3,
        (sc, tokens, ids, gates),
        moved=4 * rows * width,
    )


def stack_kernel(*refs):
    out, n = refs[-1], refs[0].shape[0]
    for i, r in enumerate(refs[:-1]):
        out[i * n : (i + 1) * n] = r[...]


def stack(xs):
    n, width = xs[0].shape
    return call(
        stack_kernel, shape((n * len(xs), width)), [VM] * len(xs), xs, moved=4 * len(xs) * n * width
    )


def up_kernel(nd, ne, nz, rows, width, sc, tg, tu, sg, su, *rest):
    count = nd * ne
    own, line = rest[:count], rest[count : 2 * count]
    at_ref, act_ref, f1_ref, f2_ref, xs_out = rest[2 * count : 2 * count + 5]
    xs, w_ref, tbuf, sbuf, sem, tsem, ssem, wsem, xsem = rest[2 * count + 5 :]
    bt, bs = tbuf.shape[3], sbuf.shape[4]
    nt, ns = tg.shape[2] // bt, sg.shape[1] // bs

    def teacher(i, slot):
        cols = pl.ds(pl.multiple_of(i * bt, bt), bt)
        return [
            pltpu.make_async_copy(w.at[0, :, cols], tbuf.at[slot, k], tsem.at[slot, k])
            for k, w in enumerate((tg, tu))
        ]

    def student(i):
        cols = pl.ds(pl.multiple_of(i * bs, bs), bs)
        return [
            pltpu.make_async_copy(w.at[:, cols], sbuf.at[i, k, 0], ssem.at[i, k])
            for k, w in enumerate((sg, su))
        ]

    def row_of(n):
        return pl.multiple_of((n % ne * nd + (sc[0] ^ (n // ne))) * rows, rows)

    copies = []
    for n in range(count):
        for j in range(nz):
            col = pl.multiple_of((sc[2] ^ j) * width, 128)
            src = line[n].at[pl.ds((j - 1) * rows, rows), :] if j else own[n].at[:, pl.ds(0, width)]
            dst = xs.at[pl.ds(row_of(n), rows), pl.ds(col, width)]
            copies.append(pltpu.make_async_copy(src, dst, sem.at[n * nz + j]))
    tails = [
        pltpu.make_async_copy(own[n].at[:, pl.ds(width, 128)], w_ref.at[n], wsem.at[n])
        for n in range(count)
    ]
    for c in teacher(0, 0) + tails + copies:
        c.start()
    for i in range(ns):
        for c in student(i):
            c.start()
    for c in tails + copies:
        c.wait()
    keep = pltpu.make_async_copy(xs, xs_out, xsem)
    keep.start()

    weights = []
    for b in range(ne):
        pair = []
        for a in range(nd):
            m = w_ref[a * ne + b].astype(F32)
            lanes = lax.broadcasted_iota(jnp.int32, m.shape, 1)
            ours = (lanes % ne == sc[1]) & (lanes < 3 * ne)
            pair.append(jnp.sum(jnp.where(ours, m, 0.0), axis=1, keepdims=True))
        for d in range(nd):
            value = pair[0]
            for a in range(1, nd):
                value = jnp.where((sc[0] ^ a) == d, pair[a], value)
            weights.append(value)
    w = jnp.concatenate(weights, axis=0)

    @pl.loop(0, nt)
    def _(i):
        slot = lax.rem(i, 2)

        @pl.when(i + 1 < nt)
        def _():
            for c in teacher(i + 1, 1 - slot):
                c.start()

        for c in teacher(i, slot):
            c.wait()
        at = pl.ds(pl.multiple_of(i * bt, bt), bt)
        g = dot(xs[...], tbuf[slot, 0])
        u = dot(xs[...], tbuf[slot, 1])
        a = g * jax.nn.sigmoid(g) * u
        at_ref[:, at] = jnp.where(w != 0.0, -w * a, 0.0).astype(BF)

    @pl.loop(0, ns)
    def _(i):
        for c in student(i):
            c.wait()
        at = pl.ds(pl.multiple_of(i * bs, bs), bs)
        g = dot(xs[...], sbuf[i, 0, 0])
        u = dot(xs[...], sbuf[i, 1, 0])
        s = jax.nn.sigmoid(g)
        f2 = g * s
        act_ref[:, at] = (f2 * u).astype(BF)
        f1_ref[:, at] = u * s * (1.0 + g * (1.0 - s))
        f2_ref[:, at] = f2

    keep.wait()


def up(sc, tg, tu, sg, su, own, line, dims):
    nd, ne, nz, rows, width = dims
    total, model = rows * nd * ne, width * nz
    ht, hs = tg.shape[2], sg.shape[1]
    bt, bs = tile_of(ht, 256), tile_of(hs, 256)
    count = nd * ne
    return call(
        functools.partial(up_kernel, nd, ne, nz, rows, width),
        [
            shape((total, ht)),
            shape((total, hs)),
            shape((total, hs), F32),
            shape((total, hs), F32),
            shape((total, model)),
        ],
        [SM] + [ANY] * (4 + 2 * count),
        (sc, tg, tu, sg, su, *own, *line),
        flops=4 * total * model * (ht + hs),
        moved=4 * model * (ht + hs),
        scratch=[
            pltpu.VMEM((total, model), BF),
            pltpu.VMEM((count, rows, 128), BF),
            pltpu.VMEM((2, 2, model, bt), BF),
            pltpu.VMEM((hs // bs, 2, 1, model, bs), BF),
            pltpu.SemaphoreType.DMA((count * nz,)),
            pltpu.SemaphoreType.DMA((2, 2)),
            pltpu.SemaphoreType.DMA((hs // bs, 2)),
            pltpu.SemaphoreType.DMA((count,)),
            pltpu.SemaphoreType.DMA,
        ],
        out_specs=[VM, VM, VM, VM, HBM],
        limit=28,
    )


def down_kernel(kept, chunk, chunks, nd, ne, *refs):
    if kept:
        sc, at, act, td, sd, got = refs[:6]
        outs, scratch = refs[6 : 6 + ne], refs[6 + ne :]
    else:
        sc, at, td = refs[:3]
        outs, scratch = refs[3:4], refs[4:]
    model = td.shape[2]
    width = model // nd // chunks
    bn = tile_of(width, 640)
    base = (sc[0] if kept else 1 - sc[0]) * (model // nd) + chunk * width
    tbuf, tsem = scratch[:2]
    n = width // bn

    def fetch(i):
        cols = pl.ds(pl.multiple_of(base + i * bn, 128), bn)
        copies = [pltpu.make_async_copy(td.at[0, :, cols], tbuf.at[i], tsem.at[i])]
        if kept:
            sbuf, ssem = scratch[2:]
            copies.append(pltpu.make_async_copy(sd.at[:, cols], sbuf.at[i], ssem.at[i]))
        return copies

    for i in range(n):
        for c in fetch(i):
            c.start()
    for i in range(n):
        for c in fetch(i):
            c.wait()
        p = dot(at[...], tbuf[i])
        here = slice(i * bn, (i + 1) * bn)
        if kept:
            p = p + dot(act[...], scratch[2][i]) + got[:, here].astype(F32)
            rb = p.shape[0] // ne
            for b in range(ne):
                outs[b][:, here] = p[b * rb : (b + 1) * rb].astype(BF)
        else:
            outs[0][:, here] = p.astype(BF)


def down(sc, at, act, td, sd, got, chunk, nd, ne):
    kept = got is not None
    total, ht = at.shape
    hs, model = sd.shape
    width = model // nd // CHUNKS
    bn = tile_of(width, 640)
    n = width // bn
    scratch = [pltpu.VMEM((n, ht, bn), BF), pltpu.SemaphoreType.DMA((n,))]
    if kept:
        scratch += [pltpu.VMEM((n, hs, bn), BF), pltpu.SemaphoreType.DMA((n,))]
        args, specs = (sc, at, act, td, sd, got), [SM, VM, VM, ANY, ANY, VM]
        out = [shape((total // ne, width))] * ne
    else:
        args, specs = (sc, at, td), [SM, VM, ANY]
        out = [shape((total, width))]
    return call(
        functools.partial(down_kernel, kept, chunk, CHUNKS, nd, ne),
        out,
        specs,
        args,
        flops=2 * total * width * (ht + (hs if kept else 0)),
        moved=2 * width * (ht + (hs if kept else 0)),
        scratch=scratch,
        limit=10,
    )


def sum_kernel(nz, count, sc, *refs):
    parts, outs = refs[:count], refs[count:]
    rp = outs[0].shape[0]
    for j in range(nz):
        rows = pl.ds(pl.multiple_of((sc[2] ^ j) * rp, rp), rp)
        outs[j][...] = sum(p[rows, :].astype(F32) for p in parts).astype(BF)


def sum_parts(sc, parts, nz):
    rb, width = parts[0].shape
    return call(
        functools.partial(sum_kernel, nz, len(parts)),
        [shape((rb // nz, width))] * nz,
        [SM] + [VM] * len(parts),
        (sc, *parts),
        moved=4 * len(parts) * rb * width,
    )


def final_kernel(chunks, scale, *refs):
    parts, out = refs[:-1], refs[-1]
    count = len(parts) // chunks
    width = parts[0].shape[1]
    for c in range(chunks):
        total = sum(whole(p) for p in parts[c * count : (c + 1) * count])
        out[:, c * width : (c + 1) * width] = (total * scale).astype(BF)


def final(parts, scale):
    rp, width = parts[0][0].shape
    flat = [p for line in parts for p in line]
    return call(
        functools.partial(final_kernel, len(parts), scale),
        shape((rp, width * len(parts))),
        [VM] * len(flat),
        flat,
        moved=4 * len(flat) * rp * width,
    )


def back_kernel(nd, ne, nz, model_tokens, grad_scale, sc, act, sd, f1, f2, *rest):
    count = nd * ne
    own, line = rest[:count], rest[count : 2 * count]
    gd, dgp, dup, loss, d_ref, act_t, sq, gbuf, sem, gsem = rest[2 * count :]
    rp, half = own[0].shape
    total, hs = act.shape
    model = half * nd
    rb = total // ne

    copies = []
    for n in range(count):
        for j in range(nz):
            row = pl.multiple_of(n % ne * rb + (sc[2] ^ j) * rp, rp)
            col = pl.multiple_of((sc[0] ^ (n // ne)) * half, 128)
            src = line[n].at[pl.ds((j - 1) * rp, rp), :] if j else own[n]
            dst = d_ref.at[pl.ds(row, rp), pl.ds(col, half)]
            copies.append(pltpu.make_async_copy(src, dst, sem.at[n * nz + j]))
    for c in copies:
        c.start()
    act_t[...] = act[...].T
    for c in copies:
        c.wait()
    bn = tile_of(model, 1280)
    n = model // bn
    dact = jnp.zeros((total, hs), F32)
    for i in range(n):
        cols = slice(i * bn, (i + 1) * bn)
        dact = dact + lax.dot_general(
            d_ref[:, cols], sd[:, cols], (((1,), (1,)), ((), ())), preferred_element_type=F32
        )
    dgp[...] = (dact * f1[...]).astype(BF)
    dup[...] = (dact * f2[...]).astype(BF)
    s = jnp.zeros((total, 128), F32)
    out = [
        pltpu.make_async_copy(gbuf.at[i], gd.at[:, i * bn : (i + 1) * bn], gsem.at[i])
        for i in range(n)
    ]
    for i in range(n):
        d = d_ref[:, i * bn : (i + 1) * bn]
        gbuf[i] = dot(act_t[...], d).astype(BF)
        out[i].start()
        f = d.astype(F32)
        for k in range(bn // 128):
            part = f[:, k * 128 : (k + 1) * 128]
            s = s + part * part
    sq[...] = s
    tot = jnp.zeros((rb, 128), F32)
    for e in range(ne):
        tot = tot + sq[pl.ds(pl.multiple_of((sc[1] ^ e) * rb, rb), rb), :]
    value = jnp.sum(jnp.sum(tot, axis=0, keepdims=True), axis=1, keepdims=True)
    loss[...] = value * (1.0 / (grad_scale * grad_scale)) / model_tokens
    for c in out:
        c.wait()


def back(sc, act, sd, f1, f2, own, line, dims, model_tokens, grad_scale):
    nd, ne, nz = dims
    total, hs = act.shape
    model = sd.shape[1]
    bn = tile_of(model, 1280)
    n = model // bn
    return call(
        functools.partial(back_kernel, nd, ne, nz, model_tokens, grad_scale),
        [shape((hs, model)), shape((total, hs)), shape((total, hs)), shape((1, 1), F32)],
        [SM] + [VM] * 4 + [ANY] * (2 * nd * ne),
        (sc, act, sd, f1, f2, *own, *line),
        flops=4 * total * model * hs,
        moved=2 * model * hs,
        scratch=[
            pltpu.VMEM((total, model), BF),
            pltpu.VMEM((hs, total), BF),
            pltpu.VMEM((total, 128), F32),
            pltpu.VMEM((n, hs, bn), BF),
            pltpu.SemaphoreType.DMA((nd * ne * nz,)),
            pltpu.SemaphoreType.DMA((n,)),
        ],
        out_specs=[HBM, VM, VM, VM],
        limit=20,
    )


def grad_kernel(xs, dgp, dup, gg, gu, buf, sem):
    model = xs.shape[1]
    bn = tile_of(model, 1280)
    dims = (((0,), (0,)), ((), ()))
    out = []
    for i in range(model // bn):
        rows = slice(i * bn, (i + 1) * bn)
        for k, (d, g) in enumerate(((dgp, gg), (dup, gu))):
            n = 2 * i + k
            buf[n] = lax.dot_general(
                xs[:, rows], d[...], dims, preferred_element_type=F32
            ).astype(BF)
            out.append(pltpu.make_async_copy(buf.at[n], g.at[rows, :], sem.at[n]))
            out[-1].start()
    for c in out:
        c.wait()


def grad(xs, dgp, dup):
    total, model = xs.shape
    hs = dgp.shape[1]
    bn = tile_of(model, 1280)
    n = 2 * (model // bn)
    return call(
        grad_kernel,
        [shape((model, hs))] * 2,
        [VM] * 3,
        (xs, dgp, dup),
        flops=4 * total * model * hs,
        moved=4 * model * hs,
        scratch=[pltpu.VMEM((n, bn, hs), BF), pltpu.SemaphoreType.DMA((n,))],
        out_specs=[HBM] * 2,
        limit=24,
    )


def body(tokens, expert_ids, gate_weights, t_gate, t_up, t_down, s_gate, s_up, s_down):
    nd, ne, nz = lax.axis_size("dp"), lax.axis_size("expert"), lax.axis_size("tensor")
    rows, width = tokens.shape
    model = width * nz
    total = rows * ne * nd
    sc = jnp.stack(
        [lax.axis_index("dp"), lax.axis_index("expert"), lax.axis_index("tensor")]
    ).astype(jnp.int32)

    def spread(x, packed):
        line = [swap(x, "tensor", nz, j) for j in range(1, nz)]
        own = [packed] + [swap(packed, "expert", ne, b) for b in range(1, ne)]
        line = stack(line)
        lines = [line] + [swap(line, "expert", ne, b) for b in range(1, ne)]
        far = lambda xs: xs + [swap(z, "dp", nd, 1) for z in xs]
        return far(own), far(lines)

    own, lines = spread(tokens, pack(sc, tokens, expert_ids, gate_weights, ne))
    at, act, f1, f2, xs = up(
        sc, t_gate, t_up, s_gate, s_up, own, lines, (nd, ne, nz, rows, width)
    )

    sent = [down(sc, at, act, t_down, s_down, None, c, nd, ne)[0] for c in range(CHUNKS)]
    got = [swap(s, "dp", nd, 1) for s in sent]
    last = []
    for c in range(CHUNKS):
        kept = down(sc, at, act, t_down, s_down, got[c], c, nd, ne)
        parts = [kept[0]] + [swap(kept[b], "expert", ne, b) for b in range(1, ne)]
        own = sum_parts(sc, parts, nz)
        last.append([own[0]] + [swap(own[j], "tensor", nz, j) for j in range(1, nz)])
    grad_scale = 1.0 / math.sqrt(total)
    d_out = final(last, grad_scale)

    own, lines = spread(d_out, d_out)
    gd, dgp, dup, loss = back(
        sc, act, s_down, f1, f2, own, lines, (nd, ne, nz), total * model, grad_scale
    )
    gg, gu = grad(xs, dgp, dup)
    return gg, gu, gd, loss[0, 0]


def solution(mesh):
    return jax.shard_map(
        body,
        mesh=mesh,
        in_specs=(
            P(("dp", "expert"), "tensor"),
            P(("dp", "expert"), None),
            P(("dp", "expert"), None),
            P("expert", None, ("dp", "tensor")),
            P("expert", None, ("dp", "tensor")),
            P("expert", ("dp", "tensor"), None),
            P(None, ("expert", "tensor")),
            P(None, ("expert", "tensor")),
            P(("expert", "tensor"), None),
        ),
        out_specs=(
            P(None, ("expert", "tensor")),
            P(None, ("expert", "tensor")),
            P(("expert", "tensor"), None),
            P(),
        ),
        check_vma=False,
    )
```

time: 363 us -> 136 us (0.37)
  waiting for transfers between devices: 167 us -> 41.6 us
  blocking collectives: 77.7 us -> 0 us
  matrix products: 51.2 us -> 0 us
  starting transfers between devices: 4.08 us -> 46.8 us
  Pallas kernels: 0 us -> 38.8 us
  local copies, waits for them, and re-layouts: 44.4 us -> 7.4 us
  between operations: 16.1 us -> 1.05 us
    reduce_scatter x3 -> x0, waiting for transfers between devices: 93.4 us -> none  [the longest x1 60.2 us: body(): lax.psum_scatter(teacher_part.astype(jnp.bfloat16), ('dp', 'tensor'), sca...]
    all_gather x3 -> x0, waiting for transfers between devices: 57.3 us -> none  [the longest x1 57.3 us: body(): gathered = lax.all_gather(d_out, ('expert', 'tensor'), axis=0, tiled=True)]
    dot_general x12 -> x0, matrix products: 51.2 us -> none  [the longest x1 7.67 us: body(): jnp.dot(shard_rows, t_gate[0], preferred_element_type=jnp.float32)]
    ppermute x0 -> x48, starting transfers between devices: none -> 46.8 us  [swap(): return lax.ppermute(x, axis, [(i, i ^ r) for i in range(n)])]
    ppermute x0 -> x48, waiting for transfers between devices: none -> 41.6 us  [swap(): return lax.ppermute(x, axis, [(i, i ^ r) for i in range(n)])]
    pallas_call x0 -> x13, Pallas kernels: none -> 38.8 us  [call(): pl.pallas_call(kernel, out_shape=out_shape, in_specs=in_specs, out_specs=...]
    psum x1 -> x0, blocking collectives: 38.4 us -> none  [body(): lax.psum(jnp.sum(residual * residual), ('dp', 'expert', 'tensor'))]
    all_to_all x1 -> x0, blocking collectives: 21.5 us -> none  [body(): lax.all_to_all(sent, 'expert', split_axis=0, concat_axis=0, tiled=True)]
  transfers between devices with their start and end apart: 8 -> 48, of which waited for: 5 -> 20; matrix products, arithmetic and copies ran while one was open for 15% -> 1% of each run, Pallas kernels for 0% -> 7%
where the time goes in v2:
time: 136 us
  starting transfers between devices  46.8 us (34%)
  waiting for transfers between devices  41.6 us (31%)
  Pallas kernels  38.8 us (29%)
  local copies, waits for them, and re-layouts  7.4 us (5%)
    ppermute x48, starting transfers between devices, swap(): return lax.ppermute(x, axis, [(i, i ^ r) for i in range(n)])  46.8 us
    ppermute x48, waiting for transfers between devices, swap(): return lax.ppermute(x, axis, [(i, i ^ r) for i in range(n)])  41.6 us
    pallas_call x13, Pallas kernels, call(): pl.pallas_call(kernel, out_shape=out_shape, in_specs=in_specs, out_specs=...  38.8 us
    unnamed x18, local copies, waits for them, and re-layouts  7.4 us
  transfers between devices with their start and end apart: 48, of which 20 were waited for; matrix products, arithmetic and copies ran while one was open for 1% of the time, Pallas kernels for 7%

profile of v2, /device:TPU:0, one launch (start us, length us, event | category | flops | bytes accessed | tf_op | source)
XLA Modules:
  0.0 135.8 jit_solution(1657235115934174356)
XLA Ops:
  0.6 3.1 %collective-permute-start.7 = (bf16[32,1280]{1,0:T(8,128)(2,1)}, bf16[32,1280]{1,0:T(8,128)(2,1)S(1)}, u32[]{:S(2)}, u32[]{:S(2)}) collective-permute-start(bf16[32,1280]{1,0:T(8,128)(2,1)} %tokens.1), channel_id=1, source_target_pairs={{0,1},{1,0},{2,3},{3,2},{4,5},{5,4},{6,7},{7,6},{8,9},{9,8},{10,11... | collective-permute-start | bytes 245768 | tf_op jit(solution)/shard_map/ppermute | solution.py:23
  3.7 2.5 %collective-permute-start.9 = (bf16[32,1280]{1,0:T(8,128)(2,1)}, bf16[32,1280]{1,0:T(8,128)(2,1)S(1)}, u32[]{:S(2)}, u32[]{:S(2)}) collective-permute-start(bf16[32,1280]{1,0:T(8,128)(2,1)} %tokens.1), channel_id=1, source_target_pairs={{0,3},{1,2},{2,1},{3,0},{4,7},{5,6},{6,5},{7,4},{8,11},{9,10},{10,... | collective-permute-start | bytes 245768 | tf_op jit(solution)/shard_map/ppermute | solution.py:23
  6.4 5.1 %collective-permute-done.9.refs_2_ = bf16[32,1280]{1,0:T(8,128)(2,1)S(1)} collective-permute-done((bf16[32,1280]{1,0:T(8,128)(2,1)}, bf16[32,1280]{1,0:T(8,128)(2,1)S(1)}, u32[]{:S(2)}, u32[]{:S(2)}) %collective-permute-start.9) | collective-permute-done | bytes 81952 | tf_op jit(solution)/shard_map/ppermute | solution.py:23
  11.5 2.6 %collective-permute-done.8.refs_1_ = bf16[32,1280]{1,0:T(8,128)(2,1)S(1)} collective-permute-done((bf16[32,1280]{1,0:T(8,128)(2,1)}, bf16[32,1280]{1,0:T(8,128)(2,1)S(1)}, u32[]{:S(2)}, u32[]{:S(2)}) %collective-permute-start.8) | collective-permute-done | bytes 81952 | tf_op jit(solution)/shard_map/ppermute | solution.py:23
  14.1 2.5 %collective-permute-start.12 = (bf16[96,1280]{1,0:T(8,128)(2,1)S(1)}, bf16[96,1280]{1,0:T(8,128)(2,1)S(1)}, u32[]{:S(2)}, u32[]{:S(2)}) collective-permute-start(bf16[96,1280]{1,0:T(8,128)(2,1)S(1)} %shard_map.121.rest_8_), channel_id=1, source_target_pairs={{0,12},{4,8},{8,4},{12,0},{1,13},{5,9},{9,5},{13,1},{2,14},{6,10},... | collective-permute-start | bytes 737288 | tf_op jit(solution)/shard_map/ppermute | solution.py:23
  16.7 0.5 collective-permute-start.11
  17.2 0.5 collective-permute-start.10
  17.8 0.8 copy.13.ids
  18.5 0.8 copy.14.gates
  19.3 0.9 copy-done.2
  20.2 0.7 shard_map.120.rest_0_
  21.0 2.5 %collective-permute-start.2 = (bf16[32,1408]{1,0:T(8,128)(2,1)S(1)}, bf16[32,1408]{1,0:T(8,128)(2,1)S(1)}, u32[]{:S(2)}, u32[]{:S(2)}) collective-permute-start(bf16[32,1408]{1,0:T(8,128)(2,1)S(1)} %shard_map.120.rest_0_), channel_id=1, source_target_pairs={{0,12},{4,8},{8,4},{12,0},{1,13},{5,9},{9,5},{13,1},{2,14},{6,10},... | collective-permute-start | bytes 270344 | tf_op jit(solution)/shard_map/ppermute | solution.py:23
  23.5 0.5 collective-permute-start.1
  24.0 6.0 %collective-permute-done.2.rest_3_ = bf16[32,1408]{1,0:T(8,128)(2,1)S(1)} collective-permute-done((bf16[32,1408]{1,0:T(8,128)(2,1)S(1)}, bf16[32,1408]{1,0:T(8,128)(2,1)S(1)}, u32[]{:S(2)}, u32[]{:S(2)}) %collective-permute-start.2) | collective-permute-done | bytes 90144 | tf_op jit(solution)/shard_map/ppermute | solution.py:23
  30.1 1.5 %collective-permute-start = (bf16[32,1408]{1,0:T(8,128)(2,1)S(1)}, bf16[32,1408]{1,0:T(8,128)(2,1)S(1)}, u32[]{:S(2)}, u32[]{:S(2)}) collective-permute-start(bf16[32,1408]{1,0:T(8,128)(2,1)S(1)} %shard_map.120.rest_0_), channel_id=1, source_target_pairs={{0,4},{4,0},{8,12},{12,8},{1,5},{5,1},{9,13},{13,9},{2,6},{6,2},{1... | collective-permute-start | bytes 270344 | tf_op jit(solution)/shard_map/ppermute | solution.py:23
  31.6 0.3 collective-permute-done.1.rest_2_
  31.9 2.7 %collective-permute-done.rest_1_ = bf16[32,1408]{1,0:T(8,128)(2,1)S(1)} collective-permute-done((bf16[32,1408]{1,0:T(8,128)(2,1)S(1)}, bf16[32,1408]{1,0:T(8,128)(2,1)S(1)}, u32[]{:S(2)}, u32[]{:S(2)}) %collective-permute-start) | collective-permute-done | bytes 90144 | tf_op jit(solution)/shard_map/ppermute | solution.py:23
  34.6 0.5 collective-permute-start.16
  35.2 0.4 collective-permute-start.14
  35.7 1.6 %collective-permute-done.5.rest_6_ = bf16[32,1408]{1,0:T(8,128)(2,1)S(1)} collective-permute-done((bf16[32,1408]{1,0:T(8,128)(2,1)S(1)}, bf16[32,1408]{1,0:T(8,128)(2,1)S(1)}, u32[]{:S(2)}, u32[]{:S(2)}) %collective-permute-start.5) | collective-permute-done | bytes 90144 | tf_op jit(solution)/shard_map/ppermute | solution.py:23
  37.5 1.1 collective-permute-done.4.rest_5_
  38.6 2.5 %copy-done = bf16[5120,512]{1,0:T(8,128)(2,1)S(1)} copy-done((bf16[5120,512]{1,0:T(8,128)(2,1)S(1)}, bf16[5120,512]{1,0:T(8,128)(2,1)}, u32[]{:S(2)}) %copy-start) | copy-done | bytes 5242904
  41.1 2.5 %copy-done.1 = bf16[5120,512]{1,0:T(8,128)(2,1)S(1)} copy-done((bf16[5120,512]{1,0:T(8,128)(2,1)S(1)}, bf16[5120,512]{1,0:T(8,128)(2,1)}, u32[]{:S(2)}) %copy-start.1) | copy-done | bytes 5242904
  43.6 14.5 %shard_map.122 = (bf16[256,1024]{1,0:T(8,128)(2,1)S(1)}, bf16[256,512]{1,0:T(8,128)(2,1)S(1)}, f32[256,512]{1,0:T(8,128)S(1)}, f32[256,512]{1,0:T(8,128)S(1)}, bf16[256,5120]{1,0:T(8,128)(2,1)S(1)}) custom-call(s32[3]{0:T(128)S(1)} %pad_add_fusion.sc.refs_0_, bf16[1,5120,1024]{2,1,0:T(8,128)(2,1)} %tg.1, bf16[1,5120,1024]{2,1,0:T(8,128)(2,1)} %tu.1, ...), custom_call_target="tpu_custom_call" | custom-call | flops 8053063680 | bytes 31457280 | tf_op jit(solution)/shard_map/pallas_call | solution.py:34
  58.2 2.1 %shard_map.123 = bf16[256,1280]{1,0:T(8,128)(2,1)S(1)} custom-call(s32[3]{0:T(128)S(1)} %pad_add_fusion.sc.refs_0_, bf16[256,1024]{1,0:T(8,128)(2,1)S(1)} %get-tuple-element.35.refs_1_, bf16[1,1024,5120]{2,1,0:T(8,128)(2,1)S(1)} %bitcast.5), custom_call_target="tpu_custom_call" | custom-call | flops 671088640 | bytes 2621440 | tf_op jit(solution)/shard_map/pallas_call | solution.py:34
  60.5 2.1 %shard_map.126 = bf16[256,1280]{1,0:T(8,128)(2,1)S(1)} custom-call(s32[3]{0:T(128)S(1)} %pad_add_fusion.sc.refs_0_, bf16[256,1024]{1,0:T(8,128)(2,1)S(1)} %get-tuple-element.35.refs_1_, bf16[1,1024,5120]{2,1,0:T(8,128)(2,1)S(1)} %bitcast.5), custom_call_target="tpu_custom_call" | custom-call | flops 671088640 | bytes 2621440 | tf_op jit(solution)/shard_map/pallas_call | solution.py:34
  62.6 0.4 collective-permute-start.24
  63.1 2.7 %shard_map.124 = (bf16[64,1280]{1,0:T(8,128)(2,1)S(1)}, bf16[64,1280]{1,0:T(8,128)(2,1)S(1)}, bf16[64,1280]{1,0:T(8,128)(2,1)S(1)}, bf16[64,1280]{1,0:T(8,128)(2,1)S(1)}) custom-call(s32[3]{0:T(128)S(1)} %pad_add_fusion.sc.refs_0_, bf16[256,1024]{1,0:T(8,128)(2,1)S(1)} %get-tuple-element.35.refs_1_, bf16[256,512]{1,0:T(8,128)(2,1)S(1)} %get-tuple-element.32.refs_2_.act, ...), custom_call_target="tpu_custom_call" | custom-call | flops 1006632960 | bytes 3932160 | tf_op jit(solution)/shard_map/pallas_call | solution.py:34
  65.8 1.6 %collective-permute-start.18 = (bf16[64,1280]{1,0:T(8,128)(2,1)S(1)}, bf16[64,1280]{1,0:T(8,128)(2,1)S(1)}, u32[]{:S(2)}, u32[]{:S(2)}) collective-permute-start(bf16[64,1280]{1,0:T(8,128)(2,1)S(1)} %get-tuple-element.37), channel_id=1, source_target_pairs={{0,4},{4,0},{8,12},{12,8},{1,5},{5,1},{9,13},{13,9},{2,6},{6,2},{1... | collective-permute-start | bytes 491528 | tf_op jit(solution)/shard_map/ppermute | solution.py:23
  67.4 1.5 %collective-permute-start.19 = (bf16[64,1280]{1,0:T(8,128)(2,1)S(1)}, bf16[64,1280]{1,0:T(8,128)(2,1)S(1)}, u32[]{:S(2)}, u32[]{:S(2)}) collective-permute-start(bf16[64,1280]{1,0:T(8,128)(2,1)S(1)} %get-tuple-element.38), channel_id=1, source_target_pairs={{0,8},{4,12},{8,0},{12,4},{1,9},{5,13},{9,1},{13,5},{2,10},{6,14},... | collective-permute-start | bytes 491528 | tf_op jit(solution)/shard_map/ppermute | solution.py:23
  68.9 0.5 collective-permute-start.20
  69.3 2.7 %shard_map.127 = (bf16[64,1280]{1,0:T(8,128)(2,1)S(1)}, bf16[64,1280]{1,0:T(8,128)(2,1)S(1)}, bf16[64,1280]{1,0:T(8,128)(2,1)S(1)}, bf16[64,1280]{1,0:T(8,128)(2,1)S(1)}) custom-call(s32[3]{0:T(128)S(1)} %pad_add_fusion.sc.refs_0_, bf16[256,1024]{1,0:T(8,128)(2,1)S(1)} %get-tuple-element.35.refs_1_, bf16[256,512]{1,0:T(8,128)(2,1)S(1)} %get-tuple-element.32.refs_2_.act, ...), custom_call_target="tpu_custom_call" | custom-call | flops 1006632960 | bytes 3932160 | tf_op jit(solution)/shard_map/pallas_call | solution.py:34
  72.1 1.6 %collective-permute-start.25 = (bf16[64,1280]{1,0:T(8,128)(2,1)S(1)}, bf16[64,1280]{1,0:T(8,128)(2,1)S(1)}, u32[]{:S(2)}, u32[]{:S(2)}) collective-permute-start(bf16[64,1280]{1,0:T(8,128)(2,1)S(1)} %get-tuple-element.45), channel_id=1, source_target_pairs={{0,4},{4,0},{8,12},{12,8},{1,5},{5,1},{9,13},{13,9},{2,6},{6,2},{1... | collective-permute-start | bytes 491528 | tf_op jit(solution)/shard_map/ppermute | solution.py:23
  73.6 1.5 %collective-permute-start.26 = (bf16[64,1280]{1,0:T(8,128)(2,1)S(1)}, bf16[64,1280]{1,0:T(8,128)(2,1)S(1)}, u32[]{:S(2)}, u32[]{:S(2)}) collective-permute-start(bf16[64,1280]{1,0:T(8,128)(2,1)S(1)} %get-tuple-element.46), channel_id=1, source_target_pairs={{0,8},{4,12},{8,0},{12,4},{1,9},{5,13},{9,1},{13,5},{2,10},{6,14},... | collective-permute-start | bytes 491528 | tf_op jit(solution)/shard_map/ppermute | solution.py:23
  75.2 0.5 collective-permute-start.27
  75.6 1.3 collective-permute-done.19.refs_2_
  76.9 0.5 collective-permute-done.20.refs_3_
  77.4 0.6 shard_map.125
  78.1 2.2 %collective-permute-start.22 = (bf16[16,1280]{1,0:T(8,128)(2,1)S(1)}, bf16[16,1280]{1,0:T(8,128)(2,1)S(1)}, u32[]{:S(2)}, u32[]{:S(2)}) collective-permute-start(bf16[16,1280]{1,0:T(8,128)(2,1)S(1)} %get-tuple-element.42), channel_id=1, source_target_pairs={{0,2},{1,3},{2,0},{3,1},{4,6},{5,7},{6,4},{7,5},{8,10},{9,11},{10,... | collective-permute-start | bytes 122888 | tf_op jit(solution)/shard_map/ppermute | solution.py:23
  80.4 2.2 %collective-permute-start.23 = (bf16[16,1280]{1,0:T(8,128)(2,1)S(1)}, bf16[16,1280]{1,0:T(8,128)(2,1)S(1)}, u32[]{:S(2)}, u32[]{:S(2)}) collective-permute-start(bf16[16,1280]{1,0:T(8,128)(2,1)S(1)} %get-tuple-element.43), channel_id=1, source_target_pairs={{0,3},{1,2},{2,1},{3,0},{4,7},{5,6},{6,5},{7,4},{8,11},{9,10},{10,... | collective-permute-start | bytes 122888 | tf_op jit(solution)/shard_map/ppermute | solution.py:23
  82.5 1.3 collective-permute-done.26.refs_2_
  83.8 0.6 shard_map.128
  84.6 2.2 %collective-permute-start.29 = (bf16[16,1280]{1,0:T(8,128)(2,1)S(1)}, bf16[16,1280]{1,0:T(8,128)(2,1)S(1)}, u32[]{:S(2)}, u32[]{:S(2)}) collective-permute-start(bf16[16,1280]{1,0:T(8,128)(2,1)S(1)} %get-tuple-element.50), channel_id=1, source_target_pairs={{0,2},{1,3},{2,0},{3,1},{4,6},{5,7},{6,4},{7,5},{8,10},{9,11},{10,... | collective-permute-start | bytes 122888 | tf_op jit(solution)/shard_map/ppermute | solution.py:23
  86.8 2.1 %collective-permute-start.30 = (bf16[16,1280]{1,0:T(8,128)(2,1)S(1)}, bf16[16,1280]{1,0:T(8,128)(2,1)S(1)}, u32[]{:S(2)}, u32[]{:S(2)}) collective-permute-start(bf16[16,1280]{1,0:T(8,128)(2,1)S(1)} %get-tuple-element.51), channel_id=1, source_target_pairs={{0,3},{1,2},{2,1},{3,0},{4,7},{5,6},{6,5},{7,4},{8,11},{9,10},{10,... | collective-permute-start | bytes 122888 | tf_op jit(solution)/shard_map/ppermute | solution.py:23
  89.0 0.6 collective-permute-done.29.refs_6_
  89.5 3.2 %collective-permute-done.30.refs_7_ = bf16[16,1280]{1,0:T(8,128)(2,1)S(1)} collective-permute-done((bf16[16,1280]{1,0:T(8,128)(2,1)S(1)}, bf16[16,1280]{1,0:T(8,128)(2,1)S(1)}, u32[]{:S(2)}, u32[]{:S(2)}) %collective-permute-start.30) | collective-permute-done | bytes 40992 | tf_op jit(solution)/shard_map/ppermute | solution.py:23
  92.7 2.1 %collective-permute-start.40 = (bf16[16,2560]{1,0:T(8,128)(2,1)S(1)}, bf16[16,2560]{1,0:T(8,128)(2,1)S(1)}, u32[]{:S(2)}, u32[]{:S(2)}) collective-permute-start(bf16[16,2560]{1,0:T(8,128)(2,1)S(1)} %shard_map.129.rest_0_), channel_id=1, source_target_pairs={{0,3},{1,2},{2,1},{3,0},{4,7},{5,6},{6,5},{7,4},{8,11},{9,10},{10,... | collective-permute-start | bytes 245768 | tf_op jit(solution)/shard_map/ppermute | solution.py:23
  94.9 2.3 %collective-permute-start.38 = (bf16[16,2560]{1,0:T(8,128)(2,1)S(1)}, bf16[16,2560]{1,0:T(8,128)(2,1)S(1)}, u32[]{:S(2)}, u32[]{:S(2)}) collective-permute-start(bf16[16,2560]{1,0:T(8,128)(2,1)S(1)} %shard_map.129.rest_0_), channel_id=1, source_target_pairs={{0,1},{1,0},{2,3},{3,2},{4,5},{5,4},{6,7},{7,6},{8,9},{9,8},{10,11... | collective-permute-start | bytes 245768 | tf_op jit(solution)/shard_map/ppermute | solution.py:23
  97.2 1.9 %collective-permute-done.40.refs_2_ = bf16[16,2560]{1,0:T(8,128)(2,1)S(1)} collective-permute-done((bf16[16,2560]{1,0:T(8,128)(2,1)S(1)}, bf16[16,2560]{1,0:T(8,128)(2,1)S(1)}, u32[]{:S(2)}, u32[]{:S(2)}) %collective-permute-start.40) | collective-permute-done | bytes 81952 | tf_op jit(solution)/shard_map/ppermute | solution.py:23
  99.1 1.7 %collective-permute-done.39.refs_1_ = bf16[16,2560]{1,0:T(8,128)(2,1)S(1)} collective-permute-done((bf16[16,2560]{1,0:T(8,128)(2,1)S(1)}, bf16[16,2560]{1,0:T(8,128)(2,1)S(1)}, u32[]{:S(2)}, u32[]{:S(2)}) %collective-permute-start.39) | collective-permute-done | bytes 81952 | tf_op jit(solution)/shard_map/ppermute | solution.py:23
  100.8 1.5 %collective-permute-start.43 = (bf16[48,2560]{1,0:T(8,128)(2,1)S(1)}, bf16[48,2560]{1,0:T(8,128)(2,1)S(1)}, u32[]{:S(2)}, u32[]{:S(2)}) collective-permute-start(bf16[48,2560]{1,0:T(8,128)(2,1)S(1)} %shard_map.130.rest_8_), channel_id=1, source_target_pairs={{0,12},{4,8},{8,4},{12,0},{1,13},{5,9},{9,5},{13,1},{2,14},{6,10},... | collective-permute-start | bytes 737288 | tf_op jit(solution)/shard_map/ppermute | solution.py:23
  102.3 1.4 %collective-permute-start.42 = (bf16[48,2560]{1,0:T(8,128)(2,1)S(1)}, bf16[48,2560]{1,0:T(8,128)(2,1)S(1)}, u32[]{:S(2)}, u32[]{:S(2)}) collective-permute-start(bf16[48,2560]{1,0:T(8,128)(2,1)S(1)} %shard_map.130.rest_8_), channel_id=1, source_target_pairs={{0,8},{4,12},{8,0},{12,4},{1,9},{5,13},{9,1},{13,5},{2,10},{6,14},... | collective-permute-start | bytes 737288 | tf_op jit(solution)/shard_map/ppermute | solution.py:23
  103.7 0.7 collective-permute-start.41
  104.4 1.4 %collective-permute-start.33 = (bf16[16,2560]{1,0:T(8,128)(2,1)S(1)}, bf16[16,2560]{1,0:T(8,128)(2,1)S(1)}, u32[]{:S(2)}, u32[]{:S(2)}) collective-permute-start(bf16[16,2560]{1,0:T(8,128)(2,1)S(1)} %shard_map.129.rest_0_), channel_id=1, source_target_pairs={{0,12},{4,8},{8,4},{12,0},{1,13},{5,9},{9,5},{13,1},{2,14},{6,10},... | collective-permute-start | bytes 245768 | tf_op jit(solution)/shard_map/ppermute | solution.py:23
  105.8 1.4 %collective-permute-start.32 = (bf16[16,2560]{1,0:T(8,128)(2,1)S(1)}, bf16[16,2560]{1,0:T(8,128)(2,1)S(1)}, u32[]{:S(2)}, u32[]{:S(2)}) collective-permute-start(bf16[16,2560]{1,0:T(8,128)(2,1)S(1)} %shard_map.129.rest_0_), channel_id=1, source_target_pairs={{0,8},{4,12},{8,0},{12,4},{1,9},{5,13},{9,1},{13,5},{2,10},{6,14},... | collective-permute-start | bytes 245768 | tf_op jit(solution)/shard_map/ppermute | solution.py:23
  107.2 6.7 %collective-permute-done.33.rest_3_ = bf16[16,2560]{1,0:T(8,128)(2,1)S(1)} collective-permute-done((bf16[16,2560]{1,0:T(8,128)(2,1)S(1)}, bf16[16,2560]{1,0:T(8,128)(2,1)S(1)}, u32[]{:S(2)}, u32[]{:S(2)}) %collective-permute-start.33) | collective-permute-done | bytes 81952 | tf_op jit(solution)/shard_map/ppermute | solution.py:23
  114.0 2.8 %collective-permute-start.31 = (bf16[16,2560]{1,0:T(8,128)(2,1)S(1)}, bf16[16,2560]{1,0:T(8,128)(2,1)S(1)}, u32[]{:S(2)}, u32[]{:S(2)}) collective-permute-start(bf16[16,2560]{1,0:T(8,128)(2,1)S(1)} %shard_map.129.rest_0_), channel_id=1, source_target_pairs={{0,4},{4,0},{8,12},{12,8},{1,5},{5,1},{9,13},{13,9},{2,6},{6,2},{1... | collective-permute-start | bytes 245768 | tf_op jit(solution)/shard_map/ppermute | solution.py:23
  116.7 2.4 %collective-permute-done.31.rest_1_ = bf16[16,2560]{1,0:T(8,128)(2,1)S(1)} collective-permute-done((bf16[16,2560]{1,0:T(8,128)(2,1)S(1)}, bf16[16,2560]{1,0:T(8,128)(2,1)S(1)}, u32[]{:S(2)}, u32[]{:S(2)}) %collective-permute-start.31) | collective-permute-done | bytes 81952 | tf_op jit(solution)/shard_map/ppermute | solution.py:23
  119.1 0.5 collective-permute-start.47
  119.7 0.4 collective-permute-start.45
  120.6 1.1 collective-permute-done.36.rest_6_
  122.0 1.0 collective-permute-done.35.rest_5_
  123.0 8.0 %shard_map.131 = (bf16[512,5120]{1,0:T(8,128)(2,1)}, bf16[256,512]{1,0:T(8,128)(2,1)S(1)}, bf16[256,512]{1,0:T(8,128)(2,1)S(1)}, f32[1,1]{1,0:T(1,128)}) custom-call(s32[3]{0:T(128)S(1)} %pad_add_fusion.sc.refs_0_, bf16[256,512]{1,0:T(8,128)(2,1)S(1)} %get-tuple-element.32.refs_2_.act, bf16[512,5120]{1,0:T(8,128)(2,1)S(1)} %bitcast.7, ...), custom_call_target="tpu_custom_call" | custom-call | flops 2684354560 | bytes 5242880 | tf_op jit(solution)/shard_map/pallas_call | solution.py:34
  131.0 4.6 %shard_map.132 = (bf16[5120,512]{1,0:T(8,128)(2,1)}, bf16[5120,512]{1,0:T(8,128)(2,1)}) custom-call(bf16[256,5120]{1,0:T(8,128)(2,1)S(1)} %get-tuple-element.31.xs, bf16[256,512]{1,0:T(8,128)(2,1)S(1)} %get-tuple-element.52.dgp, bf16[256,512]{1,0:T(8,128)(2,1)S(1)} %get-tuple-element.53.dup), custom_call_target="tpu_custom_call" | custom-call | flops 2684354560 | bytes 10485760 | tf_op jit(solution)/shard_map/pallas_call | solution.py:34
  (66 shorter events, 2.0 us)
Async XLA Ops:
  0.6 5.8 %collective-permute-start.7 = (bf16[32,1280]{1,0:T(8,128)(2,1)}, bf16[32,1280]{1,0:T(8,128)(2,1)S(1)}, u32[]{:S(2)}, u32[]{:S(2)}) collective-permute-start(bf16[32,1280]{1,0:T(8,128)(2,1)} %tokens.1), channel_id=1, source_target_pairs={{0,1},{1,0},{2,3},{3,2},{4,5},{5,4},{6,7},{7,6},{8,9},{9,8},{10,11... | collective-permute-start | bytes 245768 | tf_op jit(solution)/shard_map/ppermute | solution.py:23
  3.7 7.8 %collective-permute-start.9 = (bf16[32,1280]{1,0:T(8,128)(2,1)}, bf16[32,1280]{1,0:T(8,128)(2,1)S(1)}, u32[]{:S(2)}, u32[]{:S(2)}) collective-permute-start(bf16[32,1280]{1,0:T(8,128)(2,1)} %tokens.1), channel_id=1, source_target_pairs={{0,3},{1,2},{2,1},{3,0},{4,7},{5,6},{6,5},{7,4},{8,11},{9,10},{10,... | collective-permute-start | bytes 245768 | tf_op jit(solution)/shard_map/ppermute | solution.py:23
  6.2 7.9 %collective-permute-start.8 = (bf16[32,1280]{1,0:T(8,128)(2,1)}, bf16[32,1280]{1,0:T(8,128)(2,1)S(1)}, u32[]{:S(2)}, u32[]{:S(2)}) collective-permute-start(bf16[32,1280]{1,0:T(8,128)(2,1)} %tokens.1), channel_id=1, source_target_pairs={{0,2},{1,3},{2,0},{3,1},{4,6},{5,7},{6,4},{7,5},{8,10},{9,11},{10,... | collective-permute-start | bytes 245768 | tf_op jit(solution)/shard_map/ppermute | solution.py:23
  14.1 44.0 %slice-start = ((s8[10485760]{0:T(1024)(128)(4,1)}), s8[2097152]{0:T(1024)(128)(4,1)S(1)}, s32[]{:S(2)}) async-start(s8[10485760]{0:T(1024)(128)(4,1)} %bitcast.4), calls=%async_computation | async-start | bytes 4194304
  14.1 20.5 %collective-permute-start.12 = (bf16[96,1280]{1,0:T(8,128)(2,1)S(1)}, bf16[96,1280]{1,0:T(8,128)(2,1)S(1)}, u32[]{:S(2)}, u32[]{:S(2)}) collective-permute-start(bf16[96,1280]{1,0:T(8,128)(2,1)S(1)} %shard_map.121.rest_8_), channel_id=1, source_target_pairs={{0,12},{4,8},{8,4},{12,0},{1,13},{5,9},{9,5},{13,1},{2,14},{6,10},... | collective-permute-start | bytes 737288 | tf_op jit(solution)/shard_map/ppermute | solution.py:23
  16.7 18.5 %collective-permute-start.11 = (bf16[96,1280]{1,0:T(8,128)(2,1)S(1)}, bf16[96,1280]{1,0:T(8,128)(2,1)S(1)}, u32[]{:S(2)}, u32[]{:S(2)}) collective-permute-start(bf16[96,1280]{1,0:T(8,128)(2,1)S(1)} %shard_map.121.rest_8_), channel_id=1, source_target_pairs={{0,8},{4,12},{8,0},{12,4},{1,9},{5,13},{9,1},{13,5},{2,10},{6,14},... | collective-permute-start | bytes 737288 | tf_op jit(solution)/shard_map/ppermute | solution.py:23
  17.2 18.0 %collective-permute-start.10 = (bf16[96,1280]{1,0:T(8,128)(2,1)S(1)}, bf16[96,1280]{1,0:T(8,128)(2,1)S(1)}, u32[]{:S(2)}, u32[]{:S(2)}) collective-permute-start(bf16[96,1280]{1,0:T(8,128)(2,1)S(1)} %shard_map.121.rest_8_), channel_id=1, source_target_pairs={{0,4},{4,0},{8,12},{12,8},{1,5},{5,1},{9,13},{13,9},{2,6},{6,2},{1... | collective-permute-start | bytes 737288 | tf_op jit(solution)/shard_map/ppermute | solution.py:23
  19.3 0.9 copy-start.2
  20.9 37.2 %slice-start.1 = ((s8[10485760]{0:T(1024)(128)(4,1)}), s8[4194304]{0:T(1024)(128)(4,1)S(1)}, s32[]{:S(2)}) async-start(s8[10485760]{0:T(1024)(128)(4,1)} %bitcast.4), calls=%async_computation.1 | async-start | bytes 8388608
  20.9 37.2 %slice-start.2 = ((s8[10485760]{0:T(1024)(128)(4,1)}), s8[4194304]{0:T(1024)(128)(4,1)S(1)}, s32[]{:S(2)}) async-start(s8[10485760]{0:T(1024)(128)(4,1)} %bitcast.4), calls=%async_computation.2 | async-start | bytes 8388608
  20.9 2.6 %collective-permute-start.3 = (bf16[32,1408]{1,0:T(8,128)(2,1)S(1)}, bf16[32,1408]{1,0:T(8,128)(2,1)S(1)}, u32[]{:S(2)}, u32[]{:S(2)}) collective-permute-start(bf16[32,1408]{1,0:T(8,128)(2,1)S(1)} %shard_map.120.rest_0_), channel_id=1, source_target_pairs={{0,16},{16,0},{1,17},{17,1},{2,18},{18,2},{3,19},{19,3},{4,20},{20... | collective-permute-start | bytes 270344 | tf_op jit(solution)/shard_map/ppermute | solution.py:23
  21.0 9.1 %collective-permute-start.2 = (bf16[32,1408]{1,0:T(8,128)(2,1)S(1)}, bf16[32,1408]{1,0:T(8,128)(2,1)S(1)}, u32[]{:S(2)}, u32[]{:S(2)}) collective-permute-start(bf16[32,1408]{1,0:T(8,128)(2,1)S(1)} %shard_map.120.rest_0_), channel_id=1, source_target_pairs={{0,12},{4,8},{8,4},{12,0},{1,13},{5,9},{9,5},{13,1},{2,14},{6,10},... | collective-permute-start | bytes 270344 | tf_op jit(solution)/shard_map/ppermute | solution.py:23
  23.5 8.3 %collective-permute-start.1 = (bf16[32,1408]{1,0:T(8,128)(2,1)S(1)}, bf16[32,1408]{1,0:T(8,128)(2,1)S(1)}, u32[]{:S(2)}, u32[]{:S(2)}) collective-permute-start(bf16[32,1408]{1,0:T(8,128)(2,1)S(1)} %shard_map.120.rest_0_), channel_id=1, source_target_pairs={{0,8},{4,12},{8,0},{12,4},{1,9},{5,13},{9,1},{13,5},{2,10},{6,14},... | collective-permute-start | bytes 270344 | tf_op jit(solution)/shard_map/ppermute | solution.py:23
  30.1 4.5 %collective-permute-start = (bf16[32,1408]{1,0:T(8,128)(2,1)S(1)}, bf16[32,1408]{1,0:T(8,128)(2,1)S(1)}, u32[]{:S(2)}, u32[]{:S(2)}) collective-permute-start(bf16[32,1408]{1,0:T(8,128)(2,1)S(1)} %shard_map.120.rest_0_), channel_id=1, source_target_pairs={{0,4},{4,0},{8,12},{12,8},{1,5},{5,1},{9,13},{13,9},{2,6},{6,2},{1... | collective-permute-start | bytes 270344 | tf_op jit(solution)/shard_map/ppermute | solution.py:23
  31.9 3.8 %collective-permute-start.6 = (bf16[32,1408]{1,0:T(8,128)(2,1)S(1)}, bf16[32,1408]{1,0:T(8,128)(2,1)S(1)}, u32[]{:S(2)}, u32[]{:S(2)}) collective-permute-start(bf16[32,1408]{1,0:T(8,128)(2,1)S(1)} %collective-permute-done.2.rest_3_), channel_id=1, source_target_pairs={{0,16},{16,0},{1,17},{17,1},{2,18},{18,2},{3,19},{19,3},{4,20},{20... | collective-permute-start | bytes 270344 | tf_op jit(solution)/shard_map/ppermute | solution.py:23
  34.6 4.0 %collective-permute-start.13 = (bf16[96,1280]{1,0:T(8,128)(2,1)S(1)}, bf16[96,1280]{1,0:T(8,128)(2,1)S(1)}, u32[]{:S(2)}, u32[]{:S(2)}) collective-permute-start(bf16[96,1280]{1,0:T(8,128)(2,1)S(1)} %shard_map.121.rest_8_), channel_id=1, source_target_pairs={{0,16},{16,0},{1,17},{17,1},{2,18},{18,2},{3,19},{19,3},{4,20},{20... | collective-permute-start | bytes 737288 | tf_op jit(solution)/shard_map/ppermute | solution.py:23
  34.6 4.0 %collective-permute-start.16 = (bf16[96,1280]{1,0:T(8,128)(2,1)S(1)}, bf16[96,1280]{1,0:T(8,128)(2,1)S(1)}, u32[]{:S(2)}, u32[]{:S(2)}) collective-permute-start(bf16[96,1280]{1,0:T(8,128)(2,1)S(1)} %collective-permute-done.12.rest_11_), channel_id=1, source_target_pairs={{0,16},{16,0},{1,17},{17,1},{2,18},{18,2},{3,19},{19,3},{4,20},{20... | collective-permute-start | bytes 737288 | tf_op jit(solution)/shard_map/ppermute | solution.py:23
  35.1 3.5 %collective-permute-start.15 = (bf16[96,1280]{1,0:T(8,128)(2,1)S(1)}, bf16[96,1280]{1,0:T(8,128)(2,1)S(1)}, u32[]{:S(2)}, u32[]{:S(2)}) collective-permute-start(bf16[96,1280]{1,0:T(8,128)(2,1)S(1)} %collective-permute-done.11.rest_10_), channel_id=1, source_target_pairs={{0,16},{16,0},{1,17},{17,1},{2,18},{18,2},{3,19},{19,3},{4,20},{20... | collective-permute-start | bytes 737288 | tf_op jit(solution)/shard_map/ppermute | solution.py:23
  35.2 3.4 %collective-permute-start.14 = (bf16[96,1280]{1,0:T(8,128)(2,1)S(1)}, bf16[96,1280]{1,0:T(8,128)(2,1)S(1)}, u32[]{:S(2)}, u32[]{:S(2)}) collective-permute-start(bf16[96,1280]{1,0:T(8,128)(2,1)S(1)} %collective-permute-done.10.rest_9_), channel_id=1, source_target_pairs={{0,16},{16,0},{1,17},{17,1},{2,18},{18,2},{3,19},{19,3},{4,20},{20... | collective-permute-start | bytes 737288 | tf_op jit(solution)/shard_map/ppermute | solution.py:23
  35.7 1.7 %collective-permute-start.5 = (bf16[32,1408]{1,0:T(8,128)(2,1)S(1)}, bf16[32,1408]{1,0:T(8,128)(2,1)S(1)}, u32[]{:S(2)}, u32[]{:S(2)}) collective-permute-start(bf16[32,1408]{1,0:T(8,128)(2,1)S(1)} %collective-permute-done.1.rest_2_), channel_id=1, source_target_pairs={{0,16},{16,0},{1,17},{17,1},{2,18},{18,2},{3,19},{19,3},{4,20},{20... | collective-permute-start | bytes 270344 | tf_op jit(solution)/shard_map/ppermute | solution.py:23
  37.3 1.3 collective-permute-start.4
  38.6 2.5 %copy-start = (bf16[5120,512]{1,0:T(8,128)(2,1)S(1)}, bf16[5120,512]{1,0:T(8,128)(2,1)}, u32[]{:S(2)}) copy-start(bf16[5120,512]{1,0:T(8,128)(2,1)} %sg.1) | copy-start | bytes 15728644
  41.1 2.5 %copy-start.1 = (bf16[5120,512]{1,0:T(8,128)(2,1)S(1)}, bf16[5120,512]{1,0:T(8,128)(2,1)}, u32[]{:S(2)}) copy-start(bf16[5120,512]{1,0:T(8,128)(2,1)} %su.1) | copy-start | bytes 15728644
  58.2 4.9 %slice-start.3 = ((s8[5242880]{0:T(1024)(128)(4,1)}), s8[4194304]{0:T(1024)(128)(4,1)S(1)}, s32[]{:S(2)}) async-start(s8[5242880]{0:T(1024)(128)(4,1)} %bitcast.6), calls=%async_computation.3 | async-start | bytes 8388608
  60.3 2.8 %slice-start.4 = ((s8[5242880]{0:T(1024)(128)(4,1)}), s8[1048576]{0:T(1024)(128)(4,1)S(1)}, s32[]{:S(2)}) async-start(s8[5242880]{0:T(1024)(128)(4,1)} %bitcast.6), calls=%async_computation.4 | async-start | bytes 2097152
  60.3 2.7 %collective-permute-start.17 = (bf16[256,1280]{1,0:T(8,128)(2,1)S(1)}, bf16[256,1280]{1,0:T(8,128)(2,1)S(1)}, u32[]{:S(2)}, u32[]{:S(2)}) collective-permute-start(bf16[256,1280]{1,0:T(8,128)(2,1)S(1)} %shard_map.123), channel_id=1, source_target_pairs={{0,16},{16,0},{1,17},{17,1},{2,18},{18,2},{3,19},{19,3},{4,20},{20... | collective-permute-start | bytes 1966088 | tf_op jit(solution)/shard_map/ppermute | solution.py:23
  62.6 6.7 %collective-permute-start.24 = (bf16[256,1280]{1,0:T(8,128)(2,1)S(1)}, bf16[256,1280]{1,0:T(8,128)(2,1)S(1)}, u32[]{:S(2)}, u32[]{:S(2)}) collective-permute-start(bf16[256,1280]{1,0:T(8,128)(2,1)S(1)} %shard_map.126), channel_id=1, source_target_pairs={{0,16},{16,0},{1,17},{17,1},{2,18},{18,2},{3,19},{19,3},{4,20},{20... | collective-permute-start | bytes 1966088 | tf_op jit(solution)/shard_map/ppermute | solution.py:23
  65.8 9.4 %collective-permute-start.18 = (bf16[64,1280]{1,0:T(8,128)(2,1)S(1)}, bf16[64,1280]{1,0:T(8,128)(2,1)S(1)}, u32[]{:S(2)}, u32[]{:S(2)}) collective-permute-start(bf16[64,1280]{1,0:T(8,128)(2,1)S(1)} %get-tuple-element.37), channel_id=1, source_target_pairs={{0,4},{4,0},{8,12},{12,8},{1,5},{5,1},{9,13},{13,9},{2,6},{6,2},{1... | collective-permute-start | bytes 491528 | tf_op jit(solution)/shard_map/ppermute | solution.py:23
  67.4 9.5 %collective-permute-start.19 = (bf16[64,1280]{1,0:T(8,128)(2,1)S(1)}, bf16[64,1280]{1,0:T(8,128)(2,1)S(1)}, u32[]{:S(2)}, u32[]{:S(2)}) collective-permute-start(bf16[64,1280]{1,0:T(8,128)(2,1)S(1)} %get-tuple-element.38), channel_id=1, source_target_pairs={{0,8},{4,12},{8,0},{12,4},{1,9},{5,13},{9,1},{13,5},{2,10},{6,14},... | collective-permute-start | bytes 491528 | tf_op jit(solution)/shard_map/ppermute | solution.py:23
  68.9 8.6 %collective-permute-start.20 = (bf16[64,1280]{1,0:T(8,128)(2,1)S(1)}, bf16[64,1280]{1,0:T(8,128)(2,1)S(1)}, u32[]{:S(2)}, u32[]{:S(2)}) collective-permute-start(bf16[64,1280]{1,0:T(8,128)(2,1)S(1)} %get-tuple-element.39), channel_id=1, source_target_pairs={{0,12},{4,8},{8,4},{12,0},{1,13},{5,9},{9,5},{13,1},{2,14},{6,10},... | collective-permute-start | bytes 491528 | tf_op jit(solution)/shard_map/ppermute | solution.py:23
  72.1 8.3 %collective-permute-start.25 = (bf16[64,1280]{1,0:T(8,128)(2,1)S(1)}, bf16[64,1280]{1,0:T(8,128)(2,1)S(1)}, u32[]{:S(2)}, u32[]{:S(2)}) collective-permute-start(bf16[64,1280]{1,0:T(8,128)(2,1)S(1)} %get-tuple-element.45), channel_id=1, source_target_pairs={{0,4},{4,0},{8,12},{12,8},{1,5},{5,1},{9,13},{13,9},{2,6},{6,2},{1... | collective-permute-start | bytes 491528 | tf_op jit(solution)/shard_map/ppermute | solution.py:23
  73.6 10.2 %collective-permute-start.26 = (bf16[64,1280]{1,0:T(8,128)(2,1)S(1)}, bf16[64,1280]{1,0:T(8,128)(2,1)S(1)}, u32[]{:S(2)}, u32[]{:S(2)}) collective-permute-start(bf16[64,1280]{1,0:T(8,128)(2,1)S(1)} %get-tuple-element.46), channel_id=1, source_target_pairs={{0,8},{4,12},{8,0},{12,4},{1,9},{5,13},{9,1},{13,5},{2,10},{6,14},... | collective-permute-start | bytes 491528 | tf_op jit(solution)/shard_map/ppermute | solution.py:23
  75.2 8.7 %collective-permute-start.27 = (bf16[64,1280]{1,0:T(8,128)(2,1)S(1)}, bf16[64,1280]{1,0:T(8,128)(2,1)S(1)}, u32[]{:S(2)}, u32[]{:S(2)}) collective-permute-start(bf16[64,1280]{1,0:T(8,128)(2,1)S(1)} %get-tuple-element.47), channel_id=1, source_target_pairs={{0,12},{4,8},{8,4},{12,0},{1,13},{5,9},{9,5},{13,1},{2,14},{6,10},... | collective-permute-start | bytes 491528 | tf_op jit(solution)/shard_map/ppermute | solution.py:23
  78.1 8.7 %collective-permute-start.21 = (bf16[16,1280]{1,0:T(8,128)(2,1)S(1)}, bf16[16,1280]{1,0:T(8,128)(2,1)S(1)}, u32[]{:S(2)}, u32[]{:S(2)}) collective-permute-start(bf16[16,1280]{1,0:T(8,128)(2,1)S(1)} %get-tuple-element.41), channel_id=1, source_target_pairs={{0,1},{1,0},{2,3},{3,2},{4,5},{5,4},{6,7},{7,6},{8,9},{9,8},{10,11... | collective-permute-start | bytes 122888 | tf_op jit(solution)/shard_map/ppermute | solution.py:23
  78.1 10.8 %collective-permute-start.22 = (bf16[16,1280]{1,0:T(8,128)(2,1)S(1)}, bf16[16,1280]{1,0:T(8,128)(2,1)S(1)}, u32[]{:S(2)}, u32[]{:S(2)}) collective-permute-start(bf16[16,1280]{1,0:T(8,128)(2,1)S(1)} %get-tuple-element.42), channel_id=1, source_target_pairs={{0,2},{1,3},{2,0},{3,1},{4,6},{5,7},{6,4},{7,5},{8,10},{9,11},{10,... | collective-permute-start | bytes 122888 | tf_op jit(solution)/shard_map/ppermute | solution.py:23
  80.4 8.6 %collective-permute-start.23 = (bf16[16,1280]{1,0:T(8,128)(2,1)S(1)}, bf16[16,1280]{1,0:T(8,128)(2,1)S(1)}, u32[]{:S(2)}, u32[]{:S(2)}) collective-permute-start(bf16[16,1280]{1,0:T(8,128)(2,1)S(1)} %get-tuple-element.43), channel_id=1, source_target_pairs={{0,3},{1,2},{2,1},{3,0},{4,7},{5,6},{6,5},{7,4},{8,11},{9,10},{10,... | collective-permute-start | bytes 122888 | tf_op jit(solution)/shard_map/ppermute | solution.py:23
  84.5 4.5 %collective-permute-start.28 = (bf16[16,1280]{1,0:T(8,128)(2,1)S(1)}, bf16[16,1280]{1,0:T(8,128)(2,1)S(1)}, u32[]{:S(2)}, u32[]{:S(2)}) collective-permute-start(bf16[16,1280]{1,0:T(8,128)(2,1)S(1)} %get-tuple-element.49), channel_id=1, source_target_pairs={{0,1},{1,0},{2,3},{3,2},{4,5},{5,4},{6,7},{7,6},{8,9},{9,8},{10,11... | collective-permute-start | bytes 122888 | tf_op jit(solution)/shard_map/ppermute | solution.py:23
  84.6 5.0 %collective-permute-start.29 = (bf16[16,1280]{1,0:T(8,128)(2,1)S(1)}, bf16[16,1280]{1,0:T(8,128)(2,1)S(1)}, u32[]{:S(2)}, u32[]{:S(2)}) collective-permute-start(bf16[16,1280]{1,0:T(8,128)(2,1)S(1)} %get-tuple-element.50), channel_id=1, source_target_pairs={{0,2},{1,3},{2,0},{3,1},{4,6},{5,7},{6,4},{7,5},{8,10},{9,11},{10,... | collective-permute-start | bytes 122888 | tf_op jit(solution)/shard_map/ppermute | solution.py:23
  86.8 5.9 %collective-permute-start.30 = (bf16[16,1280]{1,0:T(8,128)(2,1)S(1)}, bf16[16,1280]{1,0:T(8,128)(2,1)S(1)}, u32[]{:S(2)}, u32[]{:S(2)}) collective-permute-start(bf16[16,1280]{1,0:T(8,128)(2,1)S(1)} %get-tuple-element.51), channel_id=1, source_target_pairs={{0,3},{1,2},{2,1},{3,0},{4,7},{5,6},{6,5},{7,4},{8,11},{9,10},{10,... | collective-permute-start | bytes 122888 | tf_op jit(solution)/shard_map/ppermute | solution.py:23
  92.7 6.3 %collective-permute-start.40 = (bf16[16,2560]{1,0:T(8,128)(2,1)S(1)}, bf16[16,2560]{1,0:T(8,128)(2,1)S(1)}, u32[]{:S(2)}, u32[]{:S(2)}) collective-permute-start(bf16[16,2560]{1,0:T(8,128)(2,1)S(1)} %shard_map.129.rest_0_), channel_id=1, source_target_pairs={{0,3},{1,2},{2,1},{3,0},{4,7},{5,6},{6,5},{7,4},{8,11},{9,10},{10,... | collective-permute-start | bytes 245768 | tf_op jit(solution)/shard_map/ppermute | solution.py:23
  94.9 5.9 %collective-permute-start.39 = (bf16[16,2560]{1,0:T(8,128)(2,1)S(1)}, bf16[16,2560]{1,0:T(8,128)(2,1)S(1)}, u32[]{:S(2)}, u32[]{:S(2)}) collective-permute-start(bf16[16,2560]{1,0:T(8,128)(2,1)S(1)} %shard_map.129.rest_0_), channel_id=1, source_target_pairs={{0,2},{1,3},{2,0},{3,1},{4,6},{5,7},{6,4},{7,5},{8,10},{9,11},{10,... | collective-permute-start | bytes 245768 | tf_op jit(solution)/shard_map/ppermute | solution.py:23
  94.9 5.9 %collective-permute-start.38 = (bf16[16,2560]{1,0:T(8,128)(2,1)S(1)}, bf16[16,2560]{1,0:T(8,128)(2,1)S(1)}, u32[]{:S(2)}, u32[]{:S(2)}) collective-permute-start(bf16[16,2560]{1,0:T(8,128)(2,1)S(1)} %shard_map.129.rest_0_), channel_id=1, source_target_pairs={{0,1},{1,0},{2,3},{3,2},{4,5},{5,4},{6,7},{7,6},{8,9},{9,8},{10,11... | collective-permute-start | bytes 245768 | tf_op jit(solution)/shard_map/ppermute | solution.py:23
  100.8 18.3 %collective-permute-start.43 = (bf16[48,2560]{1,0:T(8,128)(2,1)S(1)}, bf16[48,2560]{1,0:T(8,128)(2,1)S(1)}, u32[]{:S(2)}, u32[]{:S(2)}) collective-permute-start(bf16[48,2560]{1,0:T(8,128)(2,1)S(1)} %shard_map.130.rest_8_), channel_id=1, source_target_pairs={{0,12},{4,8},{8,4},{12,0},{1,13},{5,9},{9,5},{13,1},{2,14},{6,10},... | collective-permute-start | bytes 737288 | tf_op jit(solution)/shard_map/ppermute | solution.py:23
  102.3 17.4 %collective-permute-start.42 = (bf16[48,2560]{1,0:T(8,128)(2,1)S(1)}, bf16[48,2560]{1,0:T(8,128)(2,1)S(1)}, u32[]{:S(2)}, u32[]{:S(2)}) collective-permute-start(bf16[48,2560]{1,0:T(8,128)(2,1)S(1)} %shard_map.130.rest_8_), channel_id=1, source_target_pairs={{0,8},{4,12},{8,0},{12,4},{1,9},{5,13},{9,1},{13,5},{2,10},{6,14},... | collective-permute-start | bytes 737288 | tf_op jit(solution)/shard_map/ppermute | solution.py:23
  103.7 16.0 %collective-permute-start.41 = (bf16[48,2560]{1,0:T(8,128)(2,1)S(1)}, bf16[48,2560]{1,0:T(8,128)(2,1)S(1)}, u32[]{:S(2)}, u32[]{:S(2)}) collective-permute-start(bf16[48,2560]{1,0:T(8,128)(2,1)S(1)} %shard_map.130.rest_8_), channel_id=1, source_target_pairs={{0,4},{4,0},{8,12},{12,8},{1,5},{5,1},{9,13},{13,9},{2,6},{6,2},{1... | collective-permute-start | bytes 737288 | tf_op jit(solution)/shard_map/ppermute | solution.py:23
  104.4 1.4 %collective-permute-start.34 = (bf16[16,2560]{1,0:T(8,128)(2,1)S(1)}, bf16[16,2560]{1,0:T(8,128)(2,1)S(1)}, u32[]{:S(2)}, u32[]{:S(2)}) collective-permute-start(bf16[16,2560]{1,0:T(8,128)(2,1)S(1)} %shard_map.129.rest_0_), channel_id=1, source_target_pairs={{0,16},{16,0},{1,17},{17,1},{2,18},{18,2},{3,19},{19,3},{4,20},{20... | collective-permute-start | bytes 245768 | tf_op jit(solution)/shard_map/ppermute | solution.py:23
  104.4 9.6 %collective-permute-start.33 = (bf16[16,2560]{1,0:T(8,128)(2,1)S(1)}, bf16[16,2560]{1,0:T(8,128)(2,1)S(1)}, u32[]{:S(2)}, u32[]{:S(2)}) collective-permute-start(bf16[16,2560]{1,0:T(8,128)(2,1)S(1)} %shard_map.129.rest_0_), channel_id=1, source_target_pairs={{0,12},{4,8},{8,4},{12,0},{1,13},{5,9},{9,5},{13,1},{2,14},{6,10},... | collective-permute-start | bytes 245768 | tf_op jit(solution)/shard_map/ppermute | solution.py:23
  105.8 10.9 %collective-permute-start.32 = (bf16[16,2560]{1,0:T(8,128)(2,1)S(1)}, bf16[16,2560]{1,0:T(8,128)(2,1)S(1)}, u32[]{:S(2)}, u32[]{:S(2)}) collective-permute-start(bf16[16,2560]{1,0:T(8,128)(2,1)S(1)} %shard_map.129.rest_0_), channel_id=1, source_target_pairs={{0,8},{4,12},{8,0},{12,4},{1,9},{5,13},{9,1},{13,5},{2,10},{6,14},... | collective-permute-start | bytes 245768 | tf_op jit(solution)/shard_map/ppermute | solution.py:23
  114.0 5.2 %collective-permute-start.31 = (bf16[16,2560]{1,0:T(8,128)(2,1)S(1)}, bf16[16,2560]{1,0:T(8,128)(2,1)S(1)}, u32[]{:S(2)}, u32[]{:S(2)}) collective-permute-start(bf16[16,2560]{1,0:T(8,128)(2,1)S(1)} %shard_map.129.rest_0_), channel_id=1, source_target_pairs={{0,4},{4,0},{8,12},{12,8},{1,5},{5,1},{9,13},{13,9},{2,6},{6,2},{1... | collective-permute-start | bytes 245768 | tf_op jit(solution)/shard_map/ppermute | solution.py:23
  116.7 6.3 %collective-permute-start.44 = (bf16[48,2560]{1,0:T(8,128)(2,1)S(1)}, bf16[48,2560]{1,0:T(8,128)(2,1)S(1)}, u32[]{:S(2)}, u32[]{:S(2)}) collective-permute-start(bf16[48,2560]{1,0:T(8,128)(2,1)S(1)} %shard_map.130.rest_8_), channel_id=1, source_target_pairs={{0,16},{16,0},{1,17},{17,1},{2,18},{18,2},{3,19},{19,3},{4,20},{20... | collective-permute-start | bytes 737288 | tf_op jit(solution)/shard_map/ppermute | solution.py:23
  119.1 1.3 collective-permute-start.37
  119.1 3.8 %collective-permute-start.47 = (bf16[48,2560]{1,0:T(8,128)(2,1)S(1)}, bf16[48,2560]{1,0:T(8,128)(2,1)S(1)}, u32[]{:S(2)}, u32[]{:S(2)}) collective-permute-start(bf16[48,2560]{1,0:T(8,128)(2,1)S(1)} %collective-permute-done.43.rest_11_), channel_id=1, source_target_pairs={{0,16},{16,0},{1,17},{17,1},{2,18},{18,2},{3,19},{19,3},{4,20},{20... | collective-permute-start | bytes 737288 | tf_op jit(solution)/shard_map/ppermute | solution.py:23
  119.7 3.3 %collective-permute-start.46 = (bf16[48,2560]{1,0:T(8,128)(2,1)S(1)}, bf16[48,2560]{1,0:T(8,128)(2,1)S(1)}, u32[]{:S(2)}, u32[]{:S(2)}) collective-permute-start(bf16[48,2560]{1,0:T(8,128)(2,1)S(1)} %collective-permute-done.42.rest_10_), channel_id=1, source_target_pairs={{0,16},{16,0},{1,17},{17,1},{2,18},{18,2},{3,19},{19,3},{4,20},{20... | collective-permute-start | bytes 737288 | tf_op jit(solution)/shard_map/ppermute | solution.py:23
  119.7 3.3 %collective-permute-start.45 = (bf16[48,2560]{1,0:T(8,128)(2,1)S(1)}, bf16[48,2560]{1,0:T(8,128)(2,1)S(1)}, u32[]{:S(2)}, u32[]{:S(2)}) collective-permute-start(bf16[48,2560]{1,0:T(8,128)(2,1)S(1)} %collective-permute-done.41.rest_9_), channel_id=1, source_target_pairs={{0,16},{16,0},{1,17},{17,1},{2,18},{18,2},{3,19},{19,3},{4,20},{20... | collective-permute-start | bytes 737288 | tf_op jit(solution)/shard_map/ppermute | solution.py:23
  120.4 1.3 collective-permute-start.36
  121.7 1.3 collective-permute-start.35

commit v3 on v2

v3 whole, which is shorter than its diff:
```python
import functools
import math

import jax
import jax.numpy as jnp
from jax import lax
from jax.experimental import pallas as pl
from jax.experimental.pallas import tpu as pltpu
from jax.sharding import PartitionSpec as P


BF = jnp.bfloat16
F32 = jnp.float32
ANY = pl.BlockSpec(memory_space=pl.ANY)
HBM = pl.BlockSpec(memory_space=pltpu.HBM)
VM = pl.BlockSpec(memory_space=pltpu.VMEM)
SM = pl.BlockSpec(memory_space=pltpu.SMEM)
MIB = 1024 * 1024


def swap(x, axis, n, r):
    return lax.ppermute(x, axis, [(i, i ^ r) for i in range(n)])


def tile_of(n, most):
    t = min(n, most)
    while n % t:
        t //= 2
    return t


def even(n):
    return max(k for k in range(128, 641, 128) if n % k == 0)


def call(kernel, out_shape, in_specs, args, flops=0, moved=0, scratch=(), limit=4, out_specs=None):
    return pl.pallas_call(
        kernel,
        out_shape=out_shape,
        in_specs=in_specs,
        out_specs=jax.tree.map(lambda _: VM, out_shape) if out_specs is None else out_specs,
        scratch_shapes=list(scratch),
        compiler_params=pltpu.CompilerParams(vmem_limit_bytes=limit * MIB),
        cost_estimate=pl.CostEstimate(
            flops=int(flops), bytes_accessed=int(moved), transcendentals=0
        ),
    )(*args)


def shape(dims, dtype=BF):
    return jax.ShapeDtypeStruct(tuple(dims), dtype)


def dot(a, b):
    return jnp.dot(a, b, preferred_element_type=F32)


def whole(ref):
    return ref[...].astype(F32)


def pack_kernel(ne, sc, tokens, ids_in, gates_in, out, ids, gates, sem):
    rows, width = tokens.shape
    copies = [
        pltpu.make_async_copy(src, dst, sem.at[n])
        for n, (src, dst) in enumerate(
            ((ids_in, ids), (gates_in, gates), (tokens, out.at[:, pl.ds(0, width)]))
        )
    ]
    for c in copies:
        c.start()
    for c in copies:
        c.wait()
    g = gates[...]
    share = g / jnp.sum(g, axis=0, keepdims=True)
    lines = lax.broadcasted_iota(jnp.int32, (128, rows), 0)
    w = jnp.zeros(lines.shape, F32)
    for k in range(ids.shape[0]):
        w = w + jnp.where(ids[k : k + 1, :] == lines % ne, share[k : k + 1, :], 0.0)
    high = w.astype(BF).astype(F32)
    middle = (w - high).astype(BF).astype(F32)
    low = w - high - middle
    terms = jnp.where(lines < ne, high, jnp.where(lines < 2 * ne, middle, low))
    terms = jnp.where(lines < 3 * ne, terms, 0.0)
    out[:, width:] = terms.T.astype(BF)


def pack(sc, tokens, ids, gates, ne):
    rows, width = tokens.shape
    return call(
        functools.partial(pack_kernel, ne),
        shape((rows, width + 128)),
        [SM, HBM, HBM, HBM],
        (sc, *map(in_hbm, (tokens, ids.T, gates.T))),
        moved=4 * rows * width,
        scratch=[
            pltpu.VMEM(ids.shape[::-1], jnp.int32),
            pltpu.VMEM(gates.shape[::-1], F32),
            pltpu.SemaphoreType.DMA((3,)),
        ],
    )


def in_hbm(x):
    return pltpu.with_memory_space_constraint(x, pltpu.HBM)


def load_kernel(*refs):
    n = (len(refs) - 2) // 2
    copies = [
        pltpu.make_async_copy(refs[1 + k], refs[1 + n + k], refs[-1].at[k]) for k in range(n)
    ]
    for c in copies:
        c.start()
    for c in copies:
        c.wait()


def load(after, weights):
    return call(
        load_kernel,
        [shape(w.shape) for w in weights],
        [ANY] + [HBM] * len(weights),
        (after, *map(in_hbm, weights)),
        moved=2 * sum(w.size for w in weights),
        scratch=[pltpu.SemaphoreType.DMA((len(weights),))],
        limit=1,
    )


def stack_kernel(*refs):
    out, n = refs[-1], refs[0].shape[0]
    for i, r in enumerate(refs[:-1]):
        out[i * n : (i + 1) * n] = r[...]


def stack(xs):
    n, width = xs[0].shape
    return call(
        stack_kernel, shape((n * len(xs), width)), [VM] * len(xs), xs, moved=4 * len(xs) * n * width
    )


def up_kernel(nd, ne, nz, rows, width, sc, tg, tu, sg_in, su_in, td_in, *rest):
    count = nd * ne
    own, line = rest[:count], rest[count : 2 * count]
    at_ref, act_ref, f1_ref, f2_ref, xs, td = rest[2 * count : 2 * count + 6]
    sg, su, w_ref, sem, wsem, dsem = rest[2 * count + 6 :]
    bt, bs = tile_of(tg.shape[2], 256), tile_of(sg.shape[1], 256)
    nt, ns = tg.shape[2] // bt, sg.shape[1] // bs

    def row_of(n):
        return pl.multiple_of((n % ne * nd + (sc[0] ^ (n // ne))) * rows, rows)

    copies = []
    for n in range(count):
        for j in range(nz):
            col = pl.multiple_of((sc[2] ^ j) * width, 128)
            src = line[n].at[pl.ds((j - 1) * rows, rows), :] if j else own[n].at[:, pl.ds(0, width)]
            dst = xs.at[pl.ds(row_of(n), rows), pl.ds(col, width)]
            copies.append(pltpu.make_async_copy(src, dst, sem.at[n * nz + j]))
    tails = [
        pltpu.make_async_copy(own[n].at[:, pl.ds(width, 128)], w_ref.at[n], wsem.at[n])
        for n in range(count)
    ]
    for c in tails + copies:
        c.start()
    for c in tails + copies:
        c.wait()
    ahead = [
        pltpu.make_async_copy(src, dst, dsem.at[k])
        for k, (src, dst) in enumerate(((sg_in, sg), (su_in, su), (td_in, td)))
    ]
    for c in ahead:
        c.start()

    weights = []
    for b in range(ne):
        pair = []
        for a in range(nd):
            m = w_ref[a * ne + b].astype(F32)
            lanes = lax.broadcasted_iota(jnp.int32, m.shape, 1)
            ours = (lanes % ne == sc[1]) & (lanes < 3 * ne)
            pair.append(jnp.sum(jnp.where(ours, m, 0.0), axis=1, keepdims=True))
        for d in range(nd):
            value = pair[0]
            for a in range(1, nd):
                value = jnp.where((sc[0] ^ a) == d, pair[a], value)
            weights.append(value)
    w = jnp.concatenate(weights, axis=0)

    cut = tile_of(nz * width, 1280)
    cuts = [slice(k, k + cut) for k in range(0, nz * width, cut)]

    @pl.loop(0, nt)
    def _(i):
        at = pl.ds(pl.multiple_of(i * bt, bt), bt)
        g = sum(dot(xs[:, k], tg[0, k, at]) for k in cuts)
        u = sum(dot(xs[:, k], tu[0, k, at]) for k in cuts)
        a = g * jax.nn.sigmoid(g) * u
        at_ref[:, at] = jnp.where(w != 0.0, -w * a, 0.0).astype(BF)

    for c in ahead[:2]:
        c.wait()

    @pl.loop(0, ns)
    def _(i):
        at = pl.ds(pl.multiple_of(i * bs, bs), bs)
        g = sum(dot(xs[:, k], sg[k, at]) for k in cuts)
        u = sum(dot(xs[:, k], su[k, at]) for k in cuts)
        s = jax.nn.sigmoid(g)
        f2 = g * s
        act_ref[:, at] = (f2 * u).astype(BF)
        f1_ref[:, at] = u * s * (1.0 + g * (1.0 - s))
        f2_ref[:, at] = f2

    for c in ahead[2:]:
        c.wait()


def up(sc, tg, tu, sg, su, td, own, line, dims):
    nd, ne, nz, rows, width = dims
    total, model = rows * nd * ne, width * nz
    ht, hs = tg.shape[2], sg.shape[1]
    count = nd * ne
    return call(
        functools.partial(up_kernel, nd, ne, nz, rows, width),
        [
            shape((total, ht)),
            shape((total, hs)),
            shape((total, hs), F32),
            shape((total, hs), F32),
            shape((total, model)),
            shape(td.shape),
        ],
        [SM] + [VM] * 2 + [HBM] * 3 + [ANY] * (2 * count),
        (sc, tg, tu, *map(in_hbm, (sg, su, td)), *own, *line),
        flops=4 * total * model * (ht + hs),
        moved=2 * total * model,
        scratch=[
            pltpu.VMEM(sg.shape, BF),
            pltpu.VMEM(su.shape, BF),
            pltpu.VMEM((count, rows, 128), BF),
            pltpu.SemaphoreType.DMA((count * nz,)),
            pltpu.SemaphoreType.DMA((count,)),
            pltpu.SemaphoreType.DMA((3,)),
        ],
        limit=15,
    )


def column(sc, other, base, model, nd, i, bn):
    half = model // nd
    start = ((1 - sc[0]) if other else sc[0]) * half + base
    return pl.ds(pl.multiple_of(start + i * bn, 128), bn)


def sent_kernel(base, nd, sc, at, td, *rest):
    out = rest[0]
    if len(rest) > 1:
        sd_in, out, sd, sem = rest
        ahead = pltpu.make_async_copy(sd_in, sd, sem)
        ahead.start()
    model, width = td.shape[2], out.shape[1]
    bn = even(width)
    for i in range(width // bn):
        cols = column(sc, True, base, model, nd, i, bn)
        out[:, i * bn : (i + 1) * bn] = dot(at[...], td[0, :, cols]).astype(BF)
    if len(rest) > 1:
        ahead.wait()


def sent_part(sc, at, td, base, width, nd, bring=()):
    total, ht = at.shape
    return call(
        functools.partial(sent_kernel, base, nd),
        [shape((total, width))] + [shape(w.shape) for w in bring],
        [SM, VM, VM] + [HBM] * len(bring),
        (sc, at, td, *map(in_hbm, bring)),
        flops=2 * total * width * ht,
        moved=2 * total * width,
        scratch=[pltpu.SemaphoreType.DMA] * len(bring),
        limit=4,
    )


def kept_kernel(base, nd, sc, at, act, td, sd, out):
    model, width = td.shape[2], out.shape[1]
    bn = even(width)
    for i in range(width // bn):
        cols = column(sc, False, base, model, nd, i, bn)
        out[:, i * bn : (i + 1) * bn] = dot(at[...], td[0, :, cols]) + dot(act[...], sd[:, cols])


def kept_part(sc, at, act, td, sd, base, width, nd):
    total, ht = at.shape
    hs = sd.shape[0]
    return call(
        functools.partial(kept_kernel, base, nd),
        shape((total, width), F32),
        [SM] + [VM] * 4,
        (sc, at, act, td, sd),
        flops=2 * total * width * (ht + hs),
        moved=2 * total * width,
        limit=4,
    )


def blocks_kernel(own, got, *outs):
    rb = outs[0].shape[0]
    for b, out in enumerate(outs):
        rows = slice(b * rb, (b + 1) * rb)
        out[...] = (own[rows] + got[rows].astype(F32)).astype(BF)


def blocks(own, got, ne):
    total, width = own.shape
    return call(
        blocks_kernel,
        [shape((total // ne, width))] * ne,
        [VM, VM],
        (own, got),
        moved=8 * total * width,
    )


def lines_kernel(ne, sc, own, got, *outs):
    nz = len(outs)
    rb = own.shape[0] // ne
    rp = rb // nz
    for j, out in enumerate(outs):
        for b in range(ne):
            rows = pl.ds(pl.multiple_of(b * rb + (sc[2] ^ j) * rp, rp), rp)
            out[b * rp : (b + 1) * rp] = (own[rows, :] + got[rows, :].astype(F32)).astype(BF)


def line_blocks(sc, own, got, ne, nz):
    total, width = own.shape
    return call(
        functools.partial(lines_kernel, ne),
        [shape((total // nz, width))] * nz,
        [SM, VM, VM],
        (sc, own, got),
        moved=8 * total * width,
    )


def sum_kernel(pick, count, sc, *refs):
    parts, outs = refs[:count], refs[count:]
    rp = outs[0].shape[0]
    for j, out in enumerate(outs):
        first = (sc[2] ^ j) * rp if pick else j * rp
        rows = pl.ds(pl.multiple_of(first, rp), rp)
        out[...] = sum(p[rows, :].astype(F32) for p in parts).astype(BF)


def sum_parts(sc, parts, n, pick):
    rb, width = parts[0].shape
    return call(
        functools.partial(sum_kernel, pick, len(parts)),
        [shape((rb // n, width))] * n,
        [SM] + [VM] * len(parts),
        (sc, *parts),
        moved=4 * len(parts) * rb * width,
    )


def final_kernel(counts, scale, *refs):
    out, at, col = refs[-1], 0, 0
    for n in counts:
        parts = refs[at : at + n]
        width = parts[0].shape[1]
        out[:, col : col + width] = (sum(whole(p) for p in parts) * scale).astype(BF)
        at, col = at + n, col + width


def final(groups, scale):
    rp = groups[0][0].shape[0]
    width = sum(g[0].shape[1] for g in groups)
    flat = [p for g in groups for p in g]
    return call(
        functools.partial(final_kernel, [len(g) for g in groups], scale),
        shape((rp, width)),
        [VM] * len(flat),
        flat,
        moved=8 * rp * width,
    )


def back_kernel(nd, ne, nz, model_tokens, grad_scale, sc, act, sd, f1, f2, x_in, *rest):
    count = nd * ne
    own, line = rest[:count], rest[count : 2 * count]
    gg, gu, gd, loss = rest[2 * count : 2 * count + 4]
    xs, d_ref, act_t, sq, dpre, dbuf, xbuf, xsem, sem, dsem, gsem = rest[2 * count + 4 :]
    rp, half = own[0].shape
    total, hs = act.shape
    model = half * nd
    rb = total // ne
    fetch = pltpu.make_async_copy(x_in, xs, xsem)
    fetch.start()
    copies = []
    for n in range(count):
        for j in range(nz):
            row = pl.multiple_of(n % ne * rb + (sc[2] ^ j) * rp, rp)
            col = pl.multiple_of((sc[0] ^ (n // ne)) * half, 128)
            src = line[n].at[pl.ds((j - 1) * rp, rp), :] if j else own[n]
            dst = d_ref.at[pl.ds(row, rp), pl.ds(col, half)]
            copies.append(pltpu.make_async_copy(src, dst, sem.at[n * nz + j]))
    for c in copies:
        c.start()
    act_t[...] = act[...].T
    for c in copies:
        c.wait()
    bn = dbuf.shape[2]
    n = model // bn
    dact = jnp.zeros((total, hs), F32)
    out = []
    s = jnp.zeros((total, 128), F32)
    for i in range(n):
        here = slice(i * bn, (i + 1) * bn)
        dbuf[i] = dot(act_t[...], d_ref[:, here]).astype(BF)
        out.append(pltpu.make_async_copy(dbuf.at[i], gd.at[:, here], dsem.at[i]))
        out[-1].start()
        dact = dact + lax.dot_general(
            d_ref[:, here], sd[:, here], (((1,), (1,)), ((), ())), preferred_element_type=F32
        )
        f = d_ref[:, here].astype(F32)
        for k in range(bn // 128):
            part = f[:, k * 128 : (k + 1) * 128]
            s = s + part * part
    dpre[:, :hs] = (dact * f1[...]).astype(BF)
    dpre[:, hs:] = (dact * f2[...]).astype(BF)
    fetch.wait()
    for i in range(n):
        here = slice(i * bn, (i + 1) * bn)
        both = lax.dot_general(
            xs[:, here], dpre[...], (((0,), (0,)), ((), ())), preferred_element_type=F32
        ).astype(BF)
        for k, g in enumerate((gg, gu)):
            at = 2 * i + k
            xbuf[at] = both[:, k * hs : (k + 1) * hs]
            out.append(pltpu.make_async_copy(xbuf.at[at], g.at[here, :], gsem.at[at]))
            out[-1].start()
    sq[...] = s
    tot = jnp.zeros((rb, 128), F32)
    for e in range(ne):
        tot = tot + sq[pl.ds(pl.multiple_of((sc[1] ^ e) * rb, rb), rb), :]
    value = jnp.sum(jnp.sum(tot, axis=0, keepdims=True), axis=1, keepdims=True)
    loss[...] = value * (1.0 / (grad_scale * grad_scale)) / model_tokens
    for c in out:
        c.wait()


def back(sc, act, sd, f1, f2, xs, own, line, dims, model_tokens, grad_scale):
    nd, ne, nz = dims
    total, hs = act.shape
    model = sd.shape[1]
    bn = tile_of(model, 1280)
    n = model // bn
    return call(
        functools.partial(back_kernel, nd, ne, nz, model_tokens, grad_scale),
        [shape((model, hs)), shape((model, hs)), shape((hs, model)), shape((1, 1), F32)],
        [SM] + [VM] * 4 + [ANY] * (1 + 2 * nd * ne),
        (sc, act, sd, f1, f2, xs, *own, *line),
        flops=8 * total * model * hs,
        moved=6 * model * hs,
        scratch=[
            pltpu.VMEM((total, model), BF),
            pltpu.VMEM((total, model), BF),
            pltpu.VMEM((hs, total), BF),
            pltpu.VMEM((total, 128), F32),
            pltpu.VMEM((total, 2 * hs), BF),
            pltpu.VMEM((n, hs, bn), BF),
            pltpu.VMEM((2 * n, bn, hs), BF),
            pltpu.SemaphoreType.DMA,
            pltpu.SemaphoreType.DMA((nd * ne * nz,)),
            pltpu.SemaphoreType.DMA((n,)),
            pltpu.SemaphoreType.DMA((2 * n,)),
        ],
        out_specs=[HBM, HBM, HBM, VM],
        limit=32,
    )


def body(tokens, expert_ids, gate_weights, t_gate, t_up, t_down, s_gate, s_up, s_down):
    nd, ne, nz = lax.axis_size("dp"), lax.axis_size("expert"), lax.axis_size("tensor")
    rows, width = tokens.shape
    model = width * nz
    total = rows * ne * nd
    sc = jnp.stack(
        [lax.axis_index("dp"), lax.axis_index("expert"), lax.axis_index("tensor")]
    ).astype(jnp.int32)

    def spread(x, packed):
        line = [swap(x, "tensor", nz, j) for j in range(1, nz)]
        own = [packed] + [swap(packed, "expert", ne, b) for b in range(1, ne)]
        line = stack(line)
        lines = [line] + [swap(line, "expert", ne, b) for b in range(1, ne)]
        own += [swap(z, "dp", nd, 1) for z in own]
        lines += [swap(z, "dp", nd, 1) for z in lines]
        return own, lines

    own, lines = spread(tokens, pack(sc, tokens, expert_ids, gate_weights, ne))
    loaded = []
    for w in (t_gate, t_up):
        loaded += load(lines[0], (w,))
    at, act, f1, f2, xs, td = up(
        sc, *loaded, s_gate, s_up, t_down, own, lines, (nd, ne, nz, rows, width)
    )

    half = model // nd
    cut = half - max(128, half // 10 // 128 * 128)
    parts = ((0, cut), (cut, half - cut))
    sent, sd = sent_part(sc, at, td, *parts[0], nd, [s_down])
    sent = [sent, *sent_part(sc, at, td, *parts[1], nd)]
    got = [swap(s, "dp", nd, 1) for s in sent]
    kept = [kept_part(sc, at, act, td, sd, *p, nd) for p in parts]

    def over(xs, axis, n):
        return [xs[0]] + [swap(xs[k], axis, n, k) for k in range(1, n)]

    wide = over(blocks(kept[0], got[0], ne), "expert", ne)
    slim = over(line_blocks(sc, kept[1], got[1], ne, nz), "tensor", nz)
    slim = over(sum_parts(sc, slim, ne, False), "expert", ne)
    wide = sum_parts(sc, wide, nz, True)
    wide = over(wide, "tensor", nz)
    grad_scale = 1.0 / math.sqrt(total)
    d_out = final((wide, slim), grad_scale)

    own, lines = spread(d_out, d_out)
    gg, gu, gd, loss = back(
        sc, act, sd, f1, f2, xs, own, lines, (nd, ne, nz), total * model, grad_scale
    )
    return gg, gu, gd, loss[0, 0]


def solution(mesh):
    return jax.shard_map(
        body,
        mesh=mesh,
        in_specs=(
            P(("dp", "expert"), "tensor"),
            P(("dp", "expert"), None),
            P(("dp", "expert"), None),
            P("expert", None, ("dp", "tensor")),
            P("expert", None, ("dp", "tensor")),
            P("expert", ("dp", "tensor"), None),
            P(None, ("expert", "tensor")),
            P(None, ("expert", "tensor")),
            P(("expert", "tensor"), None),
        ),
        out_specs=(
            P(None, ("expert", "tensor")),
            P(None, ("expert", "tensor")),
            P(("expert", "tensor"), None),
            P(),
        ),
        check_vma=False,
    )
```

time: 136 us -> 142 us (1.044)
  waiting for transfers between devices: 41.6 us -> 50.1 us
  local copies, waits for them, and re-layouts: 7.4 us -> 0 us
  Pallas kernels: 38.8 us -> 42.7 us
    ppermute x48, waiting for transfers between devices: 41.6 us -> 50.1 us  [swap(): return lax.ppermute(x, axis, [(i, i ^ r) for i in range(n)])]
    unnamed x18 -> x0, local copies, waits for them, and re-layouts: 7.4 us -> none
    pallas_call x13 -> x16, Pallas kernels: 38.8 us -> 42.7 us  [call(): pl.pallas_call(kernel, out_shape=out_shape, in_specs=in_specs, out_specs=...]
  transfers between devices with their start and end apart: 48 -> 48, of which waited for: 20 -> 22; matrix products, arithmetic and copies ran while one was open for 1% -> 0% of each run, Pallas kernels for 7% -> 12%
where the time goes in v3:
time: 142 us; the launch traced here: 141 us
  waiting for transfers between devices  50.1 us (35%)
  starting transfers between devices  47.5 us (33%)
  Pallas kernels  42.7 us (30%)
    ppermute x48, waiting for transfers between devices, swap(): return lax.ppermute(x, axis, [(i, i ^ r) for i in range(n)])  50.1 us
    ppermute x48, starting transfers between devices, swap(): return lax.ppermute(x, axis, [(i, i ^ r) for i in range(n)])  47.5 us
    pallas_call x16, Pallas kernels, call(): pl.pallas_call(kernel, out_shape=out_shape, in_specs=in_specs, out_specs=...  42.7 us
  transfers between devices with their start and end apart: 48, of which 22 were waited for; matrix products, arithmetic and copies ran while one was open for 0% of the time, Pallas kernels for 12%

profile of v3, /device:TPU:0, one launch (start us, length us, event | category | flops | bytes accessed | tf_op | source)
XLA Modules:
  0.0 141.4 jit_solution(10847644590686133331)
XLA Ops:
  0.6 4.1 %collective-permute-start.1 = (bf16[32,1280]{1,0:T(8,128)(2,1)}, bf16[32,1280]{1,0:T(8,128)(2,1)S(1)}, u32[]{:S(2)}, u32[]{:S(2)}) collective-permute-start(bf16[32,1280]{1,0:T(8,128)(2,1)} %tokens.1), channel_id=1, source_target_pairs={{0,2},{1,3},{2,0},{3,1},{4,6},{5,7},{6,4},{7,5},{8,10},{9,11},{10,... | collective-permute-start | bytes 245768 | tf_op jit(solution)/shard_map/ppermute | solution.py:22
  4.8 1.6 %collective-permute-start = (bf16[32,1280]{1,0:T(8,128)(2,1)}, bf16[32,1280]{1,0:T(8,128)(2,1)S(1)}, u32[]{:S(2)}, u32[]{:S(2)}) collective-permute-start(bf16[32,1280]{1,0:T(8,128)(2,1)} %tokens.1), channel_id=1, source_target_pairs={{0,1},{1,0},{2,3},{3,2},{4,5},{5,4},{6,7},{7,6},{8,9},{9,8},{10,11... | collective-permute-start | bytes 245768 | tf_op jit(solution)/shard_map/ppermute | solution.py:22
  6.3 3.0 %collective-permute-done.1.refs_1_ = bf16[32,1280]{1,0:T(8,128)(2,1)S(1)} collective-permute-done((bf16[32,1280]{1,0:T(8,128)(2,1)}, bf16[32,1280]{1,0:T(8,128)(2,1)S(1)}, u32[]{:S(2)}, u32[]{:S(2)}) %collective-permute-start.1) | collective-permute-done | bytes 81952 | tf_op jit(solution)/shard_map/ppermute | solution.py:22
  9.6 3.2 %collective-permute-done.2.refs_2_ = bf16[32,1280]{1,0:T(8,128)(2,1)S(1)} collective-permute-done((bf16[32,1280]{1,0:T(8,128)(2,1)}, bf16[32,1280]{1,0:T(8,128)(2,1)S(1)}, u32[]{:S(2)}, u32[]{:S(2)}) %collective-permute-start.2) | collective-permute-done | bytes 81952 | tf_op jit(solution)/shard_map/ppermute | solution.py:22
  12.8 2.6 %collective-permute-start.12 = (bf16[96,1280]{1,0:T(8,128)(2,1)S(1)}, bf16[96,1280]{1,0:T(8,128)(2,1)S(1)}, u32[]{:S(2)}, u32[]{:S(2)}) collective-permute-start(bf16[96,1280]{1,0:T(8,128)(2,1)S(1)} %shard_map.120.refs_0_.rest_8_), channel_id=1, source_target_pairs={{0,12},{4,8},{8,4},{12,0},{1,13},{5,9},{9,5},{13,1},{2,14},{6,10},... | collective-permute-start | bytes 737288 | tf_op jit(solution)/shard_map/ppermute | solution.py:22
  15.4 0.5 collective-permute-start.11
  15.9 0.5 collective-permute-start.10
  16.4 1.6 %shard_map.123.rest_0_ = bf16[32,1408]{1,0:T(8,128)(2,1)S(1)} custom-call(s32[3]{0:T(128)S(1)} %pad_add_fusion.sc, bf16[32,1280]{1,0:T(8,128)(2,1)} %tokens.1, s32[2,32]{1,0:T(2,128)} %bitcast.6, f32[2,32]{1,0:T(2,128)} %bitcast.7), custom_call_target="tpu_custom_call" | custom-call | bytes 163840 | tf_op jit(solution)/shard_map/pallas_call | solution.py:37
  18.1 2.6 %collective-permute-start.5 = (bf16[32,1408]{1,0:T(8,128)(2,1)S(1)}, bf16[32,1408]{1,0:T(8,128)(2,1)S(1)}, u32[]{:S(2)}, u32[]{:S(2)}) collective-permute-start(bf16[32,1408]{1,0:T(8,128)(2,1)S(1)} %shard_map.123.rest_0_), channel_id=1, source_target_pairs={{0,12},{4,8},{8,4},{12,0},{1,13},{5,9},{9,5},{13,1},{2,14},{6,10},... | collective-permute-start | bytes 270344 | tf_op jit(solution)/shard_map/ppermute | solution.py:22
  20.7 0.5 collective-permute-start.4
  21.2 6.0 %collective-permute-done.5.rest_3_ = bf16[32,1408]{1,0:T(8,128)(2,1)S(1)} collective-permute-done((bf16[32,1408]{1,0:T(8,128)(2,1)S(1)}, bf16[32,1408]{1,0:T(8,128)(2,1)S(1)}, u32[]{:S(2)}, u32[]{:S(2)}) %collective-permute-start.5) | collective-permute-done | bytes 90144 | tf_op jit(solution)/shard_map/ppermute | solution.py:22
  27.2 1.5 %collective-permute-start.3 = (bf16[32,1408]{1,0:T(8,128)(2,1)S(1)}, bf16[32,1408]{1,0:T(8,128)(2,1)S(1)}, u32[]{:S(2)}, u32[]{:S(2)}) collective-permute-start(bf16[32,1408]{1,0:T(8,128)(2,1)S(1)} %shard_map.123.rest_0_), channel_id=1, source_target_pairs={{0,4},{4,0},{8,12},{12,8},{1,5},{5,1},{9,13},{13,9},{2,6},{6,2},{1... | collective-permute-start | bytes 270344 | tf_op jit(solution)/shard_map/ppermute | solution.py:22
  28.7 0.3 collective-permute-done.4.rest_2_
  29.0 2.7 %collective-permute-done.3.rest_1_ = bf16[32,1408]{1,0:T(8,128)(2,1)S(1)} collective-permute-done((bf16[32,1408]{1,0:T(8,128)(2,1)S(1)}, bf16[32,1408]{1,0:T(8,128)(2,1)S(1)}, u32[]{:S(2)}, u32[]{:S(2)}) %collective-permute-start.3) | collective-permute-done | bytes 90144 | tf_op jit(solution)/shard_map/ppermute | solution.py:22
  31.7 0.5 collective-permute-start.16
  32.3 0.4 collective-permute-start.14
  32.8 1.6 %collective-permute-done.8.rest_6_ = bf16[32,1408]{1,0:T(8,128)(2,1)S(1)} collective-permute-done((bf16[32,1408]{1,0:T(8,128)(2,1)S(1)}, bf16[32,1408]{1,0:T(8,128)(2,1)S(1)}, u32[]{:S(2)}, u32[]{:S(2)}) %collective-permute-start.8) | collective-permute-done | bytes 90144 | tf_op jit(solution)/shard_map/ppermute | solution.py:22
  34.6 4.0 %shard_map.122.tu = bf16[1,5120,1024]{2,1,0:T(8,128)(2,1)S(1)} custom-call(bf16[96,1280]{1,0:T(8,128)(2,1)S(1)} %shard_map.120.refs_0_.rest_8_, bf16[1,5120,1024]{2,1,0:T(8,128)(2,1)} %refs_1_.3), custom_call_target="tpu_custom_call" | custom-call | bytes 10485760 | tf_op jit(solution)/shard_map/pallas_call | solution.py:37
  38.6 4.0 %shard_map.121.tg = bf16[1,5120,1024]{2,1,0:T(8,128)(2,1)S(1)} custom-call(bf16[96,1280]{1,0:T(8,128)(2,1)S(1)} %shard_map.120.refs_0_.rest_8_, bf16[1,5120,1024]{2,1,0:T(8,128)(2,1)} %refs_1_.2), custom_call_target="tpu_custom_call" | custom-call | bytes 10485760 | tf_op jit(solution)/shard_map/pallas_call | solution.py:37
  42.6 11.5 %shard_map.124 = (bf16[256,1024]{1,0:T(8,128)(2,1)S(1)}, bf16[256,512]{1,0:T(8,128)(2,1)S(1)}, f32[256,512]{1,0:T(8,128)S(1)}, f32[256,512]{1,0:T(8,128)S(1)}, b...) custom-call(s32[3]{0:T(128)S(1)} %pad_add_fusion.sc, bf16[1,5120,1024]{2,1,0:T(8,128)(2,1)S(1)} %shard_map.121.tg, ...), custom_call_target="tpu_custom_call" | custom-call | flops 8053063680 | bytes 2621440 | tf_op jit(solution)/shard_map/pallas_call | solution.py:37
  54.2 3.0 %shard_map.125 = (bf16[256,2304]{1,0:T(8,128)(2,1)S(1)}, bf16[512,5120]{1,0:T(8,128)(2,1)S(1)}) custom-call(s32[3]{0:T(128)S(1)} %pad_add_fusion.sc, bf16[256,1024]{1,0:T(8,128)(2,1)S(1)} %get-tuple-element.33.at, bf16[1,1024,5120]{2,1,0:T(8,128)(2,1)S(1)} %get-tuple-element.34.td, bf16[512,5120]{1,0:T(8,128)(2,1)} %rest_0_.1), custom_call_target="tpu_custom_call" | custom-call | flops 1207959552 | bytes 1179648 | tf_op jit(solution)/shard_map/pallas_call | solution.py:37
  57.2 0.4 collective-permute-start.17
  57.6 3.2 %shard_map.126.own = f32[256,2304]{1,0:T(8,128)S(1)} custom-call(s32[3]{0:T(128)S(1)} %pad_add_fusion.sc, bf16[256,1024]{1,0:T(8,128)(2,1)S(1)} %get-tuple-element.33.at, bf16[256,512]{1,0:T(8,128)(2,1)S(1)} %get-tuple-element.32.act, bf16[1,1024,5120]{2,1,0:T(8,128)(2,1)S(1)} %get-tuple-element.34.td, bf16[512,5120]{1,0:T(8,128)(2,1)S(1)} %get-tuple-element.35.sd), custom_call_target="tpu_custom_call" | custom-call | flops 1811939328 | bytes 1179648 | tf_op jit(solution)/shard_map/pallas_call | solution.py:37
  60.9 0.3 shard_map.127
  61.2 1.6 %collective-permute-start.18 = (bf16[64,2304]{1,0:T(8,128)(2,1)S(1)}, bf16[64,2304]{1,0:T(8,128)(2,1)S(1)}, u32[]{:S(2)}, u32[]{:S(2)}) collective-permute-start(bf16[64,2304]{1,0:T(8,128)(2,1)S(1)} %get-tuple-element.41), channel_id=1, source_target_pairs={{0,4},{4,0},{8,12},{12,8},{1,5},{5,1},{9,13},{13,9},{2,6},{6,2},{1... | collective-permute-start | bytes 884744 | tf_op jit(solution)/shard_map/ppermute | solution.py:22
  62.8 1.8 %collective-permute-start.19 = (bf16[64,2304]{1,0:T(8,128)(2,1)S(1)}, bf16[64,2304]{1,0:T(8,128)(2,1)S(1)}, u32[]{:S(2)}, u32[]{:S(2)}) collective-permute-start(bf16[64,2304]{1,0:T(8,128)(2,1)S(1)} %get-tuple-element.42), channel_id=1, source_target_pairs={{0,8},{4,12},{8,0},{12,4},{1,9},{5,13},{9,1},{13,5},{2,10},{6,14},... | collective-permute-start | bytes 884744 | tf_op jit(solution)/shard_map/ppermute | solution.py:22
  64.8 0.9 shard_map.130
  65.7 0.9 shard_map.129.own
  66.6 0.4 collective-permute-done.24.got
  67.0 0.6 shard_map.131
  67.6 2.4 %collective-permute-start.25 = (bf16[64,256]{1,0:T(8,128)(2,1)S(1)}, bf16[64,256]{1,0:T(8,128)(2,1)S(1)}, u32[]{:S(2)}, u32[]{:S(2)}) collective-permute-start(bf16[64,256]{1,0:T(8,128)(2,1)S(1)} %get-tuple-element.49), channel_id=1, source_target_pairs={{0,1},{1,0},{2,3},{3,2},{4,5},{5,4},{6,7},{7,6},{8,9},{9,8},{10,11... | collective-permute-start | bytes 98312 | tf_op jit(solution)/shard_map/ppermute | solution.py:22
  70.1 1.1 collective-permute-done.18.refs_1_
  71.1 6.1 %collective-permute-done.19.refs_2_ = bf16[64,2304]{1,0:T(8,128)(2,1)S(1)} collective-permute-done((bf16[64,2304]{1,0:T(8,128)(2,1)S(1)}, bf16[64,2304]{1,0:T(8,128)(2,1)S(1)}, u32[]{:S(2)}, u32[]{:S(2)}) %collective-permute-start.19) | collective-permute-done | bytes 294944 | tf_op jit(solution)/shard_map/ppermute | solution.py:22
  77.3 0.7 collective-permute-done.20.refs_3_
  78.0 0.7 shard_map.128
  78.7 2.3 %collective-permute-start.21 = (bf16[16,2304]{1,0:T(8,128)(2,1)S(1)}, bf16[16,2304]{1,0:T(8,128)(2,1)S(1)}, u32[]{:S(2)}, u32[]{:S(2)}) collective-permute-start(bf16[16,2304]{1,0:T(8,128)(2,1)S(1)} %get-tuple-element.45), channel_id=1, source_target_pairs={{0,1},{1,0},{2,3},{3,2},{4,5},{5,4},{6,7},{7,6},{8,9},{9,8},{10,11... | collective-permute-start | bytes 221192 | tf_op jit(solution)/shard_map/ppermute | solution.py:22
  81.0 1.9 %collective-permute-start.22 = (bf16[16,2304]{1,0:T(8,128)(2,1)S(1)}, bf16[16,2304]{1,0:T(8,128)(2,1)S(1)}, u32[]{:S(2)}, u32[]{:S(2)}) collective-permute-start(bf16[16,2304]{1,0:T(8,128)(2,1)S(1)} %get-tuple-element.46), channel_id=1, source_target_pairs={{0,2},{1,3},{2,0},{3,1},{4,6},{5,7},{6,4},{7,5},{8,10},{9,11},{10,... | collective-permute-start | bytes 221192 | tf_op jit(solution)/shard_map/ppermute | solution.py:22
  82.9 1.4 collective-permute-start.23
  84.3 2.0 %collective-permute-start.26 = (bf16[64,256]{1,0:T(8,128)(2,1)S(1)}, bf16[64,256]{1,0:T(8,128)(2,1)S(1)}, u32[]{:S(2)}, u32[]{:S(2)}) collective-permute-start(bf16[64,256]{1,0:T(8,128)(2,1)S(1)} %get-tuple-element.50), channel_id=1, source_target_pairs={{0,2},{1,3},{2,0},{3,1},{4,6},{5,7},{6,4},{7,5},{8,10},{9,11},{10,... | collective-permute-start | bytes 98312 | tf_op jit(solution)/shard_map/ppermute | solution.py:22
  86.3 0.9 collective-permute-start.27
  87.2 5.5 %collective-permute-done.26.refs_2_ = bf16[64,256]{1,0:T(8,128)(2,1)S(1)} collective-permute-done((bf16[64,256]{1,0:T(8,128)(2,1)S(1)}, bf16[64,256]{1,0:T(8,128)(2,1)S(1)}, u32[]{:S(2)}, u32[]{:S(2)}) %collective-permute-start.26) | collective-permute-done | bytes 32800 | tf_op jit(solution)/shard_map/ppermute | solution.py:22
  92.7 0.6 shard_map.132
  93.3 1.5 %collective-permute-start.28 = (bf16[16,256]{1,0:T(8,128)(2,1)S(1)}, bf16[16,256]{1,0:T(8,128)(2,1)S(1)}, u32[]{:S(2)}, u32[]{:S(2)}) collective-permute-start(bf16[16,256]{1,0:T(8,128)(2,1)S(1)} %get-tuple-element.53), channel_id=1, source_target_pairs={{0,4},{4,0},{8,12},{12,8},{1,5},{5,1},{9,13},{13,9},{2,6},{6,2},{1... | collective-permute-start | bytes 24584 | tf_op jit(solution)/shard_map/ppermute | solution.py:22
  94.8 0.5 collective-permute-start.29
  95.3 1.7 %collective-permute-done.28.refs_5_ = bf16[16,256]{1,0:T(8,128)(2,1)S(1)} collective-permute-done((bf16[16,256]{1,0:T(8,128)(2,1)S(1)}, bf16[16,256]{1,0:T(8,128)(2,1)S(1)}, u32[]{:S(2)}, u32[]{:S(2)}) %collective-permute-start.28) | collective-permute-done | bytes 8224 | tf_op jit(solution)/shard_map/ppermute | solution.py:22
  97.0 1.4 collective-permute-start.30
  98.5 3.1 %collective-permute-done.30.refs_7_ = bf16[16,256]{1,0:T(8,128)(2,1)S(1)} collective-permute-done((bf16[16,256]{1,0:T(8,128)(2,1)S(1)}, bf16[16,256]{1,0:T(8,128)(2,1)S(1)}, u32[]{:S(2)}, u32[]{:S(2)}) %collective-permute-start.30) | collective-permute-done | bytes 8224 | tf_op jit(solution)/shard_map/ppermute | solution.py:22
  101.6 2.6 %collective-permute-start.40 = (bf16[16,2560]{1,0:T(8,128)(2,1)S(1)}, bf16[16,2560]{1,0:T(8,128)(2,1)S(1)}, u32[]{:S(2)}, u32[]{:S(2)}) collective-permute-start(bf16[16,2560]{1,0:T(8,128)(2,1)S(1)} %shard_map.133.rest_0_), channel_id=1, source_target_pairs={{0,3},{1,2},{2,1},{3,0},{4,7},{5,6},{6,5},{7,4},{8,11},{9,10},{10,... | collective-permute-start | bytes 245768 | tf_op jit(solution)/shard_map/ppermute | solution.py:22
  104.3 1.8 %collective-permute-start.38 = (bf16[16,2560]{1,0:T(8,128)(2,1)S(1)}, bf16[16,2560]{1,0:T(8,128)(2,1)S(1)}, u32[]{:S(2)}, u32[]{:S(2)}) collective-permute-start(bf16[16,2560]{1,0:T(8,128)(2,1)S(1)} %shard_map.133.rest_0_), channel_id=1, source_target_pairs={{0,1},{1,0},{2,3},{3,2},{4,5},{5,4},{6,7},{7,6},{8,9},{9,8},{10,11... | collective-permute-start | bytes 245768 | tf_op jit(solution)/shard_map/ppermute | solution.py:22
  106.1 1.9 %collective-permute-done.40.refs_2_ = bf16[16,2560]{1,0:T(8,128)(2,1)S(1)} collective-permute-done((bf16[16,2560]{1,0:T(8,128)(2,1)S(1)}, bf16[16,2560]{1,0:T(8,128)(2,1)S(1)}, u32[]{:S(2)}, u32[]{:S(2)}) %collective-permute-start.40) | collective-permute-done | bytes 81952 | tf_op jit(solution)/shard_map/ppermute | solution.py:22
  108.0 2.0 %collective-permute-done.39.refs_1_ = bf16[16,2560]{1,0:T(8,128)(2,1)S(1)} collective-permute-done((bf16[16,2560]{1,0:T(8,128)(2,1)S(1)}, bf16[16,2560]{1,0:T(8,128)(2,1)S(1)}, u32[]{:S(2)}, u32[]{:S(2)}) %collective-permute-start.39) | collective-permute-done | bytes 81952 | tf_op jit(solution)/shard_map/ppermute | solution.py:22
  109.9 1.4 %collective-permute-start.43 = (bf16[48,2560]{1,0:T(8,128)(2,1)S(1)}, bf16[48,2560]{1,0:T(8,128)(2,1)S(1)}, u32[]{:S(2)}, u32[]{:S(2)}) collective-permute-start(bf16[48,2560]{1,0:T(8,128)(2,1)S(1)} %shard_map.134.rest_8_), channel_id=1, source_target_pairs={{0,12},{4,8},{8,4},{12,0},{1,13},{5,9},{9,5},{13,1},{2,14},{6,10},... | collective-permute-start | bytes 737288 | tf_op jit(solution)/shard_map/ppermute | solution.py:22
  111.4 1.5 %collective-permute-start.42 = (bf16[48,2560]{1,0:T(8,128)(2,1)S(1)}, bf16[48,2560]{1,0:T(8,128)(2,1)S(1)}, u32[]{:S(2)}, u32[]{:S(2)}) collective-permute-start(bf16[48,2560]{1,0:T(8,128)(2,1)S(1)} %shard_map.134.rest_8_), channel_id=1, source_target_pairs={{0,8},{4,12},{8,0},{12,4},{1,9},{5,13},{9,1},{13,5},{2,10},{6,14},... | collective-permute-start | bytes 737288 | tf_op jit(solution)/shard_map/ppermute | solution.py:22
  112.9 0.6 collective-permute-start.41
  113.5 1.4 collective-permute-start.33
  114.9 1.5 %collective-permute-start.32 = (bf16[16,2560]{1,0:T(8,128)(2,1)S(1)}, bf16[16,2560]{1,0:T(8,128)(2,1)S(1)}, u32[]{:S(2)}, u32[]{:S(2)}) collective-permute-start(bf16[16,2560]{1,0:T(8,128)(2,1)S(1)} %shard_map.133.rest_0_), channel_id=1, source_target_pairs={{0,8},{4,12},{8,0},{12,4},{1,9},{5,13},{9,1},{13,5},{2,10},{6,14},... | collective-permute-start | bytes 245768 | tf_op jit(solution)/shard_map/ppermute | solution.py:22
  116.4 5.2 %collective-permute-done.33.rest_3_ = bf16[16,2560]{1,0:T(8,128)(2,1)S(1)} collective-permute-done((bf16[16,2560]{1,0:T(8,128)(2,1)S(1)}, bf16[16,2560]{1,0:T(8,128)(2,1)S(1)}, u32[]{:S(2)}, u32[]{:S(2)}) %collective-permute-start.33) | collective-permute-done | bytes 81952 | tf_op jit(solution)/shard_map/ppermute | solution.py:22
  121.6 1.5 %collective-permute-start.31 = (bf16[16,2560]{1,0:T(8,128)(2,1)S(1)}, bf16[16,2560]{1,0:T(8,128)(2,1)S(1)}, u32[]{:S(2)}, u32[]{:S(2)}) collective-permute-start(bf16[16,2560]{1,0:T(8,128)(2,1)S(1)} %shard_map.133.rest_0_), channel_id=1, source_target_pairs={{0,4},{4,0},{8,12},{12,8},{1,5},{5,1},{9,13},{13,9},{2,6},{6,2},{1... | collective-permute-start | bytes 245768 | tf_op jit(solution)/shard_map/ppermute | solution.py:22
  123.3 2.8 %collective-permute-done.31.rest_1_ = bf16[16,2560]{1,0:T(8,128)(2,1)S(1)} collective-permute-done((bf16[16,2560]{1,0:T(8,128)(2,1)S(1)}, bf16[16,2560]{1,0:T(8,128)(2,1)S(1)}, u32[]{:S(2)}, u32[]{:S(2)}) %collective-permute-start.31) | collective-permute-done | bytes 81952 | tf_op jit(solution)/shard_map/ppermute | solution.py:22
  126.1 0.5 collective-permute-start.47
  126.7 0.4 collective-permute-start.45
  127.5 1.1 collective-permute-done.36.rest_6_
  128.9 1.0 collective-permute-done.35.rest_5_
  129.9 11.3 %shard_map.135 = (bf16[5120,512]{1,0:T(8,128)(2,1)}, bf16[5120,512]{1,0:T(8,128)(2,1)}, bf16[512,5120]{1,0:T(8,128)(2,1)}, f32[1,1]{1,0:T(1,128)}) custom-call(s32[3]{0:T(128)S(1)} %pad_add_fusion.sc, bf16[256,512]{1,0:T(8,128)(2,1)S(1)} %get-tuple-element.32.act, bf16[512,5120]{1,0:T(8,128)(2,1)S(1)} %get-tuple-element.35.sd, ...), custom_call_target="tpu_custom_call" | custom-call | flops 5368709120 | bytes 15728640 | tf_op jit(solution)/shard_map/pallas_call | solution.py:37
  (49 shorter events, 1.9 us)
Async XLA Ops:
  0.6 8.8 %collective-permute-start.1 = (bf16[32,1280]{1,0:T(8,128)(2,1)}, bf16[32,1280]{1,0:T(8,128)(2,1)S(1)}, u32[]{:S(2)}, u32[]{:S(2)}) collective-permute-start(bf16[32,1280]{1,0:T(8,128)(2,1)} %tokens.1), channel_id=1, source_target_pairs={{0,2},{1,3},{2,0},{3,1},{4,6},{5,7},{6,4},{7,5},{8,10},{9,11},{10,... | collective-permute-start | bytes 245768 | tf_op jit(solution)/shard_map/ppermute | solution.py:22
  4.8 4.8 %collective-permute-start = (bf16[32,1280]{1,0:T(8,128)(2,1)}, bf16[32,1280]{1,0:T(8,128)(2,1)S(1)}, u32[]{:S(2)}, u32[]{:S(2)}) collective-permute-start(bf16[32,1280]{1,0:T(8,128)(2,1)} %tokens.1), channel_id=1, source_target_pairs={{0,1},{1,0},{2,3},{3,2},{4,5},{5,4},{6,7},{7,6},{8,9},{9,8},{10,11... | collective-permute-start | bytes 245768 | tf_op jit(solution)/shard_map/ppermute | solution.py:22
  6.3 6.4 %collective-permute-start.2 = (bf16[32,1280]{1,0:T(8,128)(2,1)}, bf16[32,1280]{1,0:T(8,128)(2,1)S(1)}, u32[]{:S(2)}, u32[]{:S(2)}) collective-permute-start(bf16[32,1280]{1,0:T(8,128)(2,1)} %tokens.1), channel_id=1, source_target_pairs={{0,3},{1,2},{2,1},{3,0},{4,7},{5,6},{6,5},{7,4},{8,11},{9,10},{10,... | collective-permute-start | bytes 245768 | tf_op jit(solution)/shard_map/ppermute | solution.py:22
  12.8 18.9 %collective-permute-start.12 = (bf16[96,1280]{1,0:T(8,128)(2,1)S(1)}, bf16[96,1280]{1,0:T(8,128)(2,1)S(1)}, u32[]{:S(2)}, u32[]{:S(2)}) collective-permute-start(bf16[96,1280]{1,0:T(8,128)(2,1)S(1)} %shard_map.120.refs_0_.rest_8_), channel_id=1, source_target_pairs={{0,12},{4,8},{8,4},{12,0},{1,13},{5,9},{9,5},{13,1},{2,14},{6,10},... | collective-permute-start | bytes 737288 | tf_op jit(solution)/shard_map/ppermute | solution.py:22
  15.4 16.8 %collective-permute-start.11 = (bf16[96,1280]{1,0:T(8,128)(2,1)S(1)}, bf16[96,1280]{1,0:T(8,128)(2,1)S(1)}, u32[]{:S(2)}, u32[]{:S(2)}) collective-permute-start(bf16[96,1280]{1,0:T(8,128)(2,1)S(1)} %shard_map.120.refs_0_.rest_8_), channel_id=1, source_target_pairs={{0,8},{4,12},{8,0},{12,4},{1,9},{5,13},{9,1},{13,5},{2,10},{6,14},... | collective-permute-start | bytes 737288 | tf_op jit(solution)/shard_map/ppermute | solution.py:22
  15.9 16.4 %collective-permute-start.10 = (bf16[96,1280]{1,0:T(8,128)(2,1)S(1)}, bf16[96,1280]{1,0:T(8,128)(2,1)S(1)}, u32[]{:S(2)}, u32[]{:S(2)}) collective-permute-start(bf16[96,1280]{1,0:T(8,128)(2,1)S(1)} %shard_map.120.refs_0_.rest_8_), channel_id=1, source_target_pairs={{0,4},{4,0},{8,12},{12,8},{1,5},{5,1},{9,13},{13,9},{2,6},{6,2},{1... | collective-permute-start | bytes 737288 | tf_op jit(solution)/shard_map/ppermute | solution.py:22
  18.0 2.7 %collective-permute-start.6 = (bf16[32,1408]{1,0:T(8,128)(2,1)S(1)}, bf16[32,1408]{1,0:T(8,128)(2,1)S(1)}, u32[]{:S(2)}, u32[]{:S(2)}) collective-permute-start(bf16[32,1408]{1,0:T(8,128)(2,1)S(1)} %shard_map.123.rest_0_), channel_id=1, source_target_pairs={{0,16},{16,0},{1,17},{17,1},{2,18},{18,2},{3,19},{19,3},{4,20},{20... | collective-permute-start | bytes 270344 | tf_op jit(solution)/shard_map/ppermute | solution.py:22
  18.1 9.1 %collective-permute-start.5 = (bf16[32,1408]{1,0:T(8,128)(2,1)S(1)}, bf16[32,1408]{1,0:T(8,128)(2,1)S(1)}, u32[]{:S(2)}, u32[]{:S(2)}) collective-permute-start(bf16[32,1408]{1,0:T(8,128)(2,1)S(1)} %shard_map.123.rest_0_), channel_id=1, source_target_pairs={{0,12},{4,8},{8,4},{12,0},{1,13},{5,9},{9,5},{13,1},{2,14},{6,10},... | collective-permute-start | bytes 270344 | tf_op jit(solution)/shard_map/ppermute | solution.py:22
  20.7 8.3 %collective-permute-start.4 = (bf16[32,1408]{1,0:T(8,128)(2,1)S(1)}, bf16[32,1408]{1,0:T(8,128)(2,1)S(1)}, u32[]{:S(2)}, u32[]{:S(2)}) collective-permute-start(bf16[32,1408]{1,0:T(8,128)(2,1)S(1)} %shard_map.123.rest_0_), channel_id=1, source_target_pairs={{0,8},{4,12},{8,0},{12,4},{1,9},{5,13},{9,1},{13,5},{2,10},{6,14},... | collective-permute-start | bytes 270344 | tf_op jit(solution)/shard_map/ppermute | solution.py:22
  27.2 4.5 %collective-permute-start.3 = (bf16[32,1408]{1,0:T(8,128)(2,1)S(1)}, bf16[32,1408]{1,0:T(8,128)(2,1)S(1)}, u32[]{:S(2)}, u32[]{:S(2)}) collective-permute-start(bf16[32,1408]{1,0:T(8,128)(2,1)S(1)} %shard_map.123.rest_0_), channel_id=1, source_target_pairs={{0,4},{4,0},{8,12},{12,8},{1,5},{5,1},{9,13},{13,9},{2,6},{6,2},{1... | collective-permute-start | bytes 270344 | tf_op jit(solution)/shard_map/ppermute | solution.py:22
  29.0 3.7 %collective-permute-start.9 = (bf16[32,1408]{1,0:T(8,128)(2,1)S(1)}, bf16[32,1408]{1,0:T(8,128)(2,1)S(1)}, u32[]{:S(2)}, u32[]{:S(2)}) collective-permute-start(bf16[32,1408]{1,0:T(8,128)(2,1)S(1)} %collective-permute-done.5.rest_3_), channel_id=1, source_target_pairs={{0,16},{16,0},{1,17},{17,1},{2,18},{18,2},{3,19},{19,3},{4,20},{20... | collective-permute-start | bytes 270344 | tf_op jit(solution)/shard_map/ppermute | solution.py:22
  31.7 10.9 %collective-permute-start.13 = (bf16[96,1280]{1,0:T(8,128)(2,1)S(1)}, bf16[96,1280]{1,0:T(8,128)(2,1)S(1)}, u32[]{:S(2)}, u32[]{:S(2)}) collective-permute-start(bf16[96,1280]{1,0:T(8,128)(2,1)S(1)} %shard_map.120.refs_0_.rest_8_), channel_id=1, source_target_pairs={{0,16},{16,0},{1,17},{17,1},{2,18},{18,2},{3,19},{19,3},{4,20},{20... | collective-permute-start | bytes 737288 | tf_op jit(solution)/shard_map/ppermute | solution.py:22
  31.7 10.9 %collective-permute-start.16 = (bf16[96,1280]{1,0:T(8,128)(2,1)S(1)}, bf16[96,1280]{1,0:T(8,128)(2,1)S(1)}, u32[]{:S(2)}, u32[]{:S(2)}) collective-permute-start(bf16[96,1280]{1,0:T(8,128)(2,1)S(1)} %collective-permute-done.12.rest_11_), channel_id=1, source_target_pairs={{0,16},{16,0},{1,17},{17,1},{2,18},{18,2},{3,19},{19,3},{4,20},{20... | collective-permute-start | bytes 737288 | tf_op jit(solution)/shard_map/ppermute | solution.py:22
  32.2 10.4 %collective-permute-start.15 = (bf16[96,1280]{1,0:T(8,128)(2,1)S(1)}, bf16[96,1280]{1,0:T(8,128)(2,1)S(1)}, u32[]{:S(2)}, u32[]{:S(2)}) collective-permute-start(bf16[96,1280]{1,0:T(8,128)(2,1)S(1)} %collective-permute-done.11.rest_10_), channel_id=1, source_target_pairs={{0,16},{16,0},{1,17},{17,1},{2,18},{18,2},{3,19},{19,3},{4,20},{20... | collective-permute-start | bytes 737288 | tf_op jit(solution)/shard_map/ppermute | solution.py:22
  32.3 10.3 %collective-permute-start.14 = (bf16[96,1280]{1,0:T(8,128)(2,1)S(1)}, bf16[96,1280]{1,0:T(8,128)(2,1)S(1)}, u32[]{:S(2)}, u32[]{:S(2)}) collective-permute-start(bf16[96,1280]{1,0:T(8,128)(2,1)S(1)} %collective-permute-done.10.rest_9_), channel_id=1, source_target_pairs={{0,16},{16,0},{1,17},{17,1},{2,18},{18,2},{3,19},{19,3},{4,20},{20... | collective-permute-start | bytes 737288 | tf_op jit(solution)/shard_map/ppermute | solution.py:22
  32.7 1.7 %collective-permute-start.8 = (bf16[32,1408]{1,0:T(8,128)(2,1)S(1)}, bf16[32,1408]{1,0:T(8,128)(2,1)S(1)}, u32[]{:S(2)}, u32[]{:S(2)}) collective-permute-start(bf16[32,1408]{1,0:T(8,128)(2,1)S(1)} %collective-permute-done.4.rest_2_), channel_id=1, source_target_pairs={{0,16},{16,0},{1,17},{17,1},{2,18},{18,2},{3,19},{19,3},{4,20},{20... | collective-permute-start | bytes 270344 | tf_op jit(solution)/shard_map/ppermute | solution.py:22
  34.4 8.2 %collective-permute-start.7 = (bf16[32,1408]{1,0:T(8,128)(2,1)S(1)}, bf16[32,1408]{1,0:T(8,128)(2,1)S(1)}, u32[]{:S(2)}, u32[]{:S(2)}) collective-permute-start(bf16[32,1408]{1,0:T(8,128)(2,1)S(1)} %collective-permute-done.3.rest_1_), channel_id=1, source_target_pairs={{0,16},{16,0},{1,17},{17,1},{2,18},{18,2},{3,19},{19,3},{4,20},{20... | collective-permute-start | bytes 270344 | tf_op jit(solution)/shard_map/ppermute | solution.py:22
  57.2 3.7 %collective-permute-start.17 = (bf16[256,2304]{1,0:T(8,128)(2,1)S(1)}, bf16[256,2304]{1,0:T(8,128)(2,1)S(1)}, u32[]{:S(2)}, u32[]{:S(2)}) collective-permute-start(bf16[256,2304]{1,0:T(8,128)(2,1)S(1)} %get-tuple-element.39), channel_id=1, source_target_pairs={{0,16},{16,0},{1,17},{17,1},{2,18},{18,2},{3,19},{19,3},{4,20},{20... | collective-permute-start | bytes 3538952 | tf_op jit(solution)/shard_map/ppermute | solution.py:22
  61.2 9.9 %collective-permute-start.18 = (bf16[64,2304]{1,0:T(8,128)(2,1)S(1)}, bf16[64,2304]{1,0:T(8,128)(2,1)S(1)}, u32[]{:S(2)}, u32[]{:S(2)}) collective-permute-start(bf16[64,2304]{1,0:T(8,128)(2,1)S(1)} %get-tuple-element.41), channel_id=1, source_target_pairs={{0,4},{4,0},{8,12},{12,8},{1,5},{5,1},{9,13},{13,9},{2,6},{6,2},{1... | collective-permute-start | bytes 884744 | tf_op jit(solution)/shard_map/ppermute | solution.py:22
  62.8 14.5 %collective-permute-start.19 = (bf16[64,2304]{1,0:T(8,128)(2,1)S(1)}, bf16[64,2304]{1,0:T(8,128)(2,1)S(1)}, u32[]{:S(2)}, u32[]{:S(2)}) collective-permute-start(bf16[64,2304]{1,0:T(8,128)(2,1)S(1)} %get-tuple-element.42), channel_id=1, source_target_pairs={{0,8},{4,12},{8,0},{12,4},{1,9},{5,13},{9,1},{13,5},{2,10},{6,14},... | collective-permute-start | bytes 884744 | tf_op jit(solution)/shard_map/ppermute | solution.py:22
  64.6 13.4 %collective-permute-start.20 = (bf16[64,2304]{1,0:T(8,128)(2,1)S(1)}, bf16[64,2304]{1,0:T(8,128)(2,1)S(1)}, u32[]{:S(2)}, u32[]{:S(2)}) collective-permute-start(bf16[64,2304]{1,0:T(8,128)(2,1)S(1)} %get-tuple-element.43), channel_id=1, source_target_pairs={{0,12},{4,8},{8,4},{12,0},{1,13},{5,9},{9,5},{13,1},{2,14},{6,10},... | collective-permute-start | bytes 884744 | tf_op jit(solution)/shard_map/ppermute | solution.py:22
  65.6 1.4 collective-permute-start.24
  67.6 18.7 %collective-permute-start.25 = (bf16[64,256]{1,0:T(8,128)(2,1)S(1)}, bf16[64,256]{1,0:T(8,128)(2,1)S(1)}, u32[]{:S(2)}, u32[]{:S(2)}) collective-permute-start(bf16[64,256]{1,0:T(8,128)(2,1)S(1)} %get-tuple-element.49), channel_id=1, source_target_pairs={{0,1},{1,0},{2,3},{3,2},{4,5},{5,4},{6,7},{7,6},{8,9},{9,8},{10,11... | collective-permute-start | bytes 98312 | tf_op jit(solution)/shard_map/ppermute | solution.py:22
  78.7 22.9 %collective-permute-start.21 = (bf16[16,2304]{1,0:T(8,128)(2,1)S(1)}, bf16[16,2304]{1,0:T(8,128)(2,1)S(1)}, u32[]{:S(2)}, u32[]{:S(2)}) collective-permute-start(bf16[16,2304]{1,0:T(8,128)(2,1)S(1)} %get-tuple-element.45), channel_id=1, source_target_pairs={{0,1},{1,0},{2,3},{3,2},{4,5},{5,4},{6,7},{7,6},{8,9},{9,8},{10,11... | collective-permute-start | bytes 221192 | tf_op jit(solution)/shard_map/ppermute | solution.py:22
  81.0 20.6 %collective-permute-start.22 = (bf16[16,2304]{1,0:T(8,128)(2,1)S(1)}, bf16[16,2304]{1,0:T(8,128)(2,1)S(1)}, u32[]{:S(2)}, u32[]{:S(2)}) collective-permute-start(bf16[16,2304]{1,0:T(8,128)(2,1)S(1)} %get-tuple-element.46), channel_id=1, source_target_pairs={{0,2},{1,3},{2,0},{3,1},{4,6},{5,7},{6,4},{7,5},{8,10},{9,11},{10,... | collective-permute-start | bytes 221192 | tf_op jit(solution)/shard_map/ppermute | solution.py:22
  82.9 18.7 %collective-permute-start.23 = (bf16[16,2304]{1,0:T(8,128)(2,1)S(1)}, bf16[16,2304]{1,0:T(8,128)(2,1)S(1)}, u32[]{:S(2)}, u32[]{:S(2)}) collective-permute-start(bf16[16,2304]{1,0:T(8,128)(2,1)S(1)} %get-tuple-element.47), channel_id=1, source_target_pairs={{0,3},{1,2},{2,1},{3,0},{4,7},{5,6},{6,5},{7,4},{8,11},{9,10},{10,... | collective-permute-start | bytes 221192 | tf_op jit(solution)/shard_map/ppermute | solution.py:22
  84.3 8.4 %collective-permute-start.26 = (bf16[64,256]{1,0:T(8,128)(2,1)S(1)}, bf16[64,256]{1,0:T(8,128)(2,1)S(1)}, u32[]{:S(2)}, u32[]{:S(2)}) collective-permute-start(bf16[64,256]{1,0:T(8,128)(2,1)S(1)} %get-tuple-element.50), channel_id=1, source_target_pairs={{0,2},{1,3},{2,0},{3,1},{4,6},{5,7},{6,4},{7,5},{8,10},{9,11},{10,... | collective-permute-start | bytes 98312 | tf_op jit(solution)/shard_map/ppermute | solution.py:22
  86.3 6.4 %collective-permute-start.27 = (bf16[64,256]{1,0:T(8,128)(2,1)S(1)}, bf16[64,256]{1,0:T(8,128)(2,1)S(1)}, u32[]{:S(2)}, u32[]{:S(2)}) collective-permute-start(bf16[64,256]{1,0:T(8,128)(2,1)S(1)} %get-tuple-element.51), channel_id=1, source_target_pairs={{0,3},{1,2},{2,1},{3,0},{4,7},{5,6},{6,5},{7,4},{8,11},{9,10},{10,... | collective-permute-start | bytes 98312 | tf_op jit(solution)/shard_map/ppermute | solution.py:22
  93.3 3.7 %collective-permute-start.28 = (bf16[16,256]{1,0:T(8,128)(2,1)S(1)}, bf16[16,256]{1,0:T(8,128)(2,1)S(1)}, u32[]{:S(2)}, u32[]{:S(2)}) collective-permute-start(bf16[16,256]{1,0:T(8,128)(2,1)S(1)} %get-tuple-element.53), channel_id=1, source_target_pairs={{0,4},{4,0},{8,12},{12,8},{1,5},{5,1},{9,13},{13,9},{2,6},{6,2},{1... | collective-permute-start | bytes 24584 | tf_op jit(solution)/shard_map/ppermute | solution.py:22
  94.8 3.7 %collective-permute-start.29 = (bf16[16,256]{1,0:T(8,128)(2,1)S(1)}, bf16[16,256]{1,0:T(8,128)(2,1)S(1)}, u32[]{:S(2)}, u32[]{:S(2)}) collective-permute-start(bf16[16,256]{1,0:T(8,128)(2,1)S(1)} %get-tuple-element.54), channel_id=1, source_target_pairs={{0,8},{4,12},{8,0},{12,4},{1,9},{5,13},{9,1},{13,5},{2,10},{6,14},... | collective-permute-start | bytes 24584 | tf_op jit(solution)/shard_map/ppermute | solution.py:22
  97.0 4.5 %collective-permute-start.30 = (bf16[16,256]{1,0:T(8,128)(2,1)S(1)}, bf16[16,256]{1,0:T(8,128)(2,1)S(1)}, u32[]{:S(2)}, u32[]{:S(2)}) collective-permute-start(bf16[16,256]{1,0:T(8,128)(2,1)S(1)} %get-tuple-element.55), channel_id=1, source_target_pairs={{0,12},{4,8},{8,4},{12,0},{1,13},{5,9},{9,5},{13,1},{2,14},{6,10},... | collective-permute-start | bytes 24584 | tf_op jit(solution)/shard_map/ppermute | solution.py:22
  101.6 6.3 %collective-permute-start.40 = (bf16[16,2560]{1,0:T(8,128)(2,1)S(1)}, bf16[16,2560]{1,0:T(8,128)(2,1)S(1)}, u32[]{:S(2)}, u32[]{:S(2)}) collective-permute-start(bf16[16,2560]{1,0:T(8,128)(2,1)S(1)} %shard_map.133.rest_0_), channel_id=1, source_target_pairs={{0,3},{1,2},{2,1},{3,0},{4,7},{5,6},{6,5},{7,4},{8,11},{9,10},{10,... | collective-permute-start | bytes 245768 | tf_op jit(solution)/shard_map/ppermute | solution.py:22
  104.3 5.7 %collective-permute-start.39 = (bf16[16,2560]{1,0:T(8,128)(2,1)S(1)}, bf16[16,2560]{1,0:T(8,128)(2,1)S(1)}, u32[]{:S(2)}, u32[]{:S(2)}) collective-permute-start(bf16[16,2560]{1,0:T(8,128)(2,1)S(1)} %shard_map.133.rest_0_), channel_id=1, source_target_pairs={{0,2},{1,3},{2,0},{3,1},{4,6},{5,7},{6,4},{7,5},{8,10},{9,11},{10,... | collective-permute-start | bytes 245768 | tf_op jit(solution)/shard_map/ppermute | solution.py:22
  104.3 5.7 %collective-permute-start.38 = (bf16[16,2560]{1,0:T(8,128)(2,1)S(1)}, bf16[16,2560]{1,0:T(8,128)(2,1)S(1)}, u32[]{:S(2)}, u32[]{:S(2)}) collective-permute-start(bf16[16,2560]{1,0:T(8,128)(2,1)S(1)} %shard_map.133.rest_0_), channel_id=1, source_target_pairs={{0,1},{1,0},{2,3},{3,2},{4,5},{5,4},{6,7},{7,6},{8,9},{9,8},{10,11... | collective-permute-start | bytes 245768 | tf_op jit(solution)/shard_map/ppermute | solution.py:22
  109.9 16.1 %collective-permute-start.43 = (bf16[48,2560]{1,0:T(8,128)(2,1)S(1)}, bf16[48,2560]{1,0:T(8,128)(2,1)S(1)}, u32[]{:S(2)}, u32[]{:S(2)}) collective-permute-start(bf16[48,2560]{1,0:T(8,128)(2,1)S(1)} %shard_map.134.rest_8_), channel_id=1, source_target_pairs={{0,12},{4,8},{8,4},{12,0},{1,13},{5,9},{9,5},{13,1},{2,14},{6,10},... | collective-permute-start | bytes 737288 | tf_op jit(solution)/shard_map/ppermute | solution.py:22
  111.4 15.2 %collective-permute-start.42 = (bf16[48,2560]{1,0:T(8,128)(2,1)S(1)}, bf16[48,2560]{1,0:T(8,128)(2,1)S(1)}, u32[]{:S(2)}, u32[]{:S(2)}) collective-permute-start(bf16[48,2560]{1,0:T(8,128)(2,1)S(1)} %shard_map.134.rest_8_), channel_id=1, source_target_pairs={{0,8},{4,12},{8,0},{12,4},{1,9},{5,13},{9,1},{13,5},{2,10},{6,14},... | collective-permute-start | bytes 737288 | tf_op jit(solution)/shard_map/ppermute | solution.py:22
  112.9 13.7 %collective-permute-start.41 = (bf16[48,2560]{1,0:T(8,128)(2,1)S(1)}, bf16[48,2560]{1,0:T(8,128)(2,1)S(1)}, u32[]{:S(2)}, u32[]{:S(2)}) collective-permute-start(bf16[48,2560]{1,0:T(8,128)(2,1)S(1)} %shard_map.134.rest_8_), channel_id=1, source_target_pairs={{0,4},{4,0},{8,12},{12,8},{1,5},{5,1},{9,13},{13,9},{2,6},{6,2},{1... | collective-permute-start | bytes 737288 | tf_op jit(solution)/shard_map/ppermute | solution.py:22
  113.5 1.4 collective-permute-start.34
  113.5 8.1 %collective-permute-start.33 = (bf16[16,2560]{1,0:T(8,128)(2,1)S(1)}, bf16[16,2560]{1,0:T(8,128)(2,1)S(1)}, u32[]{:S(2)}, u32[]{:S(2)}) collective-permute-start(bf16[16,2560]{1,0:T(8,128)(2,1)S(1)} %shard_map.133.rest_0_), channel_id=1, source_target_pairs={{0,12},{4,8},{8,4},{12,0},{1,13},{5,9},{9,5},{13,1},{2,14},{6,10},... | collective-permute-start | bytes 245768 | tf_op jit(solution)/shard_map/ppermute | solution.py:22
  114.9 8.4 %collective-permute-start.32 = (bf16[16,2560]{1,0:T(8,128)(2,1)S(1)}, bf16[16,2560]{1,0:T(8,128)(2,1)S(1)}, u32[]{:S(2)}, u32[]{:S(2)}) collective-permute-start(bf16[16,2560]{1,0:T(8,128)(2,1)S(1)} %shard_map.133.rest_0_), channel_id=1, source_target_pairs={{0,8},{4,12},{8,0},{12,4},{1,9},{5,13},{9,1},{13,5},{2,10},{6,14},... | collective-permute-start | bytes 245768 | tf_op jit(solution)/shard_map/ppermute | solution.py:22
  121.6 4.4 %collective-permute-start.31 = (bf16[16,2560]{1,0:T(8,128)(2,1)S(1)}, bf16[16,2560]{1,0:T(8,128)(2,1)S(1)}, u32[]{:S(2)}, u32[]{:S(2)}) collective-permute-start(bf16[16,2560]{1,0:T(8,128)(2,1)S(1)} %shard_map.133.rest_0_), channel_id=1, source_target_pairs={{0,4},{4,0},{8,12},{12,8},{1,5},{5,1},{9,13},{13,9},{2,6},{6,2},{1... | collective-permute-start | bytes 245768 | tf_op jit(solution)/shard_map/ppermute | solution.py:22
  123.2 6.7 %collective-permute-start.44 = (bf16[48,2560]{1,0:T(8,128)(2,1)S(1)}, bf16[48,2560]{1,0:T(8,128)(2,1)S(1)}, u32[]{:S(2)}, u32[]{:S(2)}) collective-permute-start(bf16[48,2560]{1,0:T(8,128)(2,1)S(1)} %shard_map.134.rest_8_), channel_id=1, source_target_pairs={{0,16},{16,0},{1,17},{17,1},{2,18},{18,2},{3,19},{19,3},{4,20},{20... | collective-permute-start | bytes 737288 | tf_op jit(solution)/shard_map/ppermute | solution.py:22
  126.1 1.3 collective-permute-start.37
  126.1 3.8 %collective-permute-start.47 = (bf16[48,2560]{1,0:T(8,128)(2,1)S(1)}, bf16[48,2560]{1,0:T(8,128)(2,1)S(1)}, u32[]{:S(2)}, u32[]{:S(2)}) collective-permute-start(bf16[48,2560]{1,0:T(8,128)(2,1)S(1)} %collective-permute-done.43.rest_11_), channel_id=1, source_target_pairs={{0,16},{16,0},{1,17},{17,1},{2,18},{18,2},{3,19},{19,3},{4,20},{20... | collective-permute-start | bytes 737288 | tf_op jit(solution)/shard_map/ppermute | solution.py:22
  126.6 3.3 %collective-permute-start.46 = (bf16[48,2560]{1,0:T(8,128)(2,1)S(1)}, bf16[48,2560]{1,0:T(8,128)(2,1)S(1)}, u32[]{:S(2)}, u32[]{:S(2)}) collective-permute-start(bf16[48,2560]{1,0:T(8,128)(2,1)S(1)} %collective-permute-done.42.rest_10_), channel_id=1, source_target_pairs={{0,16},{16,0},{1,17},{17,1},{2,18},{18,2},{3,19},{19,3},{4,20},{20... | collective-permute-start | bytes 737288 | tf_op jit(solution)/shard_map/ppermute | solution.py:22
  126.7 3.3 %collective-permute-start.45 = (bf16[48,2560]{1,0:T(8,128)(2,1)S(1)}, bf16[48,2560]{1,0:T(8,128)(2,1)S(1)}, u32[]{:S(2)}, u32[]{:S(2)}) collective-permute-start(bf16[48,2560]{1,0:T(8,128)(2,1)S(1)} %collective-permute-done.41.rest_9_), channel_id=1, source_target_pairs={{0,16},{16,0},{1,17},{17,1},{2,18},{18,2},{3,19},{19,3},{4,20},{20... | collective-permute-start | bytes 737288 | tf_op jit(solution)/shard_map/ppermute | solution.py:22
  127.4 1.3 collective-permute-start.36
  128.6 1.3 collective-permute-start.35
